TPU v7x, 32 devices: a whole 2x2x4 slice. The times are simulated.
32 devices in a mesh: dp: 8 (over z, y), cp: 4 (over x, core).
Axes of the slice: x: 2, y: 2, z: 4, core: 2. Of those that a mesh axis runs over, the one named last changes fastest.
Arguments:
- inputs: bfloat16 [16, 1024, 1024], P('dp', 'cp'), may hold values from -6 to 6
- cotangent: bfloat16 [16, 1024, 1024], P('dp', 'cp'), may hold values from -6 to 6
- lengths: int32 [16], P('dp'), may hold values from 256 to 1024, as said below
- bucket_ids: int32 [2047], replicated, may hold values from 0 to 31
- attn_gain_one: bfloat16 [1024], P(('dp', 'cp')), may hold values from 0.5 to 1.5
- query_one: bfloat16 [1024, 1024], P(('dp', 'cp')), may hold values from -0.0234375 to 0.0234375
- key_one: bfloat16 [1024, 1024], P(('dp', 'cp')), may hold values from -0.1875 to 0.1875
- value_one: bfloat16 [1024, 1024], P(('dp', 'cp')), may hold values from -0.1875 to 0.1875
- output_one: bfloat16 [1024, 1024], P(('dp', 'cp')), may hold values from -1 to 1
- mlp_gain_one: bfloat16 [1024], P(('dp', 'cp')), may hold values from 0.5 to 1.5
- inner_one: bfloat16 [1024, 4096], P(('dp', 'cp')), may hold values from -0.1875 to 0.1875
- outer_one: bfloat16 [4096, 1024], P(('dp', 'cp')), may hold values from -0.09375 to 0.09375
- bias_table: bfloat16 [512], P(('dp', 'cp')), may hold values from -4 to 4
- attn_gain_two: bfloat16 [1024], P(('dp', 'cp')), may hold values from 0.5 to 1.5
- query_two: bfloat16 [1024, 1024], P(('dp', 'cp')), may hold values from -0.0234375 to 0.0234375
- key_two: bfloat16 [1024, 1024], P(('dp', 'cp')), may hold values from -0.1875 to 0.1875
- value_two: bfloat16 [1024, 1024], P(('dp', 'cp')), may hold values from -0.1875 to 0.1875
- output_two: bfloat16 [1024, 1024], P(('dp', 'cp')), may hold values from -1 to 1
- mlp_gain_two: bfloat16 [1024], P(('dp', 'cp')), may hold values from 0.5 to 1.5
- inner_two: bfloat16 [1024, 4096], P(('dp', 'cp')), may hold values from -0.1875 to 0.1875
- outer_two: bfloat16 [4096, 1024], P(('dp', 'cp')), may hold values from -0.09375 to 0.09375
Outputs:
- output: bfloat16 [16, 1024, 1024], P('dp', 'cp')
- input_grad: bfloat16 [16, 1024, 1024], P('dp', 'cp')
- grad_attn_gain_one: float32 [1024], P(('dp', 'cp'))
- grad_query_one: float32 [1024, 1024], P(('dp', 'cp'))
- grad_key_one: float32 [1024, 1024], P(('dp', 'cp'))
- grad_value_one: float32 [1024, 1024], P(('dp', 'cp'))
- grad_output_one: float32 [1024, 1024], P(('dp', 'cp'))
- grad_mlp_gain_one: float32 [1024], P(('dp', 'cp'))
- grad_inner_one: float32 [1024, 4096], P(('dp', 'cp'))
- grad_outer_one: float32 [4096, 1024], P(('dp', 'cp'))
- grad_bias_table: float32 [512], P(('dp', 'cp'))
- grad_attn_gain_two: float32 [1024], P(('dp', 'cp'))
- grad_query_two: float32 [1024, 1024], P(('dp', 'cp'))
- grad_key_two: float32 [1024, 1024], P(('dp', 'cp'))
- grad_value_two: float32 [1024, 1024], P(('dp', 'cp'))
- grad_output_two: float32 [1024, 1024], P(('dp', 'cp'))
- grad_mlp_gain_two: float32 [1024], P(('dp', 'cp'))
- grad_inner_two: float32 [1024, 4096], P(('dp', 'cp'))
- grad_outer_two: float32 [4096, 1024], P(('dp', 'cp'))
Inputs may be any that keep to these rules, and one draw needn't show every extreme that they name: `lengths`: positions at or past a sequence's length are padding; some sequence has length 1024 and some has length 256 in every draw.
All inputs are finite; a program needn't handle non-finite values.
Results may differ from a plain program's by a relative error of at most 0.023.
Values may be sent and summed in bfloat16 or wider, within the bound.
No kernel may reach another device: no remote copies, remote signals or barrier semaphores. Data moves between devices by JAX's collectives and lax.ppermute only.
A program may use at most 384 MiB of HBM per device.

v0:
```python
import jax
import jax.numpy as jnp
from jax import lax
from jax.sharding import PartitionSpec as P

HEAD_COUNT = 16
DK = 64
BUCKET_COUNT = 32
L = 1024
MICRO = 2


EPS = 1e-06
HIGH_PRECISION = lax.Precision.HIGHEST
NEGATIVE = -1e30


def rms_norm(values, norm_gain):
    return values * lax.rsqrt(jnp.mean(values * values, axis=-1, keepdims=True) + EPS) * norm_gain


def smooth_gate(values):
    return jax.nn.gelu(values, approximate=True)


def matmul_rows(left, right):
    return jnp.dot(left, right, preferred_element_type=jnp.float32)


def matmul_left(left, right):
    return lax.dot_general(
        left, right, (((0,), (0,)), ((), ())), preferred_element_type=jnp.float32
    )


def matmul_back(left, right):
    return lax.dot_general(
        left, right, (((1,), (1,)), ((), ())), preferred_element_type=jnp.float32
    )


def lane_rows(piece):
    if piece.ndim == 2:
        return piece.reshape(-1, 128)
    return piece


def restore_shapes(gathered, models):
    return tuple(
        (
            whole.reshape(-1, model.shape[1]) if model.ndim == 2 else whole
            for whole, model in zip(gathered, models)
        )
    )


def gather_forward(shards):
    lanes = tuple((lane_rows(piece) for piece in shards))
    gathered = (
        lax.all_gather(lanes[0], ("dp", "cp"), axis=0, tiled=True),
        lax.all_gather(lanes[1], ("dp", "cp"), axis=0, tiled=True),
        lax.all_gather(lanes[2], ("dp", "cp"), axis=0, tiled=True),
        lax.all_gather(lanes[3], ("dp", "cp"), axis=0, tiled=True),
        lax.all_gather(lanes[4], ("dp", "cp"), axis=0, tiled=True),
        lax.all_gather(lanes[5], ("dp", "cp"), axis=0, tiled=True),
        lax.all_gather(lanes[6], ("dp", "cp"), axis=0, tiled=True),
        lax.all_gather(lanes[7], ("dp", "cp"), axis=0, tiled=True),
        lax.all_gather(lanes[8], ("dp", "cp"), axis=0, tiled=True),
        lax.all_gather(lanes[9], ("dp", "cp"), axis=0, tiled=True),
        lax.all_gather(lanes[10], ("dp", "cp"), axis=0, tiled=True),
        lax.all_gather(lanes[11], ("dp", "cp"), axis=0, tiled=True),
        lax.all_gather(lanes[12], ("dp", "cp"), axis=0, tiled=True),
        lax.all_gather(lanes[13], ("dp", "cp"), axis=0, tiled=True),
        lax.all_gather(lanes[14], ("dp", "cp"), axis=0, tiled=True),
        lax.all_gather(lanes[15], ("dp", "cp"), axis=0, tiled=True),
        lax.all_gather(lanes[16], ("dp", "cp"), axis=0, tiled=True),
    )
    return restore_shapes(gathered, shards)


def masked_scores(query_heads, key_heads, relative_bias, key_valid):
    scores = (
        jnp.einsum("sqhd,skhd->shqk", query_heads, key_heads, preferred_element_type=jnp.float32)
        + relative_bias[None]
    )
    return jnp.where(key_valid[:, None, None, :], scores, NEGATIVE)


def layer_forward(flat_rows, seq_count, params, relative_bias, key_valid):
    attn_gain, w_query, w_key, w_value, w_output, mlp_gain, w_inner, w_outer = params
    row_count, model_width = flat_rows.shape
    local_len = row_count // seq_count
    normed = rms_norm(flat_rows, attn_gain.astype(jnp.float32)).astype(jnp.bfloat16)
    queries = matmul_rows(normed, w_query).astype(jnp.bfloat16)
    key_rows = matmul_rows(normed, w_key).astype(jnp.bfloat16)
    value_rows = matmul_rows(normed, w_value).astype(jnp.bfloat16)
    key_all, value_all = (
        lax.all_gather(
            key_rows.reshape(seq_count, local_len, model_width), "cp", axis=1, tiled=True
        ),
        lax.all_gather(
            value_rows.reshape(seq_count, local_len, model_width), "cp", axis=1, tiled=True
        ),
    )
    query_heads = queries.reshape(seq_count, local_len, HEAD_COUNT, DK)
    key_heads = key_all.reshape(seq_count, L, HEAD_COUNT, DK)
    value_heads = value_all.reshape(seq_count, L, HEAD_COUNT, DK)
    scores = masked_scores(query_heads, key_heads, relative_bias, key_valid)
    top_score = jnp.max(scores, axis=-1, keepdims=True)
    exp_scores = jnp.exp(scores - top_score)
    exp_total = jnp.sum(exp_scores, axis=-1, keepdims=True)
    log_total = (top_score + jnp.log(exp_total))[..., 0]
    probabilities = (exp_scores / exp_total).astype(jnp.bfloat16)
    context = jnp.einsum(
        "shqk,skhd->sqhd", probabilities, value_heads, preferred_element_type=jnp.float32
    )
    context = context.reshape(row_count, model_width).astype(jnp.bfloat16)
    attended = flat_rows + matmul_rows(context, w_output)
    normed_mlp = rms_norm(attended, mlp_gain.astype(jnp.float32)).astype(jnp.bfloat16)
    pre_act = matmul_rows(normed_mlp, w_inner)
    hidden = smooth_gate(pre_act).astype(jnp.bfloat16)
    result = attended + matmul_rows(hidden, w_outer)
    saved_state = (
        flat_rows,
        normed,
        query_heads,
        key_heads,
        value_heads,
        log_total,
        context,
        attended,
        normed_mlp,
        pre_act,
        hidden,
    )
    return (result, saved_state)


def layer_backward(grad_out, params, saved_state, relative_bias, key_valid):
    attn_gain, w_query, w_key, w_value, w_output, mlp_gain, w_inner, w_outer = params
    (
        flat_rows,
        normed,
        query_heads,
        key_heads,
        value_heads,
        log_total,
        context,
        attended,
        normed_mlp,
        pre_act,
        hidden,
    ) = saved_state
    row_count, model_width = flat_rows.shape
    seq_count, local_len = (query_heads.shape[0], query_heads.shape[1])
    grad_low = grad_out.astype(jnp.bfloat16)
    grad_outer = matmul_left(hidden, grad_low)
    grad_hidden = matmul_back(grad_low, w_outer)
    _, pull_gate = jax.vjp(smooth_gate, pre_act)
    grad_pre = pull_gate(grad_hidden)[0].astype(jnp.bfloat16)
    grad_inner = matmul_left(normed_mlp, grad_pre)
    grad_normed_mlp = matmul_back(grad_pre, w_inner)
    _, pull_mlp = jax.vjp(rms_norm, attended, mlp_gain.astype(jnp.float32))
    grad_branch, grad_mlp_gain = pull_mlp(grad_normed_mlp)
    grad_attended = grad_out + grad_branch
    attn_low = grad_attended.astype(jnp.bfloat16)
    grad_output = matmul_left(context, attn_low)
    grad_context = (
        matmul_back(attn_low, w_output)
        .astype(jnp.bfloat16)
        .reshape(seq_count, local_len, HEAD_COUNT, DK)
    )
    scores = masked_scores(query_heads, key_heads, relative_bias, key_valid)
    probs_again = jnp.exp(scores - log_total[..., None])
    grad_probs = jnp.einsum(
        "sqhd,skhd->shqk", grad_context, value_heads, preferred_element_type=jnp.float32
    )
    inner_sum = jnp.sum(grad_probs * probs_again, axis=-1, keepdims=True)
    grad_scores = (probs_again * (grad_probs - inner_sum)).astype(jnp.bfloat16)
    grad_query = jnp.einsum(
        "shqk,skhd->sqhd", grad_scores, key_heads, preferred_element_type=jnp.float32
    )
    grad_query = grad_query.astype(jnp.bfloat16).reshape(row_count, model_width)
    probs_low = probs_again.astype(jnp.bfloat16)
    value_part = jnp.einsum(
        "shqk,sqhd->skhd", probs_low, grad_context, preferred_element_type=jnp.float32
    )
    key_part = jnp.einsum(
        "shqk,sqhd->skhd", grad_scores, query_heads, preferred_element_type=jnp.float32
    )
    grad_key, grad_value = (
        lax.psum_scatter(
            key_part.reshape(seq_count, L, model_width).astype(jnp.bfloat16),
            "cp",
            scatter_dimension=1,
            tiled=True,
        ).astype(jnp.float32),
        lax.psum_scatter(
            value_part.reshape(seq_count, L, model_width).astype(jnp.bfloat16),
            "cp",
            scatter_dimension=1,
            tiled=True,
        ).astype(jnp.float32),
    )
    grad_key = grad_key.astype(jnp.bfloat16).reshape(row_count, model_width)
    grad_value = grad_value.astype(jnp.bfloat16).reshape(row_count, model_width)
    grad_wquery = matmul_left(normed, grad_query)
    grad_wkey = matmul_left(normed, grad_key)
    grad_wvalue = matmul_left(normed, grad_value)
    grad_normed = (
        matmul_back(grad_query, w_query)
        + matmul_back(grad_key, w_key)
        + matmul_back(grad_value, w_value)
    )
    _, pull_attn = jax.vjp(rms_norm, flat_rows, attn_gain.astype(jnp.float32))
    grad_flat, grad_attn_gain = pull_attn(grad_normed)
    grad_input = grad_attended + grad_flat
    score_sum = jnp.sum(grad_scores.astype(jnp.float32), axis=0)
    layer_grads = (
        grad_attn_gain,
        grad_wquery,
        grad_wkey,
        grad_wvalue,
        grad_output,
        grad_mlp_gain,
        grad_inner,
        grad_outer,
    )
    return (grad_input, layer_grads, score_sum)


def body(
    inputs,
    cotangent,
    lengths,
    bucket_ids,
    attn_gain_one,
    query_one,
    key_one,
    value_one,
    output_one,
    mlp_gain_one,
    inner_one,
    outer_one,
    bias_table,
    attn_gain_two,
    query_two,
    key_two,
    value_two,
    output_two,
    mlp_gain_two,
    inner_two,
    outer_two,
):
    shards = (
        attn_gain_one,
        query_one,
        key_one,
        value_one,
        output_one,
        mlp_gain_one,
        inner_one,
        outer_one,
        bias_table,
        attn_gain_two,
        query_two,
        key_two,
        value_two,
        output_two,
        mlp_gain_two,
        inner_two,
        outer_two,
    )
    seq_dev, local_len, model_width = inputs.shape
    seq_batch = seq_dev // MICRO
    row_count = seq_batch * local_len
    start_pos = lax.axis_index("cp") * local_len
    query_pos = start_pos + jnp.arange(local_len, dtype=jnp.int32)
    key_pos = jnp.arange(L, dtype=jnp.int32)
    offsets = key_pos[None, :] - query_pos[:, None] + (L - 1)
    local_ids = jnp.take(bucket_ids, offsets, axis=0)
    bucket_range = jnp.arange(BUCKET_COUNT, dtype=jnp.int32)
    bucket_indicator = (local_ids[None, :, :] == bucket_range[:, None, None]).astype(jnp.float32)
    grad_sums = None
    score_denominator = jnp.zeros((HEAD_COUNT, local_len, L), jnp.float32)
    relative_bias = None
    outputs = []
    input_grads = []
    for batch_index in range(MICRO):
        picked = slice(batch_index * seq_batch, (batch_index + 1) * seq_batch)
        seq_lengths = lengths[picked]
        key_valid = key_pos[None, :] < seq_lengths[:, None]
        row_valid = (query_pos[None, :] < seq_lengths[:, None]).astype(jnp.float32)[:, :, None]
        forward_weights = gather_forward(shards)
        if batch_index == 0:
            bucket_table = forward_weights[8].astype(jnp.float32).reshape(HEAD_COUNT, BUCKET_COUNT)
            relative_bias = jnp.einsum(
                "dez,fd->fez", bucket_indicator, bucket_table, precision=HIGH_PRECISION
            )
        layer_input = inputs[picked].astype(jnp.float32).reshape(row_count, model_width)
        middle, saved_one = layer_forward(
            layer_input, seq_batch, forward_weights[0:8], relative_bias, key_valid
        )
        final_state, saved_two = layer_forward(
            middle, seq_batch, forward_weights[9:17], relative_bias, key_valid
        )
        final_state = final_state.reshape(seq_batch, local_len, model_width) * row_valid
        outputs.append(final_state.astype(jnp.bfloat16))
        grad_final = (cotangent[picked].astype(jnp.float32) * row_valid).reshape(
            row_count, model_width
        )
        grad_middle, grads_two, scores_two = layer_backward(
            grad_final, forward_weights[9:17], saved_two, relative_bias, key_valid
        )
        grad_state, grads_one, scores_one = layer_backward(
            grad_middle, forward_weights[0:8], saved_one, relative_bias, key_valid
        )
        input_grads.append(
            grad_state.reshape(seq_batch, local_len, model_width).astype(jnp.bfloat16)
        )
        score_denominator = score_denominator + scores_one + scores_two
        batch_grads = grads_one + grads_two
        if grad_sums is None:
            grad_sums = batch_grads
        else:
            grad_sums = tuple(
                (grad_total + grad_part for grad_total, grad_part in zip(grad_sums, batch_grads))
            )
    bucket_table_grad = jnp.einsum(
        "dey,cey->dc", score_denominator, bucket_indicator, precision=HIGH_PRECISION
    ).reshape(HEAD_COUNT * BUCKET_COUNT)
    totals = (
        grad_sums[0],
        grad_sums[1],
        grad_sums[2],
        grad_sums[3],
        grad_sums[4],
        grad_sums[5],
        grad_sums[6],
        grad_sums[7],
        bucket_table_grad,
        grad_sums[8],
        grad_sums[9],
        grad_sums[10],
        grad_sums[11],
        grad_sums[12],
        grad_sums[13],
        grad_sums[14],
        grad_sums[15],
    )
    lanes = tuple((lane_rows(total) for total in totals))
    summed = (
        lax.psum_scatter(lanes[0], ("dp", "cp"), scatter_dimension=0, tiled=True),
        lax.psum_scatter(lanes[1], ("dp", "cp"), scatter_dimension=0, tiled=True),
        lax.psum_scatter(lanes[2], ("dp", "cp"), scatter_dimension=0, tiled=True),
        lax.psum_scatter(lanes[3], ("dp", "cp"), scatter_dimension=0, tiled=True),
        lax.psum_scatter(lanes[4], ("dp", "cp"), scatter_dimension=0, tiled=True),
        lax.psum_scatter(lanes[5], ("dp", "cp"), scatter_dimension=0, tiled=True),
        lax.psum_scatter(lanes[6], ("dp", "cp"), scatter_dimension=0, tiled=True),
        lax.psum_scatter(lanes[7], ("dp", "cp"), scatter_dimension=0, tiled=True),
        lax.psum_scatter(lanes[8], ("dp", "cp"), scatter_dimension=0, tiled=True),
        lax.psum_scatter(lanes[9], ("dp", "cp"), scatter_dimension=0, tiled=True),
        lax.psum_scatter(lanes[10], ("dp", "cp"), scatter_dimension=0, tiled=True),
        lax.psum_scatter(lanes[11], ("dp", "cp"), scatter_dimension=0, tiled=True),
        lax.psum_scatter(lanes[12], ("dp", "cp"), scatter_dimension=0, tiled=True),
        lax.psum_scatter(lanes[13], ("dp", "cp"), scatter_dimension=0, tiled=True),
        lax.psum_scatter(lanes[14], ("dp", "cp"), scatter_dimension=0, tiled=True),
        lax.psum_scatter(lanes[15], ("dp", "cp"), scatter_dimension=0, tiled=True),
        lax.psum_scatter(lanes[16], ("dp", "cp"), scatter_dimension=0, tiled=True),
    )
    reduced = restore_shapes(summed, totals)
    output_local = jnp.concatenate(outputs, axis=0)
    input_local = jnp.concatenate(input_grads, axis=0)
    return (
        output_local,
        input_local,
        reduced[0],
        reduced[1],
        reduced[2],
        reduced[3],
        reduced[4],
        reduced[5],
        reduced[6],
        reduced[7],
        reduced[8],
        reduced[9],
        reduced[10],
        reduced[11],
        reduced[12],
        reduced[13],
        reduced[14],
        reduced[15],
        reduced[16],
    )


def solution(mesh):
    return jax.shard_map(
        body,
        mesh=mesh,
        in_specs=(
            P("dp", "cp", None),
            P("dp", "cp", None),
            P("dp"),
            P(),
            P(("dp", "cp")),
            P(("dp", "cp"), None),
            P(("dp", "cp"), None),
            P(("dp", "cp"), None),
            P(("dp", "cp"), None),
            P(("dp", "cp")),
            P(("dp", "cp"), None),
            P(("dp", "cp"), None),
            P(("dp", "cp")),
            P(("dp", "cp")),
            P(("dp", "cp"), None),
            P(("dp", "cp"), None),
            P(("dp", "cp"), None),
            P(("dp", "cp"), None),
            P(("dp", "cp")),
            P(("dp", "cp"), None),
            P(("dp", "cp"), None),
        ),
        out_specs=(
            P("dp", "cp", None),
            P("dp", "cp", None),
            P(("dp", "cp")),
            P(("dp", "cp"), None),
            P(("dp", "cp"), None),
            P(("dp", "cp"), None),
            P(("dp", "cp"), None),
            P(("dp", "cp")),
            P(("dp", "cp"), None),
            P(("dp", "cp"), None),
            P(("dp", "cp")),
            P(("dp", "cp")),
            P(("dp", "cp"), None),
            P(("dp", "cp"), None),
            P(("dp", "cp"), None),
            P(("dp", "cp"), None),
            P(("dp", "cp")),
            P(("dp", "cp"), None),
            P(("dp", "cp"), None),
        ),
        check_vma=False,
    )
```

profile of v0, /device:TPU:0, one launch (start us, length us, event | category | flops | bytes accessed | tf_op | source)
XLA Modules:
  0.0 4250.3 jit_solution(11830299508541235294)
XLA Ops:
  19.4 42.7 %all-reduce.11 = (bf16[1024]{0:T(1024)(128)(2,1)S(1)}, bf16[512]{0:T(512)(128)(2,1)}, bf16[1024]{0:T(1024)(128)(2,1)}, bf16[1024]{0:T(1024)(128)(2,1)}, bf16[1024]{0:T(1024)(128)(2,1)}) all-reduce(bf16[1024]{0:T(1024)(128)(2,1)S(1)} %dynamic-update-slice, ...), channel_id=1, replica_groups=mesh['dp'=8,'cp'=4] {'dp','cp'}, use_global_device_ids=true, to_apply=%add | all-reduce | flops 4608 | bytes 18432
  75.5 54.0 %all-gather.33.cloned.1.call-done = bf16[8192,128]{1,0:T(8,128)(2,1)} async-done(((bf16[256,128]{1,0:T(8,128)(2,1)}), bf16[8192,128]{1,0:T(8,128)(2,1)}) %all-gather.33.cloned.1.call-update) | async-done | bytes 2097168 | tf_op jit(solution)/shard_map/all_gather | solution.py:62
  150.7 1449.2 %gather_fusion = s32[262144]{0:T(1024)S(1)} fusion(s32[2047]{0:T(1024)S(1)} %copy-done, s32[262144]{0:T(1024)S(1)} %broadcast_clamp_fusion), kind=kCustom, calls=%fused_computation | custom fusion | bytes 3145728 | tf_op jit(solution)/shard_map/jit(_take)/gather | solution.py:281
  1646.0 24.2 fusion.211
  1687.3 21.2 fusion.212
  1832.9 22.0 fusion.213
  1882.6 21.7 fusion.214
  2074.7 22.6 reduce-scatter.21.cloned.1.call-done
  2100.2 31.1 reduce-scatter.23.cloned.1.call-done
  2202.7 39.9 convert_add_fusion
  2482.4 18.1 reshape.1302
  2556.7 21.8 fusion.87
  2585.2 40.1 all-reduce.10
  2629.8 35.2 reduce-scatter.55.cloned.1.call-done
  2669.8 134.6 %reduce-scatter.37.cloned.1.call-done = f32[256,128]{1,0:T(8,128)} async-done(((f32[8192,128]{1,0:T(8,128)}), f32[256,128]{1,0:T(8,128)}) %reduce-scatter.37.cloned.1.call-update) | async-done | bytes 131088 | tf_op jit(solution)/shard_map/reduce_scatter | solution.py:354
  2806.0 137.7 %reduce-scatter.43.cloned.1.call-done = f32[256,128]{1,0:T(8,128)} async-done(((f32[8192,128]{1,0:T(8,128)}), f32[256,128]{1,0:T(8,128)}) %reduce-scatter.43.cloned.1.call-update) | async-done | bytes 131088 | tf_op jit(solution)/shard_map/reduce_scatter | solution.py:357
  2945.3 137.5 %reduce-scatter.51.cloned.1.call-done = f32[256,128]{1,0:T(8,128)} async-done(((f32[8192,128]{1,0:T(8,128)}), f32[256,128]{1,0:T(8,128)}) %reduce-scatter.51.cloned.1.call-update) | async-done | bytes 131088 | tf_op jit(solution)/shard_map/reduce_scatter | solution.py:364
  3084.4 137.6 %reduce-scatter.53.cloned.1.call-done = f32[256,128]{1,0:T(8,128)} async-done(((f32[8192,128]{1,0:T(8,128)}), f32[256,128]{1,0:T(8,128)}) %reduce-scatter.53.cloned.1.call-update) | async-done | bytes 131088 | tf_op jit(solution)/shard_map/reduce_scatter | solution.py:365
  3223.6 137.5 %reduce-scatter.39.cloned.1.call-done = f32[256,128]{1,0:T(8,128)} async-done(((f32[8192,128]{1,0:T(8,128)}), f32[256,128]{1,0:T(8,128)}) %reduce-scatter.39.cloned.1.call-update) | async-done | bytes 131088 | tf_op jit(solution)/shard_map/reduce_scatter | solution.py:355
  3362.7 137.2 %reduce-scatter.41.cloned.1.call-done = f32[256,128]{1,0:T(8,128)} async-done(((f32[8192,128]{1,0:T(8,128)}), f32[256,128]{1,0:T(8,128)}) %reduce-scatter.41.cloned.1.call-update) | async-done | bytes 131088 | tf_op jit(solution)/shard_map/reduce_scatter | solution.py:356
  3501.5 179.6 %reduce-scatter.57.cloned.1.call-done = f32[1024,128]{1,0:T(8,128)} async-done(((f32[32768,128]{1,0:T(8,128)}), f32[1024,128]{1,0:T(8,128)}) %reduce-scatter.57.cloned.1.call-update) | async-done | bytes 524304 | tf_op jit(solution)/shard_map/reduce_scatter | solution.py:368
  3683.0 184.5 %reduce-scatter.59.cloned.1.call-done = f32[1024,128]{1,0:T(8,128)} async-done(((f32[32768,128]{1,0:T(8,128)}), f32[1024,128]{1,0:T(8,128)}) %reduce-scatter.59.cloned.1.call-update) | async-done | bytes 524304 | tf_op jit(solution)/shard_map/reduce_scatter | solution.py:369
  3869.5 185.1 %reduce-scatter.45.cloned.1.call-done = f32[1024,128]{1,0:T(8,128)} async-done(((f32[32768,128]{1,0:T(8,128)}), f32[1024,128]{1,0:T(8,128)}) %reduce-scatter.45.cloned.1.call-update) | async-done | bytes 524304 | tf_op jit(solution)/shard_map/reduce_scatter | solution.py:359
  4056.5 184.8 %reduce-scatter.47.cloned.1.call-done = f32[1024,128]{1,0:T(8,128)} async-done(((f32[32768,128]{1,0:T(8,128)}), f32[1024,128]{1,0:T(8,128)}) %reduce-scatter.47.cloned.1.call-update) | async-done | bytes 524304 | tf_op jit(solution)/shard_map/reduce_scatter | solution.py:360
  (761 shorter events, 832.6 us)
Async XLA Ops:
  10.4 1601.5 %all-gather.31.cloned.1.call-start = ((), (), s32[]{:S(2)}) async-start(), calls=%async_computation.21 | async-start | bytes 2162688 | tf_op jit(solution)/shard_map/all_gather | solution.py:61
  12.0 1610.2 %all-gather.35.cloned.1.call-start = ((), (), s32[]{:S(2)}) async-start(), calls=%async_computation.23 | async-start | bytes 2162688 | tf_op jit(solution)/shard_map/all_gather | solution.py:64
  13.6 1611.5 %all-gather.45.cloned.1.call-start = ((), (), s32[]{:S(2)}) async-start(), calls=%async_computation.28 | async-start | bytes 2162688 | tf_op jit(solution)/shard_map/all_gather | solution.py:71
  15.2 1614.5 %all-gather.61.cloned.1.call-start = ((), (), s32[]{:S(2)}) async-start(), calls=%async_computation.56 | async-start | bytes 2621440 | tf_op jit(solution)/shard_map/all_gather | solution.py:101
  75.5 1558.1 %all-gather.63.cloned.1.call-start = ((), (), s32[]{:S(2)}) async-start(), calls=%async_computation.57 | async-start | bytes 2621440 | tf_op jit(solution)/shard_map/all_gather | solution.py:98
  134.0 1503.5 %all-gather.53.cloned.1.call-start = ((), (), s32[]{:S(2)}) async-start(), calls=%async_computation.52 | async-start | bytes 2621440 | tf_op jit(solution)/shard_map/all_gather | solution.py:101
  137.4 1504.1 %all-gather.55.cloned.1.call-start = ((), (), s32[]{:S(2)}) async-start(), calls=%async_computation.53 | async-start | bytes 2621440 | tf_op jit(solution)/shard_map/all_gather | solution.py:98
  139.0 1586.2 %all-gather.39.cloned.1.call-start = ((), (), s32[]{:S(2)}) async-start(), calls=%async_computation.25 | async-start | bytes 8650752 | tf_op jit(solution)/shard_map/all_gather | solution.py:67
  139.9 1599.1 %all-gather.37.cloned.1.call-start = ((), (), s32[]{:S(2)}) async-start(), calls=%async_computation.24 | async-start | bytes 8650752 | tf_op jit(solution)/shard_map/all_gather | solution.py:66
  141.8 1628.9 %all-gather.41.cloned.1.call-start = ((), (), s32[]{:S(2)}) async-start(), calls=%async_computation.26 | async-start | bytes 2162688 | tf_op jit(solution)/shard_map/all_gather | solution.py:72
  142.5 1638.7 %all-gather.43.cloned.1.call-start = ((), (), s32[]{:S(2)}) async-start(), calls=%async_computation.27 | async-start | bytes 2162688 | tf_op jit(solution)/shard_map/all_gather | solution.py:70
  143.3 1642.1 %all-gather.47.cloned.1.call-start = ((), (), s32[]{:S(2)}) async-start(), calls=%async_computation.29 | async-start | bytes 2162688 | tf_op jit(solution)/shard_map/all_gather | solution.py:73
  144.8 1657.2 %all-gather.51.cloned.1.call-start = ((), (), s32[]{:S(2)}) async-start(), calls=%async_computation.31 | async-start | bytes 8650752 | tf_op jit(solution)/shard_map/all_gather | solution.py:76
  146.7 1668.9 %all-gather.49.cloned.1.call-start = ((), (), s32[]{:S(2)}) async-start(), calls=%async_computation.30 | async-start | bytes 8650752 | tf_op jit(solution)/shard_map/all_gather | solution.py:75
  148.5 1680.5 %all-gather.67.cloned.1.call-start = ((), (), s32[]{:S(2)}) async-start(), calls=%async_computation.59 | async-start | bytes 2621440 | tf_op jit(solution)/shard_map/all_gather | solution.py:98
  2317.8 625.9 %reduce-scatter.43.cloned.1.call-start = ((), (), s32[]{:S(2)}) async-start(), calls=%async_computation.43 | async-start | bytes 4325376 | tf_op jit(solution)/shard_map/reduce_scatter | solution.py:357
  2328.7 754.1 %reduce-scatter.51.cloned.1.call-start = ((), (), s32[]{:S(2)}) async-start(), calls=%async_computation.47 | async-start | bytes 4325376 | tf_op jit(solution)/shard_map/reduce_scatter | solution.py:364
  2338.5 883.4 %reduce-scatter.53.cloned.1.call-start = ((), (), s32[]{:S(2)}) async-start(), calls=%async_computation.48 | async-start | bytes 4325376 | tf_op jit(solution)/shard_map/reduce_scatter | solution.py:365
  2348.0 1013.1 %reduce-scatter.39.cloned.1.call-start = ((), (), s32[]{:S(2)}) async-start(), calls=%async_computation.41 | async-start | bytes 4325376 | tf_op jit(solution)/shard_map/reduce_scatter | solution.py:355
  2362.3 1137.6 %reduce-scatter.41.cloned.1.call-start = ((), (), s32[]{:S(2)}) async-start(), calls=%async_computation.42 | async-start | bytes 4325376 | tf_op jit(solution)/shard_map/reduce_scatter | solution.py:356
  2392.9 1288.2 %reduce-scatter.57.cloned.1.call-start = ((), (), s32[]{:S(2)}) async-start(), calls=%async_computation.50 | async-start | bytes 17301504 | tf_op jit(solution)/shard_map/reduce_scatter | solution.py:368
  2426.0 1441.6 %reduce-scatter.59.cloned.1.call-start = ((), (), s32[]{:S(2)}) async-start(), calls=%async_computation.51 | async-start | bytes 17301504 | tf_op jit(solution)/shard_map/reduce_scatter | solution.py:369
  2467.4 1587.2 %reduce-scatter.45.cloned.1.call-start = ((), (), s32[]{:S(2)}) async-start(), calls=%async_computation.44 | async-start | bytes 17301504 | tf_op jit(solution)/shard_map/reduce_scatter | solution.py:359
  2500.5 1740.8 %reduce-scatter.47.cloned.1.call-start = ((), (), s32[]{:S(2)}) async-start(), calls=%async_computation.45 | async-start | bytes 17301504 | tf_op jit(solution)/shard_map/reduce_scatter | solution.py:360
  (228 other events, 14303.5 us)
Sparse Core Ops, SparseCore 0:
  11.5 59.5 all-gather.28
  74.5 55.0 all-gather.32
  133.0 55.2 all-gather.30
  191.6 55.2 all-gather.34
  250.1 55.2 all-gather.44
  405.9 77.4 all-gather.38
  486.2 76.0 all-gather.36
  565.6 54.9 all-gather.40
  624.0 55.2 all-gather.42
  682.6 55.2 all-gather.46
  740.6 76.2 all-gather.50
  819.6 76.0 all-gather.48
  2385.0 140.9 reduce-scatter.48
  2528.1 136.8 reduce-scatter.54
  2667.3 137.0 reduce-scatter.36
  2806.7 136.9 reduce-scatter.42
  2945.8 136.9 reduce-scatter.50
  3085.1 136.8 reduce-scatter.52
  3224.2 136.7 reduce-scatter.38
  3363.2 136.6 reduce-scatter.40
  3502.0 179.0 reduce-scatter.56
  3683.4 184.1 reduce-scatter.58
  3869.7 184.7 reduce-scatter.44
  4056.9 184.3 reduce-scatter.46
  (16 shorter events, 427.6 us)
where the time goes:
time: 4260 us; the launch traced here: 4250 us
  local copies, waits for them, and re-layouts  1760 us (41%)
  waiting for transfers between devices  1720 us (40%)
  matrix products  554 us (13%)
  other arithmetic  104 us (2%)
  blocking collectives  82.8 us (2%)
    gather x2, local copies, waits for them, and re-layouts, body(): local_ids = jnp.take(bucket_ids, offsets, axis=0)  1450 us
    reduce_scatter x1, waiting for transfers between devices, body(): lax.psum_scatter(lanes[6], ('dp', 'cp'), scatter_dimension=0, tiled=True)  185 us
    reduce_scatter x1, waiting for transfers between devices, body(): lax.psum_scatter(lanes[7], ('dp', 'cp'), scatter_dimension=0, tiled=True)  185 us
    reduce_scatter x1, waiting for transfers between devices, body(): lax.psum_scatter(lanes[16], ('dp', 'cp'), scatter_dimension=0, tiled=True)  185 us
    reduce_scatter x1, waiting for transfers between devices, body(): lax.psum_scatter(lanes[15], ('dp', 'cp'), scatter_dimension=0, tiled=True)  180 us
    reduce_scatter x1, waiting for transfers between devices, body(): lax.psum_scatter(lanes[4], ('dp', 'cp'), scatter_dimension=0, tiled=True)  138 us
    reduce_scatter x1, waiting for transfers between devices, body(): lax.psum_scatter(lanes[12], ('dp', 'cp'), scatter_dimension=0, tiled=True)  138 us
    reduce_scatter x1, waiting for transfers between devices, body(): lax.psum_scatter(lanes[11], ('dp', 'cp'), scatter_dimension=0, tiled=True)  138 us
  transfers between devices with their start and end apart: 40, of which 16 were waited for; matrix products, arithmetic and copies ran while one was open for 52% of the time, Pallas kernels for 0%

commit v1 on v0

v1 whole, which is shorter than its diff:
```python
import functools

import jax
import jax.numpy as jnp
import numpy as np
from jax import lax
from jax.experimental import pallas as pl
from jax.experimental.pallas import tpu as pltpu
from jax.sharding import Mesh
from jax.sharding import PartitionSpec as P

DK = 64
TILE = 128
EPS = 1e-06
NEGATIVE = -1e30
HIGH_PRECISION = lax.Precision.HIGHEST


def toeplitz_kernel(span, u_ref, t_ref):
    for e in range(span):
        base = TILE * (span - 1 - e)
        w = jnp.broadcast_to(u_ref[0, :, base:base + 2 * TILE], (TILE, 2 * TILE))
        t_ref[0, e] = pltpu.roll(w, TILE, 1, stride=1, stride_axis=0)[:, :TILE].astype(t_ref.dtype)

def toeplitz_tiles(u):
    heads, width = u.shape
    span = width // TILE - 1
    return pl.pallas_call(
        functools.partial(toeplitz_kernel, span),
        grid=(heads,),
        in_specs=[pl.BlockSpec((1, 1, width), lambda h: (h, 0, 0))],
        out_specs=pl.BlockSpec((1, span, TILE, TILE), lambda h: (h, 0, 0, 0)),
        out_shape=jax.ShapeDtypeStruct((heads, span, TILE, TILE), jnp.bfloat16),
        cost_estimate=pl.CostEstimate(flops=heads * span * TILE * TILE * 4, bytes_accessed=heads * span * TILE * TILE * 2, transcendentals=0),
        name="toeplitz",
    )(u.reshape(heads, 1, width))

def head_lanes(h, x):
    lane = lax.broadcasted_iota(jnp.int32, x.shape, 1)
    return jnp.where((lane // DK) == h, x, jnp.zeros_like(x))

def dot_nt(a, b):
    return lax.dot_general(a, b, (((1,), (1,)), ((), ())), preferred_element_type=jnp.float32)

def dot_tn(a, b):
    return lax.dot_general(a, b, (((0,), (0,)), ((), ())), preferred_element_type=jnp.float32)

def dot_nn(a, b):
    return lax.dot_general(a, b, (((1,), (0,)), ((), ())), preferred_element_type=jnp.float32)

def key_chunks(parts, rows, chunk):
    return [(i, s) for i in range(parts) for s in range(0, rows, chunk)]

def chunk_scores(pos_ref, k_chunk, q_head, bias_ref, h, c, chunk, blk, q_rows):
    n = chunk // blk
    sub = blk // TILE
    nq = q_rows // blk
    s = dot_nt(k_chunk, q_head)
    half = bias_ref.shape[1] // 2
    rows = []
    for kb in range(n):
        kpos = pos_ref[1 + nq + c * n + kb]
        for kk in range(sub):
            cols = []
            for qb in range(nq):
                e0 = (kpos - pos_ref[1 + qb]) + half + kk
                for qq in range(sub):
                    cols.append(bias_ref[h, e0 - qq])
            rows.append(jnp.concatenate(cols, axis=1))
    bias = jnp.concatenate(rows, axis=0).astype(jnp.float32)
    s = s + bias
    valid = []
    for kb in range(n):
        limit = pos_ref[0] - pos_ref[1 + nq + c * n + kb] * TILE
        valid.append(lax.broadcasted_iota(jnp.int32, (blk, 1), 0) < limit)
    ok = valid[0] if n == 1 else jnp.concatenate([v.astype(jnp.int32) for v in valid], axis=0) > 0
    return s, ok

def attn_fwd_kernel(parts, chunk, blk, pos_ref, q_ref, *refs):
    k_refs, v_refs = refs[:parts], refs[parts:2 * parts]
    bias_ref, o_ref, lse_ref, s_ref = refs[2 * parts:]
    q_rows = q_ref.shape[0]
    rows = k_refs[0].shape[0]
    chunks = key_chunks(parts, rows, chunk)
    outs = []
    for h in range(2):
        qh = head_lanes(h, q_ref[...])
        top = None
        for c, (i, s0) in enumerate(chunks):
            s, ok = chunk_scores(pos_ref, k_refs[i][s0:s0 + chunk, :], qh, bias_ref, h, c, chunk, blk, q_rows)
            s = jnp.where(ok, s, NEGATIVE)
            s_ref[c * chunk:(c + 1) * chunk, :] = s
            m = jnp.max(s, axis=0, keepdims=True)
            top = m if top is None else jnp.maximum(top, m)
        total = jnp.zeros((1, q_rows), jnp.float32)
        acc = jnp.zeros((2 * DK, q_rows), jnp.float32)
        for c, (i, s0) in enumerate(chunks):
            p = jnp.exp(s_ref[c * chunk:(c + 1) * chunk, :] - top)
            total = total + jnp.sum(p, axis=0, keepdims=True)
            acc = acc + dot_tn(v_refs[i][s0:s0 + chunk, :], p.astype(jnp.bfloat16))
        outs.append((acc / total)[h * DK:(h + 1) * DK])
        lse_ref[0, h:h + 1, :] = top + jnp.log(total)
    o_ref[...] = jnp.concatenate(outs, axis=0).T.astype(o_ref.dtype)

def attn_fwd(pos, q, ks, vs, bias, blk):
    q_rows, width = q.shape
    parts, rows = len(ks), ks[0].shape[0]
    keys = parts * rows
    heads = width // DK
    span = bias.shape[1]
    chunk = min(256, rows)
    spec_q = pl.BlockSpec((q_rows, 2 * DK), lambda p, s: (0, p))
    spec_k = pl.BlockSpec((rows, 2 * DK), lambda p, s: (0, p))
    o, lse = pl.pallas_call(
        functools.partial(attn_fwd_kernel, parts, chunk, blk),
        grid_spec=pltpu.PrefetchScalarGridSpec(
            num_scalar_prefetch=1,
            grid=(heads // 2,),
            in_specs=[spec_q] + [spec_k] * (2 * parts) + [pl.BlockSpec((2, span, TILE, TILE), lambda p, s: (p, 0, 0, 0))],
            out_specs=[spec_q, pl.BlockSpec((1, 2, q_rows), lambda p, s: (p, 0, 0))],
            scratch_shapes=[pltpu.VMEM((keys, q_rows), jnp.float32)],
        ),
        out_shape=[jax.ShapeDtypeStruct((q_rows, width), jnp.bfloat16), jax.ShapeDtypeStruct((heads // 2, 2, q_rows), jnp.float32)],
        compiler_params=pltpu.CompilerParams(vmem_limit_bytes=48 << 20),
        cost_estimate=pl.CostEstimate(flops=16 * q_rows * keys * width, bytes_accessed=4 * keys * width + 4 * q_rows * width + heads * span * TILE * TILE * 2, transcendentals=heads * q_rows * keys),
        name="attn_fwd",
    )(pos, q, *ks, *vs, bias)
    return o, lse

def skew_rows(x):
    width = 2 * x.shape[1]
    x = jnp.concatenate([jnp.zeros_like(x), x], axis=1)
    rows = x.shape[0]
    while rows > 8:
        rows //= 2
        x = x[:rows] + pltpu.roll(x[rows:], width - rows, 1)
    row = lax.broadcasted_iota(jnp.int32, x.shape, 0)
    for bit in (1, 2, 4):
        x = jnp.where((row & bit) != 0, pltpu.roll(x, width - bit, 1), x)
    return x

def attn_bwd_kernel(parts, chunk, blk, pos_ref, q_ref, do_ref, o_ref, lse_ref, *refs):
    k_refs, v_refs = refs[:parts], refs[parts:2 * parts]
    bias_ref, dq_ref = refs[2 * parts:2 * parts + 2]
    dk_refs, dv_refs = refs[2 * parts + 2:3 * parts + 2], refs[3 * parts + 2:4 * parts + 2]
    d_ref, e_ref = refs[4 * parts + 2:]
    q_rows = q_ref.shape[0]
    rows = k_refs[0].shape[0]
    chunks = key_chunks(parts, rows, chunk)
    span = bias_ref.shape[1]
    half = span // 2
    n, sub, nq = chunk // blk, blk // TILE, q_rows // blk
    prod = (do_ref[...].astype(jnp.float32) * o_ref[...].astype(jnp.float32)).T
    outs = []
    for h in range(2):
        qh = head_lanes(h, q_ref[...])
        doh = head_lanes(h, do_ref[...])
        inner = jnp.sum(prod[h * DK:(h + 1) * DK], axis=0, keepdims=True)
        lse = lse_ref[0, h:h + 1, :]
        acc = jnp.zeros((2 * DK, q_rows), jnp.float32)
        e_ref[...] = jnp.zeros_like(e_ref)
        for c, (i, s0) in enumerate(chunks):
            k_chunk = k_refs[i][s0:s0 + chunk, :]
            s, ok = chunk_scores(pos_ref, k_chunk, qh, bias_ref, h, c, chunk, blk, q_rows)
            p = jnp.where(ok, jnp.exp(s - lse), 0.0)
            dp = dot_nt(v_refs[i][s0:s0 + chunk, :], doh)
            ds = p * (dp - inner)
            dsb = ds.astype(jnp.bfloat16)
            dv = dot_nn(p.astype(jnp.bfloat16), doh)
            dk = dot_nn(dsb, qh)
            at = pl.ds(s0, chunk)
            if h == 0:
                dk_refs[i][at, :] = dk.astype(jnp.bfloat16)
                dv_refs[i][at, :] = dv.astype(jnp.bfloat16)
            else:
                dk_refs[i][at, :] = (dk_refs[i][at, :].astype(jnp.float32) + dk).astype(jnp.bfloat16)
                dv_refs[i][at, :] = (dv_refs[i][at, :].astype(jnp.float32) + dv).astype(jnp.bfloat16)
            acc = acc + dot_tn(k_chunk, dsb)
            for kb in range(n):
                kpos = pos_ref[1 + nq + c * n + kb]
                for qb in range(nq):
                    e0 = (kpos - pos_ref[1 + qb]) + half
                    for d in range(1 - sub, sub):
                        tot = None
                        for kk in range(sub):
                            qq = kk - d
                            if 0 <= qq < sub:
                                r0, c0 = kb * blk + kk * TILE, qb * blk + qq * TILE
                                t = ds[r0:r0 + TILE, c0:c0 + TILE]
                                tot = t if tot is None else tot + t
                        e_ref[e0 + d] += tot
        outs.append(acc[h * DK:(h + 1) * DK])
        pieces = [jnp.zeros((1, TILE), jnp.float32) for _ in range(span + 1)]
        for e in range(span):
            r = jnp.sum(skew_rows(e_ref[e]), axis=0, keepdims=True)
            b = span - 1 - e
            pieces[b] = pieces[b] + r[:, :TILE]
            pieces[b + 1] = pieces[b + 1] + r[:, TILE:]
        d_ref[0, h:h + 1, :] = jnp.concatenate(pieces, axis=1)
    dq_ref[...] = jnp.concatenate(outs, axis=0).T.astype(dq_ref.dtype)

def attn_bwd(pos, q, do, o, lse, ks, vs, bias, blk):
    q_rows, width = q.shape
    parts, rows = len(ks), ks[0].shape[0]
    keys = parts * rows
    heads = width // DK
    span = bias.shape[1]
    chunk = min(256, rows)
    spec_q = pl.BlockSpec((q_rows, 2 * DK), lambda p, s: (0, p))
    spec_k = pl.BlockSpec((rows, 2 * DK), lambda p, s: (0, p))
    spec_l = pl.BlockSpec((1, 2, q_rows), lambda p, s: (p, 0, 0))
    out = pl.pallas_call(
        functools.partial(attn_bwd_kernel, parts, chunk, blk),
        grid_spec=pltpu.PrefetchScalarGridSpec(
            num_scalar_prefetch=1,
            grid=(heads // 2,),
            in_specs=[spec_q, spec_q, spec_q, spec_l] + [spec_k] * (2 * parts) + [pl.BlockSpec((2, span, TILE, TILE), lambda p, s: (p, 0, 0, 0))],
            out_specs=[spec_q] + [spec_k] * (2 * parts) + [pl.BlockSpec((1, 2, (span + 1) * TILE), lambda p, s: (p, 0, 0))],
            scratch_shapes=[pltpu.VMEM((span, TILE, TILE), jnp.float32)],
        ),
        out_shape=[jax.ShapeDtypeStruct((q_rows, width), jnp.bfloat16)]
        + [jax.ShapeDtypeStruct((rows, width), jnp.bfloat16)] * (2 * parts)
        + [jax.ShapeDtypeStruct((heads // 2, 2, (span + 1) * TILE), jnp.float32)],
        compiler_params=pltpu.CompilerParams(vmem_limit_bytes=48 << 20),
        cost_estimate=pl.CostEstimate(flops=40 * q_rows * keys * width, bytes_accessed=8 * keys * width + 8 * q_rows * width + heads * span * TILE * TILE * 2, transcendentals=heads * q_rows * keys),
        name="attn_bwd",
    )(pos, q, do, o, lse, *ks, *vs, bias)
    dq, dks, dvs, d = out[0], out[1:1 + parts], out[1 + parts:1 + 2 * parts], out[-1]
    return dq, dks, dvs, d.reshape(heads, (span + 1) * TILE)


def matmul_rows(left, right):
    return jnp.dot(left, right, preferred_element_type=jnp.float32)


def matmul_left(left, right):
    return lax.dot_general(left, right, (((0,), (0,)), ((), ())), preferred_element_type=jnp.float32)


def matmul_back(left, right):
    return lax.dot_general(left, right, (((1,), (1,)), ((), ())), preferred_element_type=jnp.float32)


def inv_rms(values):
    return lax.rsqrt(jnp.mean(values * values, axis=-1, keepdims=True) + EPS)


def norm_pull(grad, values, gain):
    scale = inv_rms(values)
    weighted = gain * grad
    mean = jnp.mean(weighted * values, axis=-1, keepdims=True)
    grad_in = scale * weighted - values * (scale * scale * scale) * mean
    grad_gain = jnp.sum(grad * values * scale, axis=0)
    return grad_in, grad_gain


def gelu_pair(pre):
    c = np.float32(np.sqrt(2.0 / np.pi))
    sq = pre * pre
    t = jnp.tanh(c * (pre + 0.044715 * (sq * pre)))
    half = 0.5 * (1.0 + t)
    slope = half + (0.5 * c) * pre * (1.0 - t * t) * (1.0 + 0.134145 * sq)
    return (pre * half).astype(jnp.bfloat16), slope.astype(jnp.bfloat16)


SWAP = [(0, 1), (1, 0)]


class Plan:
    def __init__(self, sizes):
        self.nz, self.ny, self.ns, self.m = sizes
        self.nx = self.ns * self.m
        self.z = lax.axis_index("z")
        self.y = lax.axis_index("y")
        self.s = lax.axis_index("s")
        self.q = lax.axis_index("q")
        self.core = lax.axis_index("core")
        self.x = self.s * self.m + self.q
        self.everywhere = ("z", "y", "s", "q", "core")
        self.axes = {"x": (("s", "q") if self.m > 1 else "s", self.nx, self.x), "y": ("y", self.ny, self.y)}

    def block_of(self, order, n):
        n_z = n % self.nz
        n = n // self.nz
        place = {}
        for name in reversed(order):
            _, size, mine = self.axes[name]
            part = n % size
            n = n // size
            place[name] = part ^ mine if size == 2 else part
        core = n ^ self.core
        return ((n_z * self.ny + place["y"]) * self.nx + place["x"]) * 2 + core

    def permutation(self, order, width):
        depth = width // (self.nz * self.ny * self.nx * 2)
        n = lax.broadcasted_iota(jnp.int32, (width, width), 1)
        i = lax.broadcasted_iota(jnp.int32, (width, width), 0)
        source = self.block_of(order, n // depth) * depth + n % depth
        return (i == source).astype(jnp.bfloat16)

    def take_blocks(self, rows, table):
        return jnp.take(rows.reshape(table.shape[0], -1, rows.shape[1]), table, axis=0).reshape(rows.shape)

    def exchange(self, piece, name):
        return lax.ppermute(piece, name, SWAP)

    def scatter_sum(self, product, order, rows):
        half = rows // 2
        other = self.exchange(product(half, rows), "core")
        name_a, size_a, _ = self.axes[order[0]]
        name_b, size_b, _ = self.axes[order[1]]
        low = jnp.bfloat16
        f32 = jnp.float32
        if size_a == 2 and size_b == 2:
            quarter = half // 2
            far = (product(quarter, half).astype(f32) + other[quarter:].astype(f32)).astype(low)
            far = self.exchange(far, name_a)
            near = (product(0, quarter).astype(f32) + other[:quarter].astype(f32)).astype(low)
            eighth = quarter // 2
            side = (near[eighth:].astype(f32) + far[eighth:].astype(f32)).astype(low)
            side = self.exchange(side, name_b)
            total = near[:eighth].astype(f32) + far[:eighth].astype(f32) + side.astype(f32)
            return total.astype(low).reshape(self.nz, eighth // self.nz, -1)
        whole = (product(0, half).astype(f32) + other.astype(f32)).astype(low)
        whole = whole.reshape(size_a, half // size_a, -1)
        whole = lax.psum_scatter(whole, name_a, scatter_dimension=0, tiled=False)
        whole = whole.reshape(size_b, half // (size_a * size_b), -1)
        whole = lax.psum_scatter(whole, name_b, scatter_dimension=0, tiled=False)
        return whole.reshape(self.nz, half // (size_a * size_b * self.nz), -1)

    def sum_z(self, piece):
        if self.nz == 1:
            return piece[0].astype(jnp.float32)
        return lax.psum_scatter(piece, "z", scatter_dimension=0, tiled=False).astype(jnp.float32)

    def to_sequences(self, local):
        own = lax.dynamic_index_in_dim(local, self.s, 0, keepdims=False)
        other = lax.dynamic_index_in_dim(local, 1 - self.s, 0, keepdims=False)
        return jnp.concatenate([own, self.exchange(other, "s")], axis=0)

    def from_sequences(self, rows):
        blk = rows.shape[0] // 2
        own, other = rows[:blk], self.exchange(rows[blk:], "s")
        first = self.s == 0
        return jnp.stack([jnp.where(first, own, other), jnp.where(first, other, own)], axis=0)

    def gather_keys(self, rows):
        if self.m == 1:
            return [rows, self.exchange(rows, "core")]
        return [lax.all_gather(rows, ("q", "core"), axis=0, tiled=True)]

    def reduce_keys(self, parts):
        if self.m == 1:
            return parts[0].astype(jnp.float32) + self.exchange(parts[1], "core").astype(jnp.float32)
        return lax.psum_scatter(parts[0], ("q", "core"), scatter_dimension=0, tiled=True).astype(jnp.float32)

    def positions(self, length, blk):
        unit = blk // TILE
        mine = [(((self.s ^ j) * self.m + self.q) * 2 + self.core) * unit for j in range(2)]
        if self.m == 1:
            keys = [(((self.s ^ j) * self.m + self.q) * 2 + (self.core ^ c)) * unit for c in range(2) for j in range(2)]
        else:
            keys = [(((self.s ^ j) * self.m + q) * 2 + c) * unit for q in range(self.m) for c in range(2) for j in range(2)]
        return jnp.stack([length] + mine + keys).astype(jnp.int32)


def outer_grad_kernel(count, table_ref, *refs):
    left = jnp.concatenate([r[...] for r in refs[:count]], axis=1)
    refs[-1][...] = dot_tn(left, refs[count][...]).astype(refs[-1].dtype)


def outer_grad(hidden, grad_low, table, start, stop):
    rows, width = grad_low.shape
    count = 4 if (stop - start) % 4 == 0 else 1
    steps = (stop - start) // count
    specs = [pl.BlockSpec((rows, TILE), functools.partial(lambda j, i, t: (0, t[start + i * count + j]), j)) for j in range(count)]
    return pl.pallas_call(
        functools.partial(outer_grad_kernel, count),
        grid_spec=pltpu.PrefetchScalarGridSpec(
            num_scalar_prefetch=1,
            grid=(steps,),
            in_specs=specs + [pl.BlockSpec((rows, width), lambda i, t: (0, 0))],
            out_specs=pl.BlockSpec((count * TILE, width), lambda i, t: (i, 0)),
        ),
        out_shape=jax.ShapeDtypeStruct(((stop - start) * TILE, width), jnp.bfloat16),
        compiler_params=pltpu.CompilerParams(vmem_limit_bytes=32 << 20),
        cost_estimate=pl.CostEstimate(flops=2 * rows * width * (stop - start) * TILE, bytes_accessed=2 * (stop - start) * TILE * (rows + width) + 2 * rows * width, transcendentals=0),
        name="outer_grad",
    )(table, *([hidden] * count), grad_low)


def layer_forward(plan, x, weights, pos, bias, blk):
    attn_gain, w_qkv, w_output, mlp_gain, w_inner, w_outer = weights
    width = x.shape[1]
    normed = (x * inv_rms(x) * attn_gain).astype(jnp.bfloat16)
    qkv = matmul_rows(normed, w_qkv).astype(jnp.bfloat16)
    queries = qkv[:, :width]
    kv = plan.gather_keys(qkv[:, width:])
    keys = [p[:, :width] for p in kv]
    values = [p[:, width:] for p in kv]
    context, log_total = attn_fwd(pos, queries, keys, values, bias, blk)
    attended = x + matmul_rows(context, w_output)
    normed_mlp = (attended * inv_rms(attended) * mlp_gain).astype(jnp.bfloat16)
    hidden, slope = gelu_pair(matmul_rows(normed_mlp, w_inner))
    result = attended + matmul_rows(hidden, w_outer)
    return result, (x, normed, queries, keys, values, context, log_total, attended, normed_mlp, hidden, slope)


def layer_backward(plan, grad_out, weights, saved, pos, bias, blk, perms, table, orders):
    attn_gain, w_qkv, w_output, mlp_gain, w_inner, w_outer = weights
    x, normed, queries, keys, values, context, log_total, attended, normed_mlp, hidden, slope = saved
    low = jnp.bfloat16
    width = x.shape[1]
    grad_low = grad_out.astype(low)
    grad_pre = (matmul_back(grad_low, w_outer) * slope.astype(jnp.float32)).astype(low)
    wide = hidden.shape[1]
    if wide // (table[orders[1]].shape[0]) == TILE:
        outer_rows = lambda a, b: outer_grad(hidden, grad_low, table[orders[1]], a // TILE, b // TILE)
    else:
        outer_rows = lambda a, b: plan.take_blocks(matmul_left(hidden, grad_low).astype(low), table[orders[1]])[a:b]
    outer_piece = plan.scatter_sum(outer_rows, orders[1], wide)
    left = matmul_rows(normed_mlp, perms[orders[0]]).astype(low)
    inner_piece = plan.scatter_sum(lambda a, b: matmul_left(left[:, a:b], grad_pre).astype(low), orders[0], width)
    grad_normed_mlp = matmul_back(grad_pre, w_inner)
    grad_branch, grad_mlp_gain = norm_pull(grad_normed_mlp, attended, mlp_gain)
    grad_attended = grad_out + grad_branch
    attn_low = grad_attended.astype(low)
    grad_context = matmul_back(attn_low, w_output).astype(low)
    left_c = matmul_rows(context, perms[orders[2]]).astype(low)
    output_piece = plan.scatter_sum(lambda a, b: matmul_left(left_c[:, a:b], attn_low).astype(low), orders[2], width)
    grad_query, dk, dv, diag = attn_bwd(pos, queries, grad_context, context, log_total, keys, values, bias, blk)
    grad_kv = plan.reduce_keys([jnp.concatenate([a, b], axis=1) for a, b in zip(dk, dv)])
    grad_qkv = jnp.concatenate([grad_query, grad_kv.astype(low)], axis=1)
    left_n = matmul_rows(normed, perms[orders[3]]).astype(low)
    qkv_piece = plan.scatter_sum(lambda a, b: matmul_left(left_n[:, a:b], grad_qkv).astype(low), orders[3], width)
    grad_normed = matmul_back(grad_qkv, w_qkv)
    grad_flat, grad_attn_gain = norm_pull(grad_normed, x, attn_gain)
    attn_sum = plan.sum_z(jnp.concatenate([qkv_piece, output_piece], axis=2))
    grads = (
        grad_attn_gain,
        attn_sum[:, :width],
        attn_sum[:, width:2 * width],
        attn_sum[:, 2 * width:3 * width],
        attn_sum[:, 3 * width:],
        grad_mlp_gain,
        plan.sum_z(inner_piece),
        plan.sum_z(outer_piece),
    )
    return grad_attended + grad_flat, grads, diag


def body(sizes, inputs, cotangent, lengths, bucket_ids, *params):
    plan = Plan(sizes)
    one, bias_table, two = params[:8], params[8], params[9:]
    blk, width = inputs.shape[1], inputs.shape[2]
    f32, low = jnp.float32, jnp.bfloat16
    gains = jnp.stack([one[0], one[5], two[0], two[5]], axis=1)
    rows = gains.shape[0]
    table_column = jnp.pad(bias_table, (0, rows - bias_table.shape[0]))[:, None] if bias_table.shape[0] < rows else bias_table[:rows, None]
    small = jnp.pad(jnp.concatenate([gains, table_column], axis=1), ((0, 0), (0, TILE - 5)))
    everywhere = plan.everywhere

    def gather(piece):
        return lax.all_gather(piece, everywhere, axis=0, tiled=True)

    first = gather(jnp.concatenate([one[1], one[2], one[3], small], axis=1))
    second = gather(jnp.concatenate([one[4], one[6]], axis=1))
    outers = gather(jnp.concatenate([one[7], two[7]], axis=1))
    third = gather(jnp.concatenate([two[1], two[2], two[3], two[4], two[6]], axis=1))
    smalls = first[:, 3 * width:].astype(f32)
    gain = smalls[:, :4].T
    whole_table = smalls[:, 4].reshape(-1, rows)[:, :bias_table.shape[0]].reshape(-1)
    heads = width // DK
    buckets = whole_table.shape[0] // heads
    weights_one = (gain[0:1], first[:, :3 * width], second[:, :width], gain[1:2], second[:, width:], outers[:, :width])
    weights_two = (gain[2:3], third[:, :3 * width], third[:, 3 * width:4 * width], gain[3:4], third[:, 4 * width:], outers[:, width:])

    reversed_ids = jnp.concatenate([jnp.full((1,), -1, jnp.int32), bucket_ids[::-1]])
    indicator = (reversed_ids[None, :] == jnp.arange(buckets, dtype=jnp.int32)[:, None]).astype(low)
    bias = toeplitz_tiles(matmul_rows(whole_table.reshape(heads, buckets).astype(low), indicator))

    length = lax.dynamic_index_in_dim(lengths, plan.s, 0, keepdims=False)
    pos = plan.positions(length, blk)
    row = jnp.arange(blk, dtype=jnp.int32)
    row_pos = jnp.concatenate([row + pos[1] * TILE, row + pos[2] * TILE])
    row_valid = (row_pos < length).astype(f32)[:, None]

    x = plan.to_sequences(inputs).astype(f32)
    grad_out = plan.to_sequences(cotangent).astype(f32) * row_valid

    middle, saved_one = layer_forward(plan, x, weights_one, pos, bias, blk)
    final, saved_two = layer_forward(plan, middle, weights_two, pos, bias, blk)
    output = plan.from_sequences((final * row_valid).astype(low))

    xy, yx = ("x", "y"), ("y", "x")
    perms = {o: plan.permutation(o, width) for o in (xy, yx)}
    depth = one[7].shape[0]
    step = TILE if depth % TILE == 0 else depth
    blocks = jnp.arange(saved_one[9].shape[1] // step, dtype=jnp.int32)
    per = depth // step
    table = {o: plan.block_of(o, blocks // per) * per + blocks % per for o in (xy, yx)}
    grad_middle, grads_two, diag_two = layer_backward(plan, grad_out, weights_two, saved_two, pos, bias, blk, perms, table, (xy, yx, yx, xy))
    grad_state, grads_one, diag_one = layer_backward(plan, grad_middle, weights_one, saved_one, pos, bias, blk, perms, table, (xy, yx, xy, yx))
    input_grad = plan.from_sequences(grad_state.astype(low))

    grad_table = lax.dot_general(diag_one + diag_two, indicator.astype(f32), (((1,), (1,)), ((), ())), precision=HIGH_PRECISION)
    vectors = jnp.concatenate([grads_one[0], grads_one[5], grads_two[0], grads_two[5], grad_table.reshape(-1)])
    vectors = lax.psum(vectors, everywhere)
    device = ((plan.z * plan.ny + plan.y) * plan.nx + plan.x) * 2 + plan.core

    def share(start, count):
        return lax.dynamic_slice_in_dim(vectors, start + device * count, count, 0)

    gain_grads = [share(i * width, rows) for i in range(4)]
    table_grad = share(4 * width, bias_table.shape[0])
    return (
        output,
        input_grad,
        gain_grads[0],
        *grads_one[1:5],
        gain_grads[1],
        *grads_one[6:],
        table_grad,
        gain_grads[2],
        *grads_two[1:5],
        gain_grads[3],
        *grads_two[6:],
    )


def solution(mesh):
    dp, cp = mesh.shape["dp"], mesh.shape["cp"]
    nx = cp // 2
    ny = nx if dp % nx == 0 else 1

    def run(inputs, *rest):
        ns = inputs.shape[0] // dp
        assert ns == 2 and nx % ns == 0
        sizes = (dp // ny, ny, ns, nx // ns)
        finer = Mesh(mesh.devices.reshape(*sizes, 2), ("z", "y", "s", "q", "core"))
        dpn, cpn = ("z", "y"), ("s", "q", "core")
        tokens = P(dpn, cpn, None)
        vector, matrix = P(dpn + cpn), P(dpn + cpn, None)
        layer = (vector, matrix, matrix, matrix, matrix, vector, matrix, matrix)
        return jax.shard_map(
            functools.partial(body, sizes),
            mesh=finer,
            in_specs=(tokens, tokens, P(dpn), P()) + layer + (vector,) + layer,
            out_specs=(tokens, tokens) + layer + (vector,) + layer,
            check_vma=False,
        )(inputs, *rest)

    return run
```

time: 4260 us -> 1060 us (0.25)
  local copies, waits for them, and re-layouts: 1760 us -> 36.9 us
  waiting for transfers between devices: 1720 us -> 482 us
  matrix products: 554 us -> 196 us
  Pallas kernels: 0 us -> 142 us
    reduce_scatter x20 -> x6, waiting for transfers between devices: 1660 us -> 42.5 us  [sum_z(): lax.psum_scatter(piece, 'z', scatter_dimension=0, tiled=False)]
    gather x2 -> x0, local copies, waits for them, and re-layouts: 1450 us -> none  [body(): local_ids = jnp.take(bucket_ids, offsets, axis=0)]
    dot_general x26 -> x1, matrix products: 281 us -> 0.2 us  [body(): lax.dot_general(diag_one + diag_two, indicator.astype(f32), (((1,), (1,))...]
    reshape x50 -> x2, local copies, waits for them, and re-layouts: 231 us -> 0.88 us  [the longest x1 0.75 us: toeplitz_tiles(): u.reshape(heads, 1, width)]
    all_gather x20 -> x4, waiting for transfers between devices: 61 us -> 276 us  [gather(): return lax.all_gather(piece, everywhere, axis=0, tiled=True)]
    ppermute x0 -> x32, waiting for transfers between devices: none -> 164 us  [exchange(): return lax.ppermute(piece, name, SWAP)]
    pallas_call x0 -> x11, Pallas kernels: none -> 142 us  [the longest x2 71 us: attn_bwd(): pl.pallas_call(functools.partial(attn_bwd_kernel, parts, chunk, blk), gri...]
    unnamed x2 -> x0, blocking collectives: 82.8 us -> none
  transfers between devices with their start and end apart: 40 -> 42, of which waited for: 16 -> 18; matrix products, arithmetic and copies ran while one was open for 52% -> 25% of each run, Pallas kernels for 0% -> 12%
where the time goes in v1:
time: 1060 us; the launch traced here: 1050 us
  waiting for transfers between devices  482 us (45%)
  matrix products  196 us (18%)
  Pallas kernels  142 us (13%)
  other arithmetic  80.8 us (8%)
  blocking collectives  68.6 us (6%)
  local copies, waits for them, and re-layouts  36.9 us (3%)
  starting transfers between devices  28.1 us (3%)
  between operations  16 us (2%)
    all_gather x4, waiting for transfers between devices, gather(): return lax.all_gather(piece, everywhere, axis=0, tiled=True)  276 us
    ppermute x32, waiting for transfers between devices, exchange(): return lax.ppermute(piece, name, SWAP)  164 us
    dot_general x15, matrix products, matmul_rows(): return jnp.dot(left, right, preferred_element_type=jnp.float32)  72.3 us
    pallas_call x2, Pallas kernels, attn_bwd(): pl.pallas_call(functools.partial(attn_bwd_kernel, parts, chunk, blk), gri...  71 us
    psum x1, blocking collectives, body(): vectors = lax.psum(vectors, everywhere)  68.6 us
    dot_general x18, matrix products, matmul_left(): lax.dot_general(left, right, (((0,), (0,)), ((), ())), preferred_element_...  63 us
    dot_general x8, matrix products, matmul_back(): lax.dot_general(left, right, (((1,), (1,)), ((), ())), preferred_element_...  60.4 us
    reduce_scatter x6, waiting for transfers between devices, sum_z(): lax.psum_scatter(piece, 'z', scatter_dimension=0, tiled=False)  42.5 us
  transfers between devices with their start and end apart: 42, of which 18 were waited for; matrix products, arithmetic and copies ran while one was open for 25% of the time, Pallas kernels for 12%

profile of v1, /device:TPU:0, one launch (start us, length us, event | category | flops | bytes accessed | tf_op | source)
XLA Modules:
  0.0 1050.5 jit_solution(305890958664635081)
XLA Ops:
  26.6 10.9 %collective-permute-done = bf16[256,1024]{1,0:T(8,128)(2,1)S(1)} collective-permute-done((bf16[256,1024]{1,0:T(8,128)(2,1)}, bf16[256,1024]{1,0:T(8,128)(2,1)S(1)}, u32[]{:S(2)}, u32[]{:S(2)}) %collective-permute-start) | collective-permute-done | bytes 524320 | tf_op jit(solution)/shard_map/ppermute | solution.py:305
  38.4 15.5 %collective-permute-done.4 = bf16[256,1024]{1,0:T(8,128)(2,1)S(1)} collective-permute-done((bf16[256,1024]{1,0:T(8,128)(2,1)}, bf16[256,1024]{1,0:T(8,128)(2,1)S(1)}, u32[]{:S(2)}, u32[]{:S(2)}) %collective-permute-start.4) | collective-permute-done | bytes 524320 | tf_op jit(solution)/shard_map/ppermute | solution.py:305
  55.2 34.5 %all-gather.5.cloned.1.call-done = bf16[1024,3200]{1,0:T(8,128)(2,1)} async-done(((bf16[32,3200]{1,0:T(8,128)(2,1)}), bf16[1024,3200]{1,0:T(8,128)(2,1)}) %all-gather.5.cloned.1.call-update) | async-done | bytes 6553616 | tf_op jit(solution)/shard_map/all_gather | solution.py:464
  102.7 11.3 %toeplitz.1.refs_4_ = bf16[16,15,128,128]{3,2,1,0:T(8,128)(2,1)} custom-call(f32[16,1,2048]{2,1,0:T(1,128)} %reshape.171.u_ref), custom_call_target="tpu_custom_call" | custom-call | flops 15728640 | bytes 7864320 | tf_op jit(solution)/shard_map/toeplitz/pallas_call | solution.py:28
  120.7 19.5 %attn_fwd.2 = (bf16[512,1024]{1,0:T(8,128)(2,1)S(1)}, f32[8,2,512]{2,1,0:T(2,128)S(1)}) custom-call(s32[7]{0:T(128)S(1)} %stack.52.pos_ref, bf16[512,1024]{1,0:T(8,128)(2,1)S(1)} %get-tuple-element.78.q_ref, bf16[512,1024]{1,0:T(8,128)(2,1)S(1)} %get-tuple-element.77.refs_0_, bf16[512,1024]{1,0:T(8,128)(2,1)S(1)} %get-tuple-element.82.refs_1_, ...), custom_call_target="tpu_custom_call" | custom-call | flops 8589934592 | bytes 14155776 | tf_op jit(solution)/shard_map/attn_fwd/pallas_call | solution.py:114
  143.3 34.9 %all-gather.7.cloned.1.call-done = bf16[1024,5120]{1,0:T(8,128)(2,1)} async-done(((bf16[32,5120]{1,0:T(8,128)(2,1)}), bf16[1024,5120]{1,0:T(8,128)(2,1)}) %all-gather.7.cloned.1.call-update) | async-done | bytes 10485776 | tf_op jit(solution)/shard_map/all_gather | solution.py:464
  195.1 100.2 %all-gather.9.cloned.1.call-done = bf16[4096,2048]{1,0:T(8,128)(2,1)} async-done(((bf16[128,2048]{1,0:T(8,128)(2,1)}), bf16[4096,2048]{1,0:T(8,128)(2,1)}) %all-gather.9.cloned.1.call-update) | async-done | bytes 16777232 | tf_op jit(solution)/shard_map/all_gather | solution.py:464
  295.3 9.8 multiply_reduce_fusion.7
  305.7 105.9 %all-gather.11.cloned.1.call-done = bf16[1024,8192]{1,0:T(8,128)(2,1)} async-done(((bf16[32,8192]{1,0:T(8,128)(2,1)}), bf16[1024,8192]{1,0:T(8,128)(2,1)}) %all-gather.11.cloned.1.call-update) | async-done | bytes 16777232 | tf_op jit(solution)/shard_map/all_gather | solution.py:464
  424.2 19.5 %attn_fwd.3 = (bf16[512,1024]{1,0:T(8,128)(2,1)S(1)}, f32[8,2,512]{2,1,0:T(2,128)S(1)}) custom-call(s32[7]{0:T(128)S(1)} %stack.52.pos_ref, bf16[512,1024]{1,0:T(8,128)(2,1)S(1)} %get-tuple-element.75.q_ref, bf16[512,1024]{1,0:T(8,128)(2,1)S(1)} %get-tuple-element.74.refs_0_, bf16[512,1024]{1,0:T(8,128)(2,1)S(1)} %get-tuple-element.80.refs_1_, ...), custom_call_target="tpu_custom_call" | custom-call | flops 8589934592 | bytes 14155776 | tf_op jit(solution)/shard_map/attn_fwd/pallas_call | solution.py:114
  451.5 10.9 %multiply_convert_fusion.2 = (bf16[512,4096]{1,0:T(8,128)(2,1)S(1)}, f32[512,4096]{1,0:T(8,128)}) fusion(bf16[1024,8192]{1,0:T(8,128)(2,1)} %all-gather.11.cloned.1.call-done, f32[512,1024]{1,0:T(8,128)S(1)} %get-tuple-element.118, f32[1024]{0:T(1024)S(1)} %copy-done.87, f32[512]{0:T(512)S(1)} %get-tuple-element.110), kind=kOutput, calls=%fused_computation.26 | convolution fusion | flops 4315414528 | bytes 23074816 | tf_op jit(solution)/shard_map/dot_general | solution.py:233
  472.5 11.8 %multiply_convert_fusion.1 = bf16[512,4096]{1,0:T(8,128)(2,1)S(1)} fusion(bf16[512,1024]{1,0:T(8,128)(2,1)S(1)} %copy-done.2, bf16[4096,2048]{1,0:T(8,128)(2,1)} %all-gather.9.cloned.1.call-done, f32[512,4096]{1,0:T(8,128)} %get-tuple-element.120), kind=kOutput, calls=%fused_computation.25 | convolution fusion | flops 4334813184 | bytes 22020096 | tf_op jit(solution)/shard_map/dot_general | solution.py:241
  501.4 35.6 %attn_bwd.2 = (bf16[512,1024]{1,0:T(8,128)(2,1)S(1)}, bf16[512,1024]{1,0:T(8,128)(2,1)S(1)}, bf16[512,1024]{1,0:T(8,128)(2,1)S(1)}, bf16[512,1024]{1,0:T(8,128)(...) custom-call(s32[7]{0:T(128)S(1)} %stack.52.pos_ref, bf16[512,1024]{1,0:T(8,128)(2,1)} %copy-done.18, ...), custom_call_target="tpu_custom_call" | custom-call | flops 21474836480 | bytes 20447232 | tf_op jit(solution)/shard_map/attn_bwd/pallas_call | solution.py:212
  579.2 10.4 multiply_convert_fusion
  606.5 35.4 %attn_bwd.3 = (bf16[512,1024]{1,0:T(8,128)(2,1)S(1)}, bf16[512,1024]{1,0:T(8,128)(2,1)S(1)}, bf16[512,1024]{1,0:T(8,128)(2,1)S(1)}, bf16[512,1024]{1,0:T(8,128)(...) custom-call(s32[7]{0:T(128)S(1)} %stack.52.pos_ref, bf16[512,1024]{1,0:T(8,128)(2,1)} %copy-done.10, ...), custom_call_target="tpu_custom_call" | custom-call | flops 21474836480 | bytes 20447232 | tf_op jit(solution)/shard_map/attn_bwd/pallas_call | solution.py:212
  714.1 68.6 %psum.7 = f32[4608]{0:T(1024)S(1)} all-reduce(f32[4608]{0:T(1024)S(1)} %constant_dynamic-update-slice_fusion.6), channel_id=1, replica_groups=mesh['z'=4,'y'=2,'s'=2,'q'=1,'core'=2] {'z','y','s','q','core'}, use_global_device_ids=true, to_apply=%region_12.13 | all-reduce | flops 4608 | bytes 36864 | tf_op jit(solution)/shard_map/psum | solution.py:508
  802.4 17.6 %collective-permute-done.31 = bf16[512,1024]{1,0:T(8,128)(2,1)S(1)} collective-permute-done((bf16[512,1024]{1,0:T(8,128)(2,1)S(1)}, bf16[512,1024]{1,0:T(8,128)(2,1)S(1)}, u32[]{:S(2)}, u32[]{:S(2)}) %collective-permute-start.31) | collective-permute-done | bytes 1048608 | tf_op jit(solution)/shard_map/ppermute | solution.py:305
  828.3 25.1 %collective-permute-done.21 = bf16[256,3072]{1,0:T(8,128)(2,1)} collective-permute-done((bf16[256,3072]{1,0:T(8,128)(2,1)}, bf16[256,3072]{1,0:T(8,128)(2,1)}, u32[]{:S(2)}, u32[]{:S(2)}) %collective-permute-start.21) | collective-permute-done | bytes 1572896 | tf_op jit(solution)/shard_map/ppermute | solution.py:305
  883.6 36.3 %collective-permute-done.18 = bf16[1024,1024]{1,0:T(8,128)(2,1)} collective-permute-done((bf16[1024,1024]{1,0:T(8,128)(2,1)}, bf16[1024,1024]{1,0:T(8,128)(2,1)}, u32[]{:S(2)}, u32[]{:S(2)}) %collective-permute-start.18) | collective-permute-done | bytes 2097184 | tf_op jit(solution)/shard_map/ppermute | solution.py:305
  931.4 14.2 %collective-permute-done.19 = bf16[512,1024]{1,0:T(8,128)(2,1)S(1)} collective-permute-done((bf16[512,1024]{1,0:T(8,128)(2,1)S(1)}, bf16[512,1024]{1,0:T(8,128)(2,1)S(1)}, u32[]{:S(2)}, u32[]{:S(2)}) %collective-permute-start.19) | collective-permute-done | bytes 1048608 | tf_op jit(solution)/shard_map/ppermute | solution.py:305
  951.7 12.8 %collective-permute-done.9 = bf16[256,3072]{1,0:T(8,128)(2,1)} collective-permute-done((bf16[256,3072]{1,0:T(8,128)(2,1)}, bf16[256,3072]{1,0:T(8,128)(2,1)}, u32[]{:S(2)}, u32[]{:S(2)}) %collective-permute-start.9) | collective-permute-done | bytes 1572896 | tf_op jit(solution)/shard_map/ppermute | solution.py:305
  967.3 16.8 %collective-permute-done.16 = bf16[128,4096]{1,0:T(8,128)(2,1)} collective-permute-done((bf16[128,4096]{1,0:T(8,128)(2,1)}, bf16[128,4096]{1,0:T(8,128)(2,1)}, u32[]{:S(2)}, u32[]{:S(2)}) %collective-permute-start.16) | collective-permute-done | bytes 1048608 | tf_op jit(solution)/shard_map/ppermute | solution.py:305
  997.3 16.2 %reduce-scatter.9.cloned.1.call-done = bf16[1,32,4096]{2,1,0:T(8,128)(2,1)} async-done(((bf16[4,32,4096]{2,1,0:T(8,128)(2,1)}), bf16[1,32,4096]{2,1,0:T(8,128)(2,1)}) %reduce-scatter.9.cloned.1.call-update) | async-done | bytes 262160 | tf_op jit(solution)/shard_map/reduce_scatter | solution.py:334
  1015.3 26.3 %reduce-scatter.7.cloned.1.call-done = bf16[1,32,4096]{2,1,0:T(8,128)(2,1)} async-done(((bf16[4,32,4096]{2,1,0:T(8,128)(2,1)}), bf16[1,32,4096]{2,1,0:T(8,128)(2,1)}) %reduce-scatter.7.cloned.1.call-update) | async-done | bytes 262160 | tf_op jit(solution)/shard_map/reduce_scatter | solution.py:334
  (444 shorter events, 334.5 us)
Async XLA Ops:
  7.2 82.5 %all-gather.5.cloned.1.call-start = ((), (), s32[]{:S(2)}) async-start(), calls=%async_computation.6 | async-start | bytes 6758400 | tf_op jit(solution)/shard_map/all_gather | solution.py:464
  10.5 167.7 %all-gather.7.cloned.1.call-start = ((), (), s32[]{:S(2)}) async-start(), calls=%async_computation.7 | async-start | bytes 10813440 | tf_op jit(solution)/shard_map/all_gather | solution.py:464
  12.3 283.0 %all-gather.9.cloned.1.call-start = ((), (), s32[]{:S(2)}) async-start(), calls=%async_computation.8 | async-start | bytes 17301504 | tf_op jit(solution)/shard_map/all_gather | solution.py:464
  14.3 397.4 %all-gather.11.cloned.1.call-start = ((), (), s32[]{:S(2)}) async-start(), calls=%async_computation.9 | async-start | bytes 17301504 | tf_op jit(solution)/shard_map/all_gather | solution.py:464
  19.5 967.8 %reduce-scatter.17.cloned.1.call-start = ((), (), s32[]{:S(2)}) async-start(), calls=%async_computation.15 | async-start | bytes 1310720 | tf_op jit(solution)/shard_map/reduce_scatter | solution.py:334
  471.2 90.9 %collective-permute-start.3 = (bf16[256,1024]{1,0:T(8,128)(2,1)}, bf16[256,1024]{1,0:T(8,128)(2,1)}, u32[]{:S(2)}, u32[]{:S(2)}) collective-permute-start(bf16[256,1024]{1,0:T(8,128)(2,1)} %slice.458), channel_id=1, source_target_pairs={{0,2},{2,0},{1,3},{3,1},{4,6},{6,4},{5,7},{7,5},{8,10},{10,8},{9,1... | collective-permute-start | bytes 1572872 | tf_op jit(solution)/shard_map/ppermute | solution.py:305
  543.9 143.1 %collective-permute-start.26 = (bf16[512,4096]{1,0:T(8,128)(2,1)}, bf16[512,4096]{1,0:T(8,128)(2,1)}, u32[]{:S(2)}, u32[]{:S(2)}) collective-permute-start(bf16[512,4096]{1,0:T(8,128)(2,1)} %convolution_convert_fusion), channel_id=1, source_target_pairs={{0,1},{1,0},{2,3},{3,2},{4,5},{5,4},{6,7},{7,6},{8,9},{9,8},{10,11... | collective-permute-start | bytes 12582920 | tf_op jit(solution)/shard_map/ppermute | solution.py:305
  552.2 140.0 %collective-permute-start.29 = (bf16[2048,1024]{1,0:T(8,128)(2,1)}, bf16[2048,1024]{1,0:T(8,128)(2,1)}, u32[]{:S(2)}, u32[]{:S(2)}) collective-permute-start(bf16[2048,1024]{1,0:T(8,128)(2,1)} %outer_grad.10), channel_id=1, source_target_pairs={{0,1},{1,0},{2,3},{3,2},{4,5},{5,4},{6,7},{7,6},{8,9},{9,8},{10,11... | collective-permute-start | bytes 12582920 | tf_op jit(solution)/shard_map/ppermute | solution.py:305
  602.7 54.5 %collective-permute-start.11 = (bf16[512,1024]{1,0:T(8,128)(2,1)}, bf16[512,1024]{1,0:T(8,128)(2,1)}, u32[]{:S(2)}, u32[]{:S(2)}) collective-permute-start(bf16[512,1024]{1,0:T(8,128)(2,1)} %convolution_convert_fusion.19), channel_id=1, source_target_pairs={{0,1},{1,0},{2,3},{3,2},{4,5},{5,4},{6,7},{7,6},{8,9},{9,8},{10,11... | collective-permute-start | bytes 3145736 | tf_op jit(solution)/shard_map/ppermute | solution.py:305
  645.6 59.0 %collective-permute-start.6 = (bf16[512,2048]{1,0:T(8,128)(2,1)}, bf16[512,2048]{1,0:T(8,128)(2,1)}, u32[]{:S(2)}, u32[]{:S(2)}) collective-permute-start(bf16[512,2048]{1,0:T(8,128)(2,1)} %pad_maximum_fusion.3), channel_id=1, source_target_pairs={{0,1},{1,0},{2,3},{3,2},{4,5},{5,4},{6,7},{7,6},{8,9},{9,8},{10,11... | collective-permute-start | bytes 6291464 | tf_op jit(solution)/shard_map/ppermute | solution.py:305
  661.4 206.6 %collective-permute-start.14 = (bf16[512,4096]{1,0:T(8,128)(2,1)}, bf16[512,4096]{1,0:T(8,128)(2,1)}, u32[]{:S(2)}, u32[]{:S(2)}) collective-permute-start(bf16[512,4096]{1,0:T(8,128)(2,1)} %convolution_convert_fusion.1), channel_id=1, source_target_pairs={{0,1},{1,0},{2,3},{3,2},{4,5},{5,4},{6,7},{7,6},{8,9},{9,8},{10,11... | collective-permute-start | bytes 12582920 | tf_op jit(solution)/shard_map/ppermute | solution.py:305
  685.3 108.5 %collective-permute-start.20 = (bf16[512,3072]{1,0:T(8,128)(2,1)}, bf16[512,3072]{1,0:T(8,128)(2,1)}, u32[]{:S(2)}, u32[]{:S(2)}) collective-permute-start(bf16[512,3072]{1,0:T(8,128)(2,1)} %convolution_convert_fusion.6), channel_id=1, source_target_pairs={{0,1},{1,0},{2,3},{3,2},{4,5},{5,4},{6,7},{7,6},{8,9},{9,8},{10,11... | collective-permute-start | bytes 9437192 | tf_op jit(solution)/shard_map/ppermute | solution.py:305
  691.4 108.4 %collective-permute-start.27 = (bf16[256,4096]{1,0:T(8,128)(2,1)}, bf16[256,4096]{1,0:T(8,128)(2,1)}, u32[]{:S(2)}, u32[]{:S(2)}) collective-permute-start(bf16[256,4096]{1,0:T(8,128)(2,1)} %add_convert_fusion.2), channel_id=1, source_target_pairs={{0,2},{2,0},{1,3},{3,1},{4,6},{6,4},{5,7},{7,5},{8,10},{10,8},{9,1... | collective-permute-start | bytes 6291464 | tf_op jit(solution)/shard_map/ppermute | solution.py:305
  698.8 93.0 %collective-permute-start.30 = (bf16[1024,1024]{1,0:T(8,128)(2,1)}, bf16[1024,1024]{1,0:T(8,128)(2,1)}, u32[]{:S(2)}, u32[]{:S(2)}) collective-permute-start(bf16[1024,1024]{1,0:T(8,128)(2,1)} %get-tuple-element.70), channel_id=1, source_target_pairs={{0,4},{4,0},{1,5},{5,1},{2,6},{6,2},{3,7},{7,3},{8,12},{12,8},{9,1... | collective-permute-start | bytes 6291464 | tf_op jit(solution)/shard_map/ppermute | solution.py:305
  713.4 75.9 %collective-permute-start.7 = (bf16[256,1024]{1,0:T(8,128)(2,1)}, bf16[256,1024]{1,0:T(8,128)(2,1)}, u32[]{:S(2)}, u32[]{:S(2)}) collective-permute-start(bf16[256,1024]{1,0:T(8,128)(2,1)} %slice.460), channel_id=1, source_target_pairs={{0,2},{2,0},{1,3},{3,1},{4,6},{6,4},{5,7},{7,5},{8,10},{10,8},{9,1... | collective-permute-start | bytes 1572872 | tf_op jit(solution)/shard_map/ppermute | solution.py:305
  789.3 71.1 %collective-permute-start.17 = (bf16[2048,1024]{1,0:T(8,128)(2,1)}, bf16[2048,1024]{1,0:T(8,128)(2,1)}, u32[]{:S(2)}, u32[]{:S(2)}) collective-permute-start(bf16[2048,1024]{1,0:T(8,128)(2,1)} %outer_grad.7), channel_id=1, source_target_pairs={{0,1},{1,0},{2,3},{3,2},{4,5},{5,4},{6,7},{7,6},{8,9},{9,8},{10,11... | collective-permute-start | bytes 12582920 | tf_op jit(solution)/shard_map/ppermute | solution.py:305
  791.8 131.3 %collective-permute-start.8 = (bf16[512,3072]{1,0:T(8,128)(2,1)}, bf16[512,3072]{1,0:T(8,128)(2,1)}, u32[]{:S(2)}, u32[]{:S(2)}) collective-permute-start(bf16[512,3072]{1,0:T(8,128)(2,1)} %convolution_convert_fusion.7), channel_id=1, source_target_pairs={{0,1},{1,0},{2,3},{3,2},{4,5},{5,4},{6,7},{7,6},{8,9},{9,8},{10,11... | collective-permute-start | bytes 9437192 | tf_op jit(solution)/shard_map/ppermute | solution.py:305
  825.0 164.1 %reduce-scatter.15.cloned.1.call-start = ((), (), s32[]{:S(2)}) async-start(), calls=%async_computation.14 | async-start | bytes 1310720 | tf_op jit(solution)/shard_map/reduce_scatter | solution.py:334
  860.4 133.3 %reduce-scatter.13.cloned.1.call-start = ((), (), s32[]{:S(2)}) async-start(), calls=%async_computation.13 | async-start | bytes 1310720 | tf_op jit(solution)/shard_map/reduce_scatter | solution.py:334
  872.5 55.6 %collective-permute-start.15 = (bf16[256,4096]{1,0:T(8,128)(2,1)}, bf16[256,4096]{1,0:T(8,128)(2,1)}, u32[]{:S(2)}, u32[]{:S(2)}) collective-permute-start(bf16[256,4096]{1,0:T(8,128)(2,1)} %add_convert_fusion.6), channel_id=1, source_target_pairs={{0,2},{2,0},{1,3},{3,1},{4,6},{6,4},{5,7},{7,5},{8,10},{10,8},{9,1... | collective-permute-start | bytes 6291464 | tf_op jit(solution)/shard_map/ppermute | solution.py:305
  878.9 116.6 %reduce-scatter.11.cloned.1.call-start = ((), (), s32[]{:S(2)}) async-start(), calls=%async_computation.12 | async-start | bytes 1310720 | tf_op jit(solution)/shard_map/reduce_scatter | solution.py:334
  930.5 53.6 %collective-permute-start.16 = (bf16[128,4096]{1,0:T(8,128)(2,1)}, bf16[128,4096]{1,0:T(8,128)(2,1)}, u32[]{:S(2)}, u32[]{:S(2)}) collective-permute-start(bf16[128,4096]{1,0:T(8,128)(2,1)} %add_convert_fusion.17), channel_id=1, source_target_pairs={{0,4},{4,0},{1,5},{5,1},{2,6},{6,2},{3,7},{7,3},{8,12},{12,8},{9,1... | collective-permute-start | bytes 3145736 | tf_op jit(solution)/shard_map/ppermute | solution.py:305
  948.4 65.1 %reduce-scatter.9.cloned.1.call-start = ((), (), s32[]{:S(2)}) async-start(), calls=%async_computation.11 | async-start | bytes 1310720 | tf_op jit(solution)/shard_map/reduce_scatter | solution.py:334
  987.2 54.4 %reduce-scatter.7.cloned.1.call-start = ((), (), s32[]{:S(2)}) async-start(), calls=%async_computation.10 | async-start | bytes 1310720 | tf_op jit(solution)/shard_map/reduce_scatter | solution.py:334
  (128 other events, 2827.6 us)
Sparse Core Ops, SparseCore 0:
  10.9 78.8 all-gather.4
  93.1 85.0 all-gather.6
  181.7 113.6 all-gather.8
  298.6 113.0 all-gather.10
  825.1 26.0 reduce-scatter.16
  860.5 26.0 reduce-scatter.14
  888.9 25.7 reduce-scatter.12
  948.5 26.3 reduce-scatter.10
  987.3 26.0 reduce-scatter.8
  1015.7 25.8 reduce-scatter.6

commit v2 on v1

--- a/solution.py
+++ b/solution.py
@@ -199,23 +199,28 @@
         d_ref[0, h:h + 1, :] = jnp.concatenate(pieces, axis=1)
     dq_ref[...] = jnp.concatenate(outs, axis=0).T.astype(dq_ref.dtype)
 
-def attn_bwd(pos, q, do, o, lse, ks, vs, bias, blk):
+def attn_bwd(pos, q, do, o, lse, ks, vs, bias, blk, share, shares):
     q_rows, width = q.shape
     parts, rows = len(ks), ks[0].shape[0]
     keys = parts * rows
-    heads = width // DK
+    heads = width // DK // shares
+    width = width // shares
     span = bias.shape[1]
     chunk = min(256, rows)
-    spec_q = pl.BlockSpec((q_rows, 2 * DK), lambda p, s: (0, p))
-    spec_k = pl.BlockSpec((rows, 2 * DK), lambda p, s: (0, p))
-    spec_l = pl.BlockSpec((1, 2, q_rows), lambda p, s: (p, 0, 0))
+    first = share * (heads // 2)
+    spec_q = pl.BlockSpec((q_rows, 2 * DK), lambda p, s: (0, first + p))
+    spec_k = pl.BlockSpec((rows, 2 * DK), lambda p, s: (0, first + p))
+    spec_l = pl.BlockSpec((1, 2, q_rows), lambda p, s: (first + p, 0, 0))
+    spec_b = pl.BlockSpec((2, span, TILE, TILE), lambda p, s: (first + p, 0, 0, 0))
+    out_q = pl.BlockSpec((q_rows, 2 * DK), lambda p, s: (0, p))
+    out_k = pl.BlockSpec((rows, 2 * DK), lambda p, s: (0, p))
     out = pl.pallas_call(
         functools.partial(attn_bwd_kernel, parts, chunk, blk),
         grid_spec=pltpu.PrefetchScalarGridSpec(
             num_scalar_prefetch=1,
             grid=(heads // 2,),
-            in_specs=[spec_q, spec_q, spec_q, spec_l] + [spec_k] * (2 * parts) + [pl.BlockSpec((2, span, TILE, TILE), lambda p, s: (p, 0, 0, 0))],
-            out_specs=[spec_q] + [spec_k] * (2 * parts) + [pl.BlockSpec((1, 2, (span + 1) * TILE), lambda p, s: (p, 0, 0))],
+            in_specs=[spec_q, spec_q, spec_q, spec_l] + [spec_k] * (2 * parts) + [spec_b],
+            out_specs=[out_q] + [out_k] * (2 * parts) + [pl.BlockSpec((1, 2, (span + 1) * TILE), lambda p, s: (p, 0, 0))],
             scratch_shapes=[pltpu.VMEM((span, TILE, TILE), jnp.float32)],
         ),
         out_shape=[jax.ShapeDtypeStruct((q_rows, width), jnp.bfloat16)]
@@ -304,34 +309,21 @@
     def exchange(self, piece, name):
         return lax.ppermute(piece, name, SWAP)
 
-    def scatter_sum(self, product, order, rows):
-        half = rows // 2
-        other = self.exchange(product(half, rows), "core")
-        name_a, size_a, _ = self.axes[order[0]]
-        name_b, size_b, _ = self.axes[order[1]]
-        low = jnp.bfloat16
-        f32 = jnp.float32
-        if size_a == 2 and size_b == 2:
-            quarter = half // 2
-            far = (product(quarter, half).astype(f32) + other[quarter:].astype(f32)).astype(low)
-            far = self.exchange(far, name_a)
-            near = (product(0, quarter).astype(f32) + other[:quarter].astype(f32)).astype(low)
-            eighth = quarter // 2
-            side = (near[eighth:].astype(f32) + far[eighth:].astype(f32)).astype(low)
-            side = self.exchange(side, name_b)
-            total = near[:eighth].astype(f32) + far[:eighth].astype(f32) + side.astype(f32)
-            return total.astype(low).reshape(self.nz, eighth // self.nz, -1)
-        whole = (product(0, half).astype(f32) + other.astype(f32)).astype(low)
-        whole = whole.reshape(size_a, half // size_a, -1)
-        whole = lax.psum_scatter(whole, name_a, scatter_dimension=0, tiled=False)
-        whole = whole.reshape(size_b, half // (size_a * size_b), -1)
-        whole = lax.psum_scatter(whole, name_b, scatter_dimension=0, tiled=False)
-        return whole.reshape(self.nz, half // (size_a * size_b * self.nz), -1)
-
     def sum_z(self, piece):
         if self.nz == 1:
-            return piece[0].astype(jnp.float32)
-        return lax.psum_scatter(piece, "z", scatter_dimension=0, tiled=False).astype(jnp.float32)
+            return piece[0]
+        return lax.psum_scatter(piece, "z", scatter_dimension=0, tiled=False)
+
+    def sum_vector(self, vector):
+        for name, size in (("core", 2), ("z", self.nz), ("y", self.ny), ("q", self.m), ("s", self.ns)):
+            if size & (size - 1):
+                vector = lax.psum(vector, name)
+                continue
+            step = 1
+            while step < size:
+                vector = vector + lax.ppermute(vector, name, [(i, i ^ step) for i in range(size)])
+                step *= 2
+        return vector
 
     def to_sequences(self, local):
         own = lax.dynamic_index_in_dim(local, self.s, 0, keepdims=False)
@@ -340,7 +332,9 @@
 
     def from_sequences(self, rows):
         blk = rows.shape[0] // 2
-        own, other = rows[:blk], self.exchange(rows[blk:], "s")
+        return self.in_order(rows[:blk], self.exchange(rows[blk:], "s"))
+
+    def in_order(self, own, other):
         first = self.s == 0
         return jnp.stack([jnp.where(first, own, other), jnp.where(first, other, own)], axis=0)
 
@@ -362,6 +356,188 @@
         else:
             keys = [(((self.s ^ j) * self.m + q) * 2 + c) * unit for q in range(self.m) for c in range(2) for j in range(2)]
         return jnp.stack([length] + mine + keys).astype(jnp.int32)
+
+
+def assemble_kernel(steps, depth, table_ref, *refs):
+    i = pl.program_id(0)
+    out = refs[-1]
+    core, x = table_ref[0], table_ref[1]
+    quads = [refs[j:j + 4] for j in range(0, len(refs) - 1, 4)]
+    for quad, (start, count) in zip(quads, steps):
+
+        @pl.when(jnp.logical_and(i >= start, i < start + count))
+        def _(quad=quad):
+            for j, r in enumerate(quad):
+                place = (x ^ (j // 2)) * 2 + (core ^ (j % 2))
+                out[pl.ds(pl.multiple_of(place * depth, depth), depth), :] = r[...]
+
+
+def assemble(table, quads, depth):
+    width = quads[0][0].shape[1]
+    steps, at = [], 0
+    for q in quads:
+        steps.append((at, q[0].shape[0] // depth))
+        at += q[0].shape[0] // depth
+
+    def source_map(start, count):
+        return lambda i, t: (jnp.clip(i - start, 0, count - 1), 0)
+
+    return pl.pallas_call(
+        functools.partial(assemble_kernel, steps, depth),
+        grid_spec=pltpu.PrefetchScalarGridSpec(
+            num_scalar_prefetch=1,
+            grid=(at,),
+            in_specs=[pl.BlockSpec((depth, width), source_map(*s)) for s in steps for _ in range(4)],
+            out_specs=pl.BlockSpec((4 * depth, width), lambda i, t: (t[2 + i], 0)),
+        ),
+        out_shape=jax.ShapeDtypeStruct((at * 4 * depth, width), quads[0][0].dtype),
+        compiler_params=pltpu.CompilerParams(vmem_limit_bytes=48 << 20),
+        cost_estimate=pl.CostEstimate(flops=0, bytes_accessed=16 * at * depth * width, transcendentals=0),
+        name="assemble",
+    )(table, *[r for q in quads for r in q])
+
+
+class Held:
+    def __init__(self, value):
+        self.value = value
+
+
+def tie(main, *held):
+    got = lax.optimization_barrier((main,) + tuple(h.value for h in held))
+    for h, v in zip(held, got[1:]):
+        h.value = v
+    return got[0]
+
+
+class Fetch:
+    def __init__(self, plan, shard):
+        self.plan, self.shard = plan, Held(shard)
+        self.pairs = plan.nx == 2 and plan.ny == 2 and plan.nz % 2 == 0
+        self.depth = shard.shape[0]
+
+    def start(self):
+        axes = "z" if self.pairs else self.plan.everywhere
+        self.near = Held(lax.all_gather(self.shard.value, axes, axis=0, tiled=True))
+
+    def send(self, piece, name):
+        return Held(self.plan.exchange(piece.value, name))
+
+    def a(self, main, following=None):
+        held = [self.near] + ([following.shard] if following else [])
+        main = tie(main, *held)
+        if following:
+            following.start()
+        if self.pairs:
+            self.by_x, self.by_y, self.near_twin = [self.send(self.near, n) for n in ("s", "y", "core")]
+        return main
+
+    def b(self, main):
+        if self.pairs:
+            main = tie(main, self.by_x, self.by_y, self.near_twin)
+            half = self.by_x.value.shape[0] // 2
+            self.low = Held(self.plan.exchange(self.by_y.value[:half], "s"))
+            self.high = Held(self.plan.exchange(self.by_x.value[half:], "y"))
+            self.x_twin, self.y_twin = self.send(self.by_x, "core"), self.send(self.by_y, "core")
+        return main
+
+    def c(self, main):
+        return tie(main, self.x_twin, self.y_twin) if self.pairs else main
+
+    def d(self, main):
+        if self.pairs:
+            main = tie(main, self.low, self.high)
+            self.low_twin, self.high_twin = self.send(self.low, "core"), self.send(self.high, "core")
+        return main
+
+    def e(self, main):
+        if not self.pairs:
+            return main, self.near.value
+        main = tie(main, self.low_twin, self.high_twin)
+        plan = self.plan
+        half = self.low.value.shape[0]
+        by_y, y_twin = self.by_y.value, self.y_twin.value
+        quads = [
+            (self.near.value, self.near_twin.value, self.by_x.value, self.x_twin.value),
+            (by_y[:half], y_twin[:half], self.low.value, self.low_twin.value),
+            (by_y[half:], y_twin[half:], self.high.value, self.high_twin.value),
+        ]
+        z = jnp.arange(plan.nz, dtype=jnp.int32)
+        order = jnp.concatenate([z * 2 + plan.y, z * 2 + (1 - plan.y)])
+        table = jnp.concatenate([jnp.stack([plan.core, plan.x]).astype(jnp.int32), order.astype(jnp.int32)])
+        whole = Held(assemble(table, quads, self.depth))
+        main = tie(main, whole)
+        return main, whole.value
+
+
+def add_low(*terms):
+    total = terms[0].astype(jnp.float32)
+    for t in terms[1:]:
+        total = total + t.astype(jnp.float32)
+    return total.astype(jnp.bfloat16)
+
+
+class Chain:
+    def __init__(self, plan, product, order, rows):
+        self.plan, self.product, self.rows = plan, product, rows
+        self.name_a, self.size_a, _ = plan.axes[order[0]]
+        self.name_b, self.size_b, _ = plan.axes[order[1]]
+        self.pairs = self.size_a == 2 and self.size_b == 2
+        self.part = None
+
+    def one(self):
+        self.part = Held(self.product(self.rows // 2, self.rows))
+        return self.part
+
+    def send_one(self):
+        self.other = Held(self.plan.exchange(self.part.value, "core"))
+
+    def two(self):
+        half = self.rows // 2
+        if self.pairs:
+            quarter = half // 2
+            self.part = Held(add_low(self.product(quarter, half), self.other.value[quarter:]))
+        else:
+            self.part = Held(add_low(self.product(0, half), self.other.value))
+        return self.part
+
+    def send_two(self):
+        if self.pairs:
+            self.far = Held(self.plan.exchange(self.part.value, self.name_a))
+        else:
+            whole = self.part.value.reshape(self.size_a, self.rows // (2 * self.size_a), -1)
+            self.far = Held(lax.psum_scatter(whole, self.name_a, scatter_dimension=0, tiled=False))
+
+    def near(self):
+        if self.pairs:
+            quarter = self.rows // 4
+            self.close_by = Held(add_low(self.product(0, quarter), self.other.value[:quarter]))
+            return self.close_by
+        return self.far
+
+    def three(self):
+        if self.pairs:
+            eighth = self.rows // 8
+            self.part = Held(add_low(self.close_by.value[eighth:], self.far.value[eighth:]))
+        else:
+            self.part = self.far
+        return self.part
+
+    def send_three(self):
+        if self.pairs:
+            self.side = Held(self.plan.exchange(self.part.value, self.name_b))
+        else:
+            whole = self.part.value.reshape(self.size_b, self.part.value.shape[0] // self.size_b, -1)
+            self.side = Held(lax.psum_scatter(whole, self.name_b, scatter_dimension=0, tiled=False))
+
+    def close(self):
+        nz = self.plan.nz
+        if self.pairs:
+            eighth = self.rows // 8
+            total = add_low(self.close_by.value[:eighth], self.far.value[:eighth], self.side.value)
+        else:
+            total = self.side.value
+        self.piece = Held(total.reshape(nz, total.shape[0] // nz, -1))
+        return self.piece
 
 
 def outer_grad_kernel(count, table_ref, *refs):
@@ -389,64 +565,129 @@
     )(table, *([hidden] * count), grad_low)
 
 
-def layer_forward(plan, x, weights, pos, bias, blk):
-    attn_gain, w_qkv, w_output, mlp_gain, w_inner, w_outer = weights
-    width = x.shape[1]
-    normed = (x * inv_rms(x) * attn_gain).astype(jnp.bfloat16)
-    qkv = matmul_rows(normed, w_qkv).astype(jnp.bfloat16)
-    queries = qkv[:, :width]
-    kv = plan.gather_keys(qkv[:, width:])
-    keys = [p[:, :width] for p in kv]
-    values = [p[:, width:] for p in kv]
-    context, log_total = attn_fwd(pos, queries, keys, values, bias, blk)
-    attended = x + matmul_rows(context, w_output)
-    normed_mlp = (attended * inv_rms(attended) * mlp_gain).astype(jnp.bfloat16)
-    hidden, slope = gelu_pair(matmul_rows(normed_mlp, w_inner))
-    result = attended + matmul_rows(hidden, w_outer)
-    return result, (x, normed, queries, keys, values, context, log_total, attended, normed_mlp, hidden, slope)
-
-
-def layer_backward(plan, grad_out, weights, saved, pos, bias, blk, perms, table, orders):
-    attn_gain, w_qkv, w_output, mlp_gain, w_inner, w_outer = weights
-    x, normed, queries, keys, values, context, log_total, attended, normed_mlp, hidden, slope = saved
-    low = jnp.bfloat16
-    width = x.shape[1]
-    grad_low = grad_out.astype(low)
-    grad_pre = (matmul_back(grad_low, w_outer) * slope.astype(jnp.float32)).astype(low)
-    wide = hidden.shape[1]
-    if wide // (table[orders[1]].shape[0]) == TILE:
-        outer_rows = lambda a, b: outer_grad(hidden, grad_low, table[orders[1]], a // TILE, b // TILE)
-    else:
-        outer_rows = lambda a, b: plan.take_blocks(matmul_left(hidden, grad_low).astype(low), table[orders[1]])[a:b]
-    outer_piece = plan.scatter_sum(outer_rows, orders[1], wide)
-    left = matmul_rows(normed_mlp, perms[orders[0]]).astype(low)
-    inner_piece = plan.scatter_sum(lambda a, b: matmul_left(left[:, a:b], grad_pre).astype(low), orders[0], width)
-    grad_normed_mlp = matmul_back(grad_pre, w_inner)
-    grad_branch, grad_mlp_gain = norm_pull(grad_normed_mlp, attended, mlp_gain)
-    grad_attended = grad_out + grad_branch
-    attn_low = grad_attended.astype(low)
-    grad_context = matmul_back(attn_low, w_output).astype(low)
-    left_c = matmul_rows(context, perms[orders[2]]).astype(low)
-    output_piece = plan.scatter_sum(lambda a, b: matmul_left(left_c[:, a:b], attn_low).astype(low), orders[2], width)
-    grad_query, dk, dv, diag = attn_bwd(pos, queries, grad_context, context, log_total, keys, values, bias, blk)
-    grad_kv = plan.reduce_keys([jnp.concatenate([a, b], axis=1) for a, b in zip(dk, dv)])
-    grad_qkv = jnp.concatenate([grad_query, grad_kv.astype(low)], axis=1)
-    left_n = matmul_rows(normed, perms[orders[3]]).astype(low)
-    qkv_piece = plan.scatter_sum(lambda a, b: matmul_left(left_n[:, a:b], grad_qkv).astype(low), orders[3], width)
-    grad_normed = matmul_back(grad_qkv, w_qkv)
-    grad_flat, grad_attn_gain = norm_pull(grad_normed, x, attn_gain)
-    attn_sum = plan.sum_z(jnp.concatenate([qkv_piece, output_piece], axis=2))
-    grads = (
-        grad_attn_gain,
-        attn_sum[:, :width],
-        attn_sum[:, width:2 * width],
-        attn_sum[:, 2 * width:3 * width],
-        attn_sum[:, 3 * width:],
-        grad_mlp_gain,
-        plan.sum_z(inner_piece),
-        plan.sum_z(outer_piece),
-    )
-    return grad_attended + grad_flat, grads, diag
+def project(x, gain, w_qkv):
+    normed = (x * inv_rms(x) * gain).astype(jnp.bfloat16)
+    return normed, matmul_rows(normed, w_qkv).astype(jnp.bfloat16)
+
+
+def widen(attended, gain, w_inner):
+    normed_mlp = (attended * inv_rms(attended) * gain).astype(jnp.bfloat16)
+    return (normed_mlp,) + gelu_pair(matmul_rows(normed_mlp, w_inner))
+
+
+def backward(plan, grad_out, layers, pos, bias, blk, perms, table, output_half):
+    low, f32 = jnp.bfloat16, jnp.float32
+    previous = None
+    results, diags = [], []
+    for weights, saved, orders in layers:
+        attn_gain, w_qkv, w_output, mlp_gain, w_inner, w_outer = weights
+        x, normed, queries, keys, values, context, log_total, attended, normed_mlp, hidden, slope = saved
+        width = x.shape[1]
+        grad_low = grad_out.astype(low)
+        wide = hidden.shape[1]
+        blocks = table[orders[1]]
+
+        def outer_rows(a, b, hidden=hidden, grad_low=grad_low, blocks=blocks, wide=wide):
+            if wide // blocks.shape[0] == TILE:
+                return outer_grad(hidden, grad_low, blocks, a // TILE, b // TILE)
+            return plan.take_blocks(matmul_left(hidden, grad_low).astype(low), blocks)[a:b]
+
+        def rows_of(left, right):
+            return lambda a, b: matmul_left(left[:, a:b], right).astype(low)
+
+        outer = Chain(plan, outer_rows, orders[1], wide)
+        late = [previous.outer.side, previous.inner.side] if previous else []
+        grad_out = tie(grad_out, outer.one(), *late)
+        outer.send_one()
+        grad_pre = (matmul_back(grad_out.astype(low), w_outer) * slope.astype(f32)).astype(low)
+        grad_pre = tie(grad_pre, outer.other)
+        left_m = matmul_rows(normed_mlp, perms[orders[0]]).astype(low)
+        inner = Chain(plan, rows_of(left_m, grad_pre), orders[0], width)
+        late = [previous.outer.close(), previous.inner.close()] if previous else []
+        grad_pre = tie(grad_pre, outer.two(), inner.one(), *late)
+        outer.send_two()
+        inner.send_one()
+        if previous:
+            previous.sum_mlp(plan)
+        grad_normed_mlp = matmul_back(grad_pre, w_inner)
+        grad_branch, grad_mlp_gain = norm_pull(grad_normed_mlp, attended, mlp_gain)
+        grad_attended = grad_out + grad_branch
+        late = [previous.qk.far, previous.ov.far] if previous else []
+        grad_attended = tie(grad_attended, inner.other, *late)
+        late = [part for c in (previous.qk, previous.ov) for part in (c.near(), c.three())] if previous else []
+        leaving = Held(output_half)
+        grad_attended = tie(grad_attended, inner.two(), *late, *([] if previous else [leaving]))
+        inner.send_two()
+        if not previous:
+            arrived = Held(plan.exchange(leaving.value, "s"))
+        if previous:
+            previous.qk.send_three()
+            previous.ov.send_three()
+        attn_low = grad_attended.astype(low)
+        grad_context = matmul_back(attn_low, w_output).astype(low)
+        left_c = matmul_rows(context, perms[orders[3]]).astype(low)
+        left_n = {o: matmul_rows(normed, perms[o]).astype(low) for o in orders[2:]}
+        grad_query, dk, dv, diag = attn_bwd(pos, queries, grad_context, context, log_total, keys, values, bias, blk, 0, 1)
+        kv_parts = [jnp.concatenate([p, r], axis=1) for p, r in zip(dk, dv)]
+        late = [previous.qk.side, previous.ov.side, previous.inner_sum, previous.outer_sum] if previous else [arrived]
+        last_part = tie(kv_parts[-1], outer.far, inner.far, *late)
+        grad_kv = plan.reduce_keys(kv_parts[:-1] + [last_part]).astype(low)
+        late = [previous.qk.close(), previous.ov.close()] if previous else []
+        grad_kv = tie(grad_kv, outer.near(), outer.three(), inner.near(), inner.three(), *late)
+        outer.send_three()
+        inner.send_three()
+        if previous:
+            previous.sum_attn(plan)
+        grad_qk = jnp.concatenate([grad_query, grad_kv[:, :width]], axis=1)
+        grad_v = grad_kv[:, width:]
+
+        def ov_rows(a, b, left_c=left_c, left_n=left_n[orders[3]], attn_low=attn_low, grad_v=grad_v):
+            return jnp.concatenate([matmul_left(left_c[:, a:b], attn_low).astype(low), matmul_left(left_n[:, a:b], grad_v).astype(low)], axis=1)
+
+        qk = Chain(plan, rows_of(left_n[orders[2]], grad_qk), orders[2], width)
+        ov = Chain(plan, ov_rows, orders[3], width)
+        grad_qk = tie(grad_qk, qk.one(), ov.one())
+        qk.send_one()
+        ov.send_one()
+        grad_normed = matmul_back(grad_qk, w_qkv[:, :2 * width]) + matmul_back(grad_v, w_qkv[:, 2 * width:])
+        grad_flat, grad_attn_gain = norm_pull(grad_normed, x, attn_gain)
+        grad_out = tie(grad_attended + grad_flat, qk.other, ov.other)
+        grad_out = tie(grad_out, qk.two(), ov.two())
+        qk.send_two()
+        ov.send_two()
+        previous = LayerSums(outer, inner, qk, ov, grad_attn_gain, grad_mlp_gain, width)
+        results.append(previous)
+        diags.append(diag)
+    grad_out = tie(grad_out, outer.side, inner.side, results[0].attn_sum)
+    grad_out = tie(grad_out, outer.close(), inner.close(), qk.near(), ov.near())
+    previous.sum_mlp(plan)
+    grad_out = tie(grad_out, qk.far, ov.far)
+    grad_out = tie(grad_out, qk.three(), ov.three())
+    qk.send_three()
+    ov.send_three()
+    qk.close()
+    ov.close()
+    previous.sum_attn(plan)
+    return grad_out, results, diags, arrived.value
+
+
+class LayerSums:
+    def __init__(self, outer, inner, qk, ov, grad_attn_gain, grad_mlp_gain, width):
+        self.outer, self.inner, self.qk, self.ov = outer, inner, qk, ov
+        self.attn_gain, self.mlp_gain, self.width = grad_attn_gain, grad_mlp_gain, width
+
+    def sum_mlp(self, plan):
+        self.inner_sum = Held(plan.sum_z(self.inner.piece.value))
+        self.outer_sum = Held(plan.sum_z(self.outer.piece.value))
+
+    def sum_attn(self, plan):
+        self.attn_sum = Held(plan.sum_z(jnp.concatenate([c.piece.value for c in (self.qk, self.ov)], axis=2)))
+
+    def grads(self):
+        w = self.width
+        f32 = jnp.float32
+        query, key, output, value = [self.attn_sum.value[:, i * w:(i + 1) * w].astype(f32) for i in range(4)]
+        return [self.attn_gain, query, key, value, output, self.mlp_gain, self.inner_sum.value.astype(f32), self.outer_sum.value.astype(f32)]
 
 
 def body(sizes, inputs, cotangent, lengths, bucket_ids, *params):
@@ -460,37 +701,90 @@
     small = jnp.pad(jnp.concatenate([gains, table_column], axis=1), ((0, 0), (0, TILE - 5)))
     everywhere = plan.everywhere
 
-    def gather(piece):
-        return lax.all_gather(piece, everywhere, axis=0, tiled=True)
-
-    first = gather(jnp.concatenate([one[1], one[2], one[3], small], axis=1))
-    second = gather(jnp.concatenate([one[4], one[6]], axis=1))
-    outers = gather(jnp.concatenate([one[7], two[7]], axis=1))
-    third = gather(jnp.concatenate([two[1], two[2], two[3], two[4], two[6]], axis=1))
-    smalls = first[:, 3 * width:].astype(f32)
-    gain = smalls[:, :4].T
-    whole_table = smalls[:, 4].reshape(-1, rows)[:, :bias_table.shape[0]].reshape(-1)
-    heads = width // DK
-    buckets = whole_table.shape[0] // heads
-    weights_one = (gain[0:1], first[:, :3 * width], second[:, :width], gain[1:2], second[:, width:], outers[:, :width])
-    weights_two = (gain[2:3], third[:, :3 * width], third[:, 3 * width:4 * width], gain[3:4], third[:, 4 * width:], outers[:, width:])
-
-    reversed_ids = jnp.concatenate([jnp.full((1,), -1, jnp.int32), bucket_ids[::-1]])
-    indicator = (reversed_ids[None, :] == jnp.arange(buckets, dtype=jnp.int32)[:, None]).astype(low)
-    bias = toeplitz_tiles(matmul_rows(whole_table.reshape(heads, buckets).astype(low), indicator))
-
     length = lax.dynamic_index_in_dim(lengths, plan.s, 0, keepdims=False)
     pos = plan.positions(length, blk)
     row = jnp.arange(blk, dtype=jnp.int32)
     row_pos = jnp.concatenate([row + pos[1] * TILE, row + pos[2] * TILE])
     row_valid = (row_pos < length).astype(f32)[:, None]
 
-    x = plan.to_sequences(inputs).astype(f32)
-    grad_out = plan.to_sequences(cotangent).astype(f32) * row_valid
-
-    middle, saved_one = layer_forward(plan, x, weights_one, pos, bias, blk)
-    final, saved_two = layer_forward(plan, middle, weights_two, pos, bias, blk)
-    output = plan.from_sequences((final * row_valid).astype(low))
+    shards = (
+        jnp.concatenate([one[1], one[2], one[3], one[4], small], axis=1),
+        one[6],
+        one[7],
+        jnp.concatenate([two[1], two[2], two[3], two[4]], axis=1),
+        two[6],
+        two[7],
+    )
+    attn_1, inner_1, outer_1, attn_2, inner_2, outer_2 = [Fetch(plan, piece) for piece in shards]
+    attn_1.start()
+    x = plan.to_sequences(inputs)
+    cotangent = plan.to_sequences(cotangent)
+    x = tie(x, inner_1.shard)
+    inner_1.start()
+    x = attn_1.a(x, outer_1)
+    x = attn_1.b(x)
+    x = attn_1.c(x)
+    x = inner_1.a(x, attn_2)
+    x = attn_1.d(x)
+    x, first = attn_1.e(x)
+    smalls = first[:, 4 * width:].astype(f32)
+    gain = smalls[:, :4].T
+    whole_table = smalls[:, 4].reshape(-1, rows)[:, :bias_table.shape[0]].reshape(-1)
+    heads = width // DK
+    buckets = whole_table.shape[0] // heads
+    reversed_ids = jnp.concatenate([jnp.full((1,), -1, jnp.int32), bucket_ids[::-1]])
+    indicator = (reversed_ids[None, :] == jnp.arange(buckets, dtype=jnp.int32)[:, None]).astype(low)
+    bias = Held(toeplitz_tiles(matmul_rows(whole_table.reshape(heads, buckets).astype(low), indicator)))
+    x = tie(x, bias)
+    bias = bias.value
+    x_one = x.astype(f32)
+    normed_one, qkv = project(x_one, gain[0:1], first[:, :3 * width])
+    qkv = inner_1.b(qkv)
+    kv = plan.gather_keys(qkv[:, width:])
+    qkv = inner_1.c(qkv)
+    qkv = outer_1.a(qkv, inner_2)
+    queries_one = qkv[:, :width]
+    keys_one, values_one = [p[:, :width] for p in kv], [p[:, width:] for p in kv]
+    context_one, log_one = attn_fwd(pos, queries_one, keys_one, values_one, bias, blk)
+    context_one = inner_1.d(context_one)
+    context_one, w_inner_one = inner_1.e(context_one)
+    attended_one = x_one + matmul_rows(context_one, first[:, 3 * width:4 * width])
+    attended_one = outer_1.b(attended_one)
+    normed_mlp_one, hidden_one, slope_one = widen(attended_one, gain[1:2], w_inner_one)
+    hidden_one = outer_1.c(hidden_one)
+    hidden_one = attn_2.a(hidden_one, outer_2)
+    hidden_one = outer_1.d(hidden_one)
+    hidden_one, w_outer_one = outer_1.e(hidden_one)
+    x_two = attended_one + matmul_rows(hidden_one, w_outer_one)
+    x_two = attn_2.b(x_two)
+    x_two = attn_2.c(x_two)
+    x_two = inner_2.a(x_two)
+    x_two = attn_2.d(x_two)
+    x_two, third = attn_2.e(x_two)
+    normed_two, qkv = project(x_two, gain[2:3], third[:, :3 * width])
+    qkv = inner_2.b(qkv)
+    kv = plan.gather_keys(qkv[:, width:])
+    qkv = inner_2.c(qkv)
+    qkv = outer_2.a(qkv)
+    queries_two = qkv[:, :width]
+    keys_two, values_two = [p[:, :width] for p in kv], [p[:, width:] for p in kv]
+    context_two, log_two = attn_fwd(pos, queries_two, keys_two, values_two, bias, blk)
+    context_two = inner_2.d(context_two)
+    context_two, w_inner_two = inner_2.e(context_two)
+    attended_two = x_two + matmul_rows(context_two, third[:, 3 * width:])
+    attended_two = outer_2.b(attended_two)
+    normed_mlp_two, hidden_two, slope_two = widen(attended_two, gain[3:4], w_inner_two)
+    hidden_two = outer_2.c(hidden_two)
+    hidden_two = outer_2.d(hidden_two)
+    hidden_two, w_outer_two = outer_2.e(hidden_two)
+    final = attended_two + matmul_rows(hidden_two, w_outer_two)
+    output_rows = (final * row_valid).astype(low)
+    grad_out = cotangent.astype(f32) * row_valid
+
+    weights_one = (gain[0:1], first[:, :3 * width], first[:, 3 * width:4 * width], gain[1:2], w_inner_one, w_outer_one)
+    weights_two = (gain[2:3], third[:, :3 * width], third[:, 3 * width:], gain[3:4], w_inner_two, w_outer_two)
+    saved_one = (x_one, normed_one, queries_one, keys_one, values_one, context_one, log_one, attended_one, normed_mlp_one, hidden_one, slope_one)
+    saved_two = (x_two, normed_two, queries_two, keys_two, values_two, context_two, log_two, attended_two, normed_mlp_two, hidden_two, slope_two)
 
     xy, yx = ("x", "y"), ("y", "x")
     perms = {o: plan.permutation(o, width) for o in (xy, yx)}
@@ -499,13 +793,17 @@
     blocks = jnp.arange(saved_one[9].shape[1] // step, dtype=jnp.int32)
     per = depth // step
     table = {o: plan.block_of(o, blocks // per) * per + blocks % per for o in (xy, yx)}
-    grad_middle, grads_two, diag_two = layer_backward(plan, grad_out, weights_two, saved_two, pos, bias, blk, perms, table, (xy, yx, yx, xy))
-    grad_state, grads_one, diag_one = layer_backward(plan, grad_middle, weights_one, saved_one, pos, bias, blk, perms, table, (xy, yx, xy, yx))
+    layers = [(weights_two, saved_two, (xy, yx, yx, xy)), (weights_one, saved_one, (xy, yx, yx, xy))]
+    grad_state, sums, diags, arrived = backward(plan, grad_out, layers, pos, bias, blk, perms, table, output_rows[blk:])
+    output = plan.in_order(output_rows[:blk], arrived)
+    grads_two, grads_one = sums[0].grads(), sums[1].grads()
     input_grad = plan.from_sequences(grad_state.astype(low))
 
-    grad_table = lax.dot_general(diag_one + diag_two, indicator.astype(f32), (((1,), (1,)), ((), ())), precision=HIGH_PRECISION)
+    grad_table = lax.dot_general(diags[0] + diags[1], indicator.astype(f32), (((1,), (1,)), ((), ())), precision=HIGH_PRECISION)
     vectors = jnp.concatenate([grads_one[0], grads_one[5], grads_two[0], grads_two[5], grad_table.reshape(-1)])
-    vectors = lax.psum(vectors, everywhere)
+    held = Held(vectors)
+    grad_state = tie(grad_state, held)
+    vectors = plan.sum_vector(held.value)
     device = ((plan.z * plan.ny + plan.y) * plan.nx + plan.x) * 2 + plan.core
 
     def share(start, count):

time: 1060 us -> 815 us (0.77)
  waiting for transfers between devices: 482 us -> 194 us
  blocking collectives: 68.6 us -> 0 us
  Pallas kernels: 142 us -> 188 us
  starting transfers between devices: 28.1 us -> 62.2 us
  local copies, waits for them, and re-layouts: 36.9 us -> 61.8 us
    all_gather x4 -> x6, waiting for transfers between devices: 276 us -> 14.1 us  [start(): self.near = Held(lax.all_gather(self.shard.value, axes, axis=0, tiled=True))]
    psum x1 -> x0, blocking collectives: 68.6 us -> none  [body(): vectors = lax.psum(vectors, everywhere)]
    pallas_call x0 -> x6, Pallas kernels: none -> 48.6 us  [assemble(): pl.pallas_call(functools.partial(assemble_kernel, steps, depth), grid_spe...]
    ppermute x32 -> x86, starting transfers between devices: 27.5 us -> 56.2 us  [exchange(): return lax.ppermute(piece, name, SWAP)]
    slice x10 -> x30, local copies, waits for them, and re-layouts: 9.67 us -> 37.2 us  [the longest x6 8.56 us: b(): self.high = Held(self.plan.exchange(self.by_x.value[half:], 'y'))]
    reduce_scatter x6, waiting for transfers between devices: 42.5 us -> 16.6 us  [sum_z(): return lax.psum_scatter(piece, 'z', scatter_dimension=0, tiled=False)]
    dot_general x18 -> x24, matrix products: 63 us -> 53.9 us  [matmul_left(): lax.dot_general(left, right, (((0,), (0,)), ((), ())), preferred_element_...]
    dot_general x8 -> x10, matrix products: 60.4 us -> 69.1 us  [matmul_back(): lax.dot_general(left, right, (((1,), (1,)), ((), ())), preferred_element_...]
  transfers between devices with their start and end apart: 42 -> 103, of which waited for: 18 -> 36; matrix products, arithmetic and copies ran while one was open for 25% -> 36% of each run, Pallas kernels for 12% -> 22%
where the time goes in v2:
time: 815 us; the launch traced here: 807 us
  matrix products  196 us (24%)
  waiting for transfers between devices  194 us (24%)
  Pallas kernels  188 us (23%)
  other arithmetic  88 us (11%)
  starting transfers between devices  62.2 us (8%)
  local copies, waits for them, and re-layouts  61.8 us (8%)
  between operations  16.5 us (2%)
    ppermute x86, waiting for transfers between devices, exchange(): return lax.ppermute(piece, name, SWAP)  158 us
    dot_general x17, matrix products, matmul_rows(): return jnp.dot(left, right, preferred_element_type=jnp.float32)  73.2 us
    pallas_call x2, Pallas kernels, attn_bwd(): pl.pallas_call(functools.partial(attn_bwd_kernel, parts, chunk, blk), gri...  71.2 us
    dot_general x10, matrix products, matmul_back(): lax.dot_general(left, right, (((1,), (1,)), ((), ())), preferred_element_...  69.1 us
    ppermute x86, starting transfers between devices, exchange(): return lax.ppermute(piece, name, SWAP)  56.2 us
    dot_general x24, matrix products, matmul_left(): lax.dot_general(left, right, (((0,), (0,)), ((), ())), preferred_element_...  53.9 us
    convert_element_type x20, other arithmetic, add_low(): return total.astype(jnp.bfloat16)  51.2 us
    pallas_call x6, Pallas kernels, assemble(): pl.pallas_call(functools.partial(assemble_kernel, steps, depth), grid_spe...  48.6 us
  transfers between devices with their start and end apart: 103, of which 36 were waited for; matrix products, arithmetic and copies ran while one was open for 36% of the time, Pallas kernels for 22%

profile of v2, /device:TPU:0, one launch (start us, length us, event | category | flops | bytes accessed | tf_op | source)
XLA Modules:
  0.0 806.6 jit_solution(10765592847938836345)
XLA Ops:
  17.3 11.9 %collective-permute-done = bf16[256,1024]{1,0:T(8,128)(2,1)S(1)} collective-permute-done((bf16[256,1024]{1,0:T(8,128)(2,1)S(1)}, bf16[256,1024]{1,0:T(8,128)(2,1)S(1)}, u32[]{:S(2)}, u32[]{:S(2)}) %collective-permute-start) | collective-permute-done | bytes 524320 | tf_op jit(solution)/shard_map/ppermute | solution.py:310
  30.3 14.0 %all-gather.7.cloned.1.call-done.refs_0_ = bf16[128,4224]{1,0:T(8,128)(2,1)} async-done(((bf16[32,4224]{1,0:T(8,128)(2,1)}), bf16[128,4224]{1,0:T(8,128)(2,1)}) %all-gather.7.cloned.1.call-update) | async-done | bytes 1081360 | tf_op jit(solution)/shard_map/all_gather | solution.py:420
  50.5 20.9 %collective-permute-done.1.refs_2_ = bf16[128,4224]{1,0:T(8,128)(2,1)} collective-permute-done((bf16[128,4224]{1,0:T(8,128)(2,1)}, bf16[128,4224]{1,0:T(8,128)(2,1)}, u32[]{:S(2)}, u32[]{:S(2)}) %collective-permute-start.1) | collective-permute-done | bytes 1081376 | tf_op jit(solution)/shard_map/ppermute | solution.py:310
  80.6 13.5 %collective-permute-done.6.refs_6_ = bf16[64,4224]{1,0:T(8,128)(2,1)S(1)} collective-permute-done((bf16[64,4224]{1,0:T(8,128)(2,1)S(1)}, bf16[64,4224]{1,0:T(8,128)(2,1)S(1)}, u32[]{:S(2)}, u32[]{:S(2)}) %collective-permute-start.6) | collective-permute-done | bytes 540704 | tf_op jit(solution)/shard_map/ppermute | solution.py:310
  107.3 10.9 %toeplitz.1.refs_4_ = bf16[16,15,128,128]{3,2,1,0:T(8,128)(2,1)} custom-call(f32[16,1,2048]{2,1,0:T(1,128)} %reshape.163.u_ref), custom_call_target="tpu_custom_call" | custom-call | flops 15728640 | bytes 7864320 | tf_op jit(solution)/shard_map/toeplitz/pallas_call | solution.py:28
  145.9 19.5 %attn_fwd.2 = (bf16[512,1024]{1,0:T(8,128)(2,1)S(1)}, f32[8,2,512]{2,1,0:T(2,128)S(1)}) custom-call(s32[7]{0:T(128)S(1)} %stack.74.pos_ref, bf16[512,1024]{1,0:T(8,128)(2,1)S(1)} %slice.473.q_ref, bf16[512,1024]{1,0:T(8,128)(2,1)S(1)} %copy-done.11, bf16[512,1024]{1,0:T(8,128)(2,1)S(1)} %get-tuple-element.478.refs_1_, ...), custom_call_target="tpu_custom_call" | custom-call | flops 8589934592 | bytes 14155776 | tf_op jit(solution)/shard_map/attn_fwd/pallas_call | solution.py:114
  187.5 9.0 %multiply_convert_fusion.3 = (bf16[512,4096]{1,0:T(8,128)(2,1)}, f32[512,4096]{1,0:T(8,128)}) fusion(bf16[1024,4096]{1,0:T(8,128)(2,1)S(1)} %copy-done.43, f32[512,1024]{1,0:T(8,128)S(1)} %convert_add_fusion, f32[1024]{0:T(1024)S(1)} %get-tuple-element.461, f32[512]{0:T(512)S(1)} %get-tuple-element.528), kind=kOutput, calls=%fused_computation.28 | convolution fusion | flops 4315414528 | bytes 23074816 | tf_op jit(solution)/shard_map/dot_general | solution.py:238
  208.4 9.7 %assemble.8 = bf16[4096,1024]{1,0:T(8,128)(2,1)} custom-call(s32[10]{0:T(128)S(1)} %pad_add_fusion.1.table_ref, bf16[512,1024]{1,0:T(8,128)(2,1)S(1)} %copy-done.3, bf16[512,1024]{1,0:T(8,128)(2,1)} %collective-permute-done.22.refs_1_, bf16[512,1024]{1,0:T(8,128)(2,1)} %collective-permute-done.20.refs_2_, bf16[512,1024]{1,0:T(8,128)(2,1)} %copy-done.82, ...), custom_call_target="tpu_custom_call" | custom-call | bytes 16777216 | tf_op jit(solution)/shard_map/assemble/pallas_call | solution.py:385
  218.2 8.7 %convolution_add_fusion = f32[512,1024]{1,0:T(8,128)} fusion(f32[512,1024]{1,0:T(8,128)S(1)} %copy-done.46, bf16[512,4096]{1,0:T(8,128)(2,1)S(1)} %copy-done, bf16[4096,1024]{1,0:T(8,128)(2,1)} %assemble.8), kind=kOutput, calls=%fused_computation.174 | convolution fusion | flops 4295491584 | bytes 16777216 | tf_op jit(solution)/shard_map/dot_general | solution.py:238
  241.1 8.1 %collective-permute-done.34.refs_6_ = bf16[64,4096]{1,0:T(8,128)(2,1)} collective-permute-done((bf16[64,4096]{1,0:T(8,128)(2,1)S(1)}, bf16[64,4096]{1,0:T(8,128)(2,1)}, u32[]{:S(2)}, u32[]{:S(2)}) %collective-permute-start.34) | collective-permute-done | bytes 524320 | tf_op jit(solution)/shard_map/ppermute | solution.py:310
  253.8 8.1 %assemble.9 = bf16[1024,4096]{1,0:T(8,128)(2,1)} custom-call(s32[10]{0:T(128)S(1)} %pad_add_fusion.1.table_ref, bf16[128,4096]{1,0:T(8,128)(2,1)S(1)} %copy-done.4, bf16[128,4096]{1,0:T(8,128)(2,1)} %copy-done.78, bf16[128,4096]{1,0:T(8,128)(2,1)} %collective-permute-done.29.refs_2_, bf16[128,4096]{1,0:T(8,128)(2,1)} %collective-permute-done.32.refs_3_, ...), custom_call_target="tpu_custom_call" | custom-call | bytes 16777216 | tf_op jit(solution)/shard_map/assemble/pallas_call | solution.py:385
  289.3 19.5 %attn_fwd.3 = (bf16[512,1024]{1,0:T(8,128)(2,1)S(1)}, f32[8,2,512]{2,1,0:T(2,128)S(1)}) custom-call(s32[7]{0:T(128)S(1)} %stack.74.pos_ref, bf16[512,1024]{1,0:T(8,128)(2,1)S(1)} %slice.498.q_ref, bf16[512,1024]{1,0:T(8,128)(2,1)S(1)} %copy-done.14, bf16[512,1024]{1,0:T(8,128)(2,1)S(1)} %get-tuple-element.476.refs_1_, ...), custom_call_target="tpu_custom_call" | custom-call | flops 8589934592 | bytes 14155776 | tf_op jit(solution)/shard_map/attn_fwd/pallas_call | solution.py:114
  311.8 8.2 %assemble.10 = bf16[1024,4096]{1,0:T(8,128)(2,1)} custom-call(s32[10]{0:T(128)S(1)} %pad_add_fusion.1.table_ref, bf16[128,4096]{1,0:T(8,128)(2,1)S(1)} %copy-done.7, bf16[128,4096]{1,0:T(8,128)(2,1)} %copy-done.74, bf16[128,4096]{1,0:T(8,128)(2,1)} %copy-done.66, bf16[128,4096]{1,0:T(8,128)(2,1)} %copy-done.81, ...), custom_call_target="tpu_custom_call" | custom-call | bytes 16777216 | tf_op jit(solution)/shard_map/assemble/pallas_call | solution.py:385
  329.1 8.4 %multiply_convert_fusion.2 = (bf16[512,4096]{1,0:T(8,128)(2,1)S(1)}, f32[512,4096]{1,0:T(8,128)}) fusion(bf16[1024,4096]{1,0:T(8,128)(2,1)S(1)} %copy-done.44, f32[512,1024]{1,0:T(8,128)S(1)} %fusion.88, f32[1024]{0:T(1024)S(1)} %copy-done.112, f32[512]{0:T(512)S(1)} %get-tuple-element.532), kind=kOutput, calls=%fused_computation.26 | convolution fusion | flops 4315414528 | bytes 23074816 | tf_op jit(solution)/shard_map/dot_general | solution.py:238
  364.0 12.1 %multiply_convert_fusion.1 = bf16[512,4096]{1,0:T(8,128)(2,1)S(1)} fusion(bf16[4096,1024]{1,0:T(8,128)(2,1)} %assemble.11, f32[512,4096]{1,0:T(8,128)} %get-tuple-element.536, f32[512,1024]{1,0:T(8,128)} %get-tuple-element.347), kind=kOutput, calls=%fused_computation.25 | convolution fusion | flops 4335337472 | bytes 23068672 | tf_op jit(solution)/shard_map/dot_general | solution.py:246
  417.5 35.6 %attn_bwd.2 = (bf16[512,1024]{1,0:T(8,128)(2,1)S(1)}, bf16[512,1024]{1,0:T(8,128)(2,1)S(1)}, bf16[512,1024]{1,0:T(8,128)(2,1)S(1)}, bf16[512,1024]{1,0:T(8,128)(...) custom-call(s32[7]{0:T(128)S(1)} %copy-done.17, bf16[512,1024]{1,0:T(8,128)(2,1)} %copy-done.9, ...), custom_call_target="tpu_custom_call" | custom-call | flops 21474836480 | bytes 20447232 | tf_op jit(solution)/shard_map/attn_bwd/pallas_call | solution.py:217
  453.8 20.9 %collective-permute-done.62 = bf16[256,1024]{1,0:T(8,128)(2,1)S(1)} collective-permute-done((bf16[256,1024]{1,0:T(8,128)(2,1)S(1)}, bf16[256,1024]{1,0:T(8,128)(2,1)S(1)}, u32[]{:S(2)}, u32[]{:S(2)}) %collective-permute-start.62) | collective-permute-done | bytes 524320 | tf_op jit(solution)/shard_map/ppermute | solution.py:310
  529.1 11.9 %multiply_convert_fusion = bf16[512,4096]{1,0:T(8,128)(2,1)S(1)} fusion(bf16[4096,1024]{1,0:T(8,128)(2,1)} %assemble.8, f32[512,4096]{1,0:T(8,128)} %get-tuple-element.534, f32[512,1024]{1,0:T(8,128)S(1)} %subtract_add_fusion.1), kind=kOutput, calls=%fused_computation.24 | convolution fusion | flops 4335337472 | bytes 23068672 | tf_op jit(solution)/shard_map/dot_general | solution.py:246
  560.1 10.3 %multiply_reduce_fusion.2 = (f32[1024]{0:T(1024)}, f32[512]{0:T(512)S(1)}, f32[512,1024]{1,0:T(8,128)}) fusion(f32[512,1024]{1,0:T(8,128)S(1)} %copy-done.48, f32[512]{0:T(512)S(1)} %copy-done.123, f32[1024]{0:T(1024)S(1)} %copy-done.111, bf16[512,4096]{1,0:T(8,128)(2,1)S(1)} %copy-done.22, bf16[1024,4096]{1,0:T(8,128)(2,1)} %assemble.7), kind=kOutput, calls=%fused_computation.128 | convolution fusion | flops 4298111488 | bytes 16789504 | tf_op jit(solution)/shard_map/dot_general | solution.py:246
  597.2 35.6 %attn_bwd.3 = (bf16[512,1024]{1,0:T(8,128)(2,1)S(1)}, bf16[512,1024]{1,0:T(8,128)(2,1)S(1)}, bf16[512,1024]{1,0:T(8,128)(2,1)S(1)}, bf16[512,1024]{1,0:T(8,128)(...) custom-call(s32[7]{0:T(128)S(1)} %copy-done.17, bf16[512,1024]{1,0:T(8,128)(2,1)} %copy-done.8, ...), custom_call_target="tpu_custom_call" | custom-call | flops 21474836480 | bytes 20447232 | tf_op jit(solution)/shard_map/attn_bwd/pallas_call | solution.py:217
  642.8 8.9 %collective-permute-done.74 = bf16[128,2048]{1,0:T(8,128)(2,1)} collective-permute-done((bf16[128,2048]{1,0:T(8,128)(2,1)}, bf16[128,2048]{1,0:T(8,128)(2,1)}, u32[]{:S(2)}, u32[]{:S(2)}) %collective-permute-start.74) | collective-permute-done | bytes 524320 | tf_op jit(solution)/shard_map/ppermute | solution.py:310
  696.1 11.1 %collective-permute-done.79 = bf16[512,1024]{1,0:T(8,128)(2,1)S(1)} collective-permute-done((bf16[512,1024]{1,0:T(8,128)(2,1)S(1)}, bf16[512,1024]{1,0:T(8,128)(2,1)S(1)}, u32[]{:S(2)}, u32[]{:S(2)}) %collective-permute-start.79) | collective-permute-done | bytes 1048608 | tf_op jit(solution)/shard_map/ppermute | solution.py:310
  717.6 22.3 %collective-permute-done.81 = bf16[256,2048]{1,0:T(8,128)(2,1)} collective-permute-done((bf16[256,2048]{1,0:T(8,128)(2,1)}, bf16[256,2048]{1,0:T(8,128)(2,1)}, u32[]{:S(2)}, u32[]{:S(2)}) %collective-permute-start.81) | collective-permute-done | bytes 1048608 | tf_op jit(solution)/shard_map/ppermute | solution.py:310
  781.1 16.6 %reduce-scatter.13.cloned.1.call-done = bf16[1,32,4096]{2,1,0:T(8,128)(2,1)} async-done(((bf16[4,32,4096]{2,1,0:T(8,128)(2,1)}), bf16[1,32,4096]{2,1,0:T(8,128)(2,1)}) %reduce-scatter.13.cloned.1.call-update) | async-done | bytes 262160 | tf_op jit(solution)/shard_map/reduce_scatter | solution.py:315
  (680 shorter events, 434.4 us)
Async XLA Ops:
  13.0 66.5 %all-gather.9.cloned.1.call-start = ((), (), s32[]{:S(2)}) async-start(), calls=%async_computation.7 | async-start | bytes 1310720 | tf_op jit(solution)/shard_map/all_gather | solution.py:420
  48.3 81.1 %collective-permute-start.57 = (bf16[256,1024]{1,0:T(8,128)(2,1)}, bf16[256,1024]{1,0:T(8,128)(2,1)}, u32[]{:S(2)}, u32[]{:S(2)}) collective-permute-start(bf16[256,1024]{1,0:T(8,128)(2,1)} %get-tuple-element.498), channel_id=1, source_target_pairs={{0,2},{2,0},{1,3},{3,1},{4,6},{6,4},{5,7},{7,5},{8,10},{10,8},{9,1... | collective-permute-start | bytes 1572872 | tf_op jit(solution)/shard_map/ppermute | solution.py:310
  50.4 89.9 %all-gather.11.cloned.1.call-start = ((), (), s32[]{:S(2)}) async-start(), calls=%async_computation.8 | async-start | bytes 1310720 | tf_op jit(solution)/shard_map/all_gather | solution.py:420
  79.3 117.2 %all-gather.13.cloned.1.call-start = ((), (), s32[]{:S(2)}) async-start(), calls=%async_computation.9 | async-start | bytes 1310720 | tf_op jit(solution)/shard_map/all_gather | solution.py:420
  79.4 47.5 %collective-permute-start.10 = (bf16[128,4096]{1,0:T(8,128)(2,1)}, bf16[128,4096]{1,0:T(8,128)(2,1)}, u32[]{:S(2)}, u32[]{:S(2)}) collective-permute-start(bf16[128,4096]{1,0:T(8,128)(2,1)} %all-gather.9.cloned.1.call-done.refs_0_), channel_id=1, source_target_pairs={{0,2},{2,0},{1,3},{3,1},{4,6},{6,4},{5,7},{7,5},{8,10},{10,8},{9,1... | collective-permute-start | bytes 3145736 | tf_op jit(solution)/shard_map/ppermute | solution.py:310
  80.1 46.9 %collective-permute-start.11 = (bf16[128,4096]{1,0:T(8,128)(2,1)}, bf16[128,4096]{1,0:T(8,128)(2,1)}, u32[]{:S(2)}, u32[]{:S(2)}) collective-permute-start(bf16[128,4096]{1,0:T(8,128)(2,1)} %all-gather.9.cloned.1.call-done.refs_0_), channel_id=1, source_target_pairs={{0,4},{4,0},{1,5},{5,1},{2,6},{6,2},{3,7},{7,3},{8,12},{12,8},{9,1... | collective-permute-start | bytes 3145736 | tf_op jit(solution)/shard_map/ppermute | solution.py:310
  132.1 108.0 %all-gather.15.cloned.1.call-start = ((), (), s32[]{:S(2)}) async-start(), calls=%async_computation.10 | async-start | bytes 1310720 | tf_op jit(solution)/shard_map/all_gather | solution.py:420
  140.4 39.1 %collective-permute-start.20 = (bf16[512,1024]{1,0:T(8,128)(2,1)}, bf16[512,1024]{1,0:T(8,128)(2,1)}, u32[]{:S(2)}, u32[]{:S(2)}) collective-permute-start(bf16[512,1024]{1,0:T(8,128)(2,1)} %all-gather.11.cloned.1.call-done.refs_0_), channel_id=1, source_target_pairs={{0,2},{2,0},{1,3},{3,1},{4,6},{6,4},{5,7},{7,5},{8,10},{10,8},{9,1... | collective-permute-start | bytes 3145736 | tf_op jit(solution)/shard_map/ppermute | solution.py:310
  204.5 78.5 %all-gather.17.cloned.1.call-start = ((), (), s32[]{:S(2)}) async-start(), calls=%async_computation.11 | async-start | bytes 1310720 | tf_op jit(solution)/shard_map/all_gather | solution.py:420
  239.9 402.9 %reduce-scatter.7.cloned.1.call-start = ((), (), s32[]{:S(2)}) async-start(), calls=%async_computation.12 | async-start | bytes 1310720 | tf_op jit(solution)/shard_map/reduce_scatter | solution.py:315
  282.9 40.1 %collective-permute-start.48 = (bf16[512,1024]{1,0:T(8,128)(2,1)}, bf16[512,1024]{1,0:T(8,128)(2,1)S(1)}, u32[]{:S(2)}, u32[]{:S(2)}) collective-permute-start(bf16[512,1024]{1,0:T(8,128)(2,1)} %all-gather.17.cloned.1.call-done.refs_0_), channel_id=1, source_target_pairs={{0,2},{2,0},{1,3},{3,1},{4,6},{6,4},{5,7},{7,5},{8,10},{10,8},{9,1... | collective-permute-start | bytes 3145736 | tf_op jit(solution)/shard_map/ppermute | solution.py:310
  284.4 38.6 %collective-permute-start.49 = (bf16[512,1024]{1,0:T(8,128)(2,1)}, bf16[512,1024]{1,0:T(8,128)(2,1)}, u32[]{:S(2)}, u32[]{:S(2)}) collective-permute-start(bf16[512,1024]{1,0:T(8,128)(2,1)} %all-gather.17.cloned.1.call-done.refs_0_), channel_id=1, source_target_pairs={{0,4},{4,0},{1,5},{5,1},{2,6},{6,2},{3,7},{7,3},{8,12},{12,8},{9,1... | collective-permute-start | bytes 3145736 | tf_op jit(solution)/shard_map/ppermute | solution.py:310
  396.3 57.5 %collective-permute-start.60 = (bf16[1024,1024]{1,0:T(8,128)(2,1)}, bf16[1024,1024]{1,0:T(8,128)(2,1)S(1)}, u32[]{:S(2)}, u32[]{:S(2)}) collective-permute-start(bf16[1024,1024]{1,0:T(8,128)(2,1)} %get-tuple-element.359), channel_id=1, source_target_pairs={{0,4},{4,0},{1,5},{5,1},{2,6},{6,2},{3,7},{7,3},{8,12},{12,8},{9,1... | collective-permute-start | bytes 6291464 | tf_op jit(solution)/shard_map/ppermute | solution.py:310
  415.5 59.2 %collective-permute-start.61 = (bf16[256,4096]{1,0:T(8,128)(2,1)}, bf16[256,4096]{1,0:T(8,128)(2,1)}, u32[]{:S(2)}, u32[]{:S(2)}) collective-permute-start(bf16[256,4096]{1,0:T(8,128)(2,1)} %fusion.31), channel_id=1, source_target_pairs={{0,2},{2,0},{1,3},{3,1},{4,6},{6,4},{5,7},{7,5},{8,10},{10,8},{9,1... | collective-permute-start | bytes 6291464 | tf_op jit(solution)/shard_map/ppermute | solution.py:310
  416.9 57.8 %collective-permute-start.62 = (bf16[256,1024]{1,0:T(8,128)(2,1)S(1)}, bf16[256,1024]{1,0:T(8,128)(2,1)S(1)}, u32[]{:S(2)}, u32[]{:S(2)}) collective-permute-start(bf16[256,1024]{1,0:T(8,128)(2,1)S(1)} %slice.620), channel_id=1, source_target_pairs={{0,2},{2,0},{1,3},{3,1},{4,6},{6,4},{5,7},{7,5},{8,10},{10,8},{9,1... | collective-permute-start | bytes 1572872 | tf_op jit(solution)/shard_map/ppermute | solution.py:310
  552.6 90.2 %reduce-scatter.9.cloned.1.call-start = ((), (), s32[]{:S(2)}) async-start(), calls=%async_computation.13 | async-start | bytes 1310720 | tf_op jit(solution)/shard_map/reduce_scatter | solution.py:315
  570.4 72.4 %collective-permute-start.72 = (bf16[1024,1024]{1,0:T(8,128)(2,1)}, bf16[1024,1024]{1,0:T(8,128)(2,1)}, u32[]{:S(2)}, u32[]{:S(2)}) collective-permute-start(bf16[1024,1024]{1,0:T(8,128)(2,1)} %get-tuple-element.402), channel_id=1, source_target_pairs={{0,4},{4,0},{1,5},{5,1},{2,6},{6,2},{3,7},{7,3},{8,12},{12,8},{9,1... | collective-permute-start | bytes 6291464 | tf_op jit(solution)/shard_map/ppermute | solution.py:310
  571.7 136.4 %reduce-scatter.11.cloned.1.call-start = ((), (), s32[]{:S(2)}) async-start(), calls=%async_computation.14 | async-start | bytes 1310720 | tf_op jit(solution)/shard_map/reduce_scatter | solution.py:315
  594.3 57.3 %collective-permute-start.73 = (bf16[256,4096]{1,0:T(8,128)(2,1)}, bf16[256,4096]{1,0:T(8,128)(2,1)}, u32[]{:S(2)}, u32[]{:S(2)}) collective-permute-start(bf16[256,4096]{1,0:T(8,128)(2,1)} %fusion.25), channel_id=1, source_target_pairs={{0,2},{2,0},{1,3},{3,1},{4,6},{6,4},{5,7},{7,5},{8,10},{10,8},{9,1... | collective-permute-start | bytes 6291464 | tf_op jit(solution)/shard_map/ppermute | solution.py:310
  594.9 56.8 %collective-permute-start.74 = (bf16[128,2048]{1,0:T(8,128)(2,1)}, bf16[128,2048]{1,0:T(8,128)(2,1)}, u32[]{:S(2)}, u32[]{:S(2)}) collective-permute-start(bf16[128,2048]{1,0:T(8,128)(2,1)} %add_convert_fusion.29), channel_id=1, source_target_pairs={{0,2},{2,0},{1,3},{3,1},{4,6},{6,4},{5,7},{7,5},{8,10},{10,8},{9,1... | collective-permute-start | bytes 1572872 | tf_op jit(solution)/shard_map/ppermute | solution.py:310
  596.4 55.3 %collective-permute-start.75 = (bf16[128,2048]{1,0:T(8,128)(2,1)}, bf16[128,2048]{1,0:T(8,128)(2,1)}, u32[]{:S(2)}, u32[]{:S(2)}) collective-permute-start(bf16[128,2048]{1,0:T(8,128)(2,1)} %add_convert_fusion.28), channel_id=1, source_target_pairs={{0,4},{4,0},{1,5},{5,1},{2,6},{6,2},{3,7},{7,3},{8,12},{12,8},{9,1... | collective-permute-start | bytes 1572872 | tf_op jit(solution)/shard_map/ppermute | solution.py:310
  674.2 103.4 %reduce-scatter.17.cloned.1.call-start = ((), (), s32[]{:S(2)}) async-start(), calls=%async_computation.17 | async-start | bytes 1310720 | tf_op jit(solution)/shard_map/reduce_scatter | solution.py:315
  714.6 64.7 %reduce-scatter.15.cloned.1.call-start = ((), (), s32[]{:S(2)}) async-start(), calls=%async_computation.16 | async-start | bytes 1310720 | tf_op jit(solution)/shard_map/reduce_scatter | solution.py:315
  717.6 80.2 %reduce-scatter.13.cloned.1.call-start = ((), (), s32[]{:S(2)}) async-start(), calls=%async_computation.15 | async-start | bytes 1310720 | tf_op jit(solution)/shard_map/reduce_scatter | solution.py:315
  (218 other events, 3894.2 us)
Sparse Core Ops, SparseCore 0:
  13.1 31.1 all-gather.6
  50.5 26.4 all-gather.8
  79.5 26.6 all-gather.10
  132.2 27.4 all-gather.12
  204.6 26.5 all-gather.14
  240.1 25.5 all-gather.16
  552.7 24.8 reduce-scatter.6
  579.9 25.7 reduce-scatter.8
  674.3 25.7 reduce-scatter.10
  714.7 25.8 reduce-scatter.16
  743.0 26.6 reduce-scatter.14
  771.9 25.7 reduce-scatter.12

commit v3 on v2

--- a/solution.py
+++ b/solution.py
@@ -14,6 +14,7 @@
 EPS = 1e-06
 NEGATIVE = -1e30
 HIGH_PRECISION = lax.Precision.HIGHEST
+BRIEF = pl.CostEstimate(flops=1024, bytes_accessed=1024, transcendentals=0)
 
 
 def toeplitz_kernel(span, u_ref, t_ref):
@@ -31,7 +32,7 @@
         in_specs=[pl.BlockSpec((1, 1, width), lambda h: (h, 0, 0))],
         out_specs=pl.BlockSpec((1, span, TILE, TILE), lambda h: (h, 0, 0, 0)),
         out_shape=jax.ShapeDtypeStruct((heads, span, TILE, TILE), jnp.bfloat16),
-        cost_estimate=pl.CostEstimate(flops=heads * span * TILE * TILE * 4, bytes_accessed=heads * span * TILE * TILE * 2, transcendentals=0),
+        cost_estimate=BRIEF,
         name="toeplitz",
     )(u.reshape(heads, 1, width))
 
@@ -122,7 +123,7 @@
         ),
         out_shape=[jax.ShapeDtypeStruct((q_rows, width), jnp.bfloat16), jax.ShapeDtypeStruct((heads // 2, 2, q_rows), jnp.float32)],
         compiler_params=pltpu.CompilerParams(vmem_limit_bytes=48 << 20),
-        cost_estimate=pl.CostEstimate(flops=16 * q_rows * keys * width, bytes_accessed=4 * keys * width + 4 * q_rows * width + heads * span * TILE * TILE * 2, transcendentals=heads * q_rows * keys),
+        cost_estimate=BRIEF,
         name="attn_fwd",
     )(pos, q, *ks, *vs, bias)
     return o, lse
@@ -227,7 +228,7 @@
         + [jax.ShapeDtypeStruct((rows, width), jnp.bfloat16)] * (2 * parts)
         + [jax.ShapeDtypeStruct((heads // 2, 2, (span + 1) * TILE), jnp.float32)],
         compiler_params=pltpu.CompilerParams(vmem_limit_bytes=48 << 20),
-        cost_estimate=pl.CostEstimate(flops=40 * q_rows * keys * width, bytes_accessed=8 * keys * width + 8 * q_rows * width + heads * span * TILE * TILE * 2, transcendentals=heads * q_rows * keys),
+        cost_estimate=BRIEF,
         name="attn_bwd",
     )(pos, q, do, o, lse, *ks, *vs, bias)
     dq, dks, dvs, d = out[0], out[1:1 + parts], out[1 + parts:1 + 2 * parts], out[-1]
@@ -250,13 +251,97 @@
     return lax.rsqrt(jnp.mean(values * values, axis=-1, keepdims=True) + EPS)
 
 
-def norm_pull(grad, values, gain):
+def norm_back(grad, values, gain):
     scale = inv_rms(values)
     weighted = gain * grad
     mean = jnp.mean(weighted * values, axis=-1, keepdims=True)
     grad_in = scale * weighted - values * (scale * scale * scale) * mean
-    grad_gain = jnp.sum(grad * values * scale, axis=0)
-    return grad_in, grad_gain
+    return grad_in, jnp.sum(grad * values * scale, axis=0, keepdims=True)
+
+
+def mlp_back_kernel(grad_ref, value_ref, gain_ref, outer_ref, inner_ref, slope_ref, pre_ref, out_ref, low_ref, gain_grad_ref, acc_ref, left_ref):
+    i = pl.program_id(0)
+
+    @pl.when(i == 0)
+    def _():
+        left_ref[...] = grad_ref[...].astype(jnp.bfloat16)
+        acc_ref[...] = jnp.zeros_like(acc_ref)
+
+    grad_pre = (dot_nt(left_ref[...], outer_ref[...]) * slope_ref[...].astype(jnp.float32)).astype(jnp.bfloat16)
+    pre_ref[...] = grad_pre
+    acc_ref[...] += dot_nt(grad_pre, inner_ref[...])
+
+    @pl.when(i == pl.num_programs(0) - 1)
+    def _():
+        grad_in, grad_gain = norm_back(acc_ref[...], value_ref[...], gain_ref[...])
+        total = grad_ref[...] + grad_in
+        out_ref[...] = total
+        low_ref[...] = total.astype(jnp.bfloat16)
+        gain_grad_ref[...] = grad_gain
+
+
+def mlp_back(grad_out, attended, gain, w_outer, w_inner, slope):
+    rows, width = grad_out.shape
+    wide = w_outer.shape[0]
+    tile = 512
+    whole = pl.BlockSpec((rows, width), lambda i: (0, 0))
+    line = pl.BlockSpec((1, width), lambda i: (0, 0))
+    return pl.pallas_call(
+        mlp_back_kernel,
+        grid=(wide // tile,),
+        in_specs=[
+            whole,
+            whole,
+            line,
+            pl.BlockSpec((tile, width), lambda i: (i, 0)),
+            pl.BlockSpec((width, tile), lambda i: (0, i)),
+            pl.BlockSpec((rows, tile), lambda i: (0, i)),
+        ],
+        out_specs=[pl.BlockSpec((rows, tile), lambda i: (0, i)), whole, whole, line],
+        out_shape=[
+            jax.ShapeDtypeStruct((rows, wide), jnp.bfloat16),
+            jax.ShapeDtypeStruct((rows, width), jnp.float32),
+            jax.ShapeDtypeStruct((rows, width), jnp.bfloat16),
+            jax.ShapeDtypeStruct((1, width), jnp.float32),
+        ],
+        scratch_shapes=[pltpu.VMEM((rows, width), jnp.float32), pltpu.VMEM((rows, width), jnp.bfloat16)],
+        compiler_params=pltpu.CompilerParams(vmem_limit_bytes=48 << 20),
+        cost_estimate=BRIEF,
+        name="mlp_back",
+    )(grad_out, attended, gain, w_outer, w_inner, slope)
+
+
+def project_back_kernel(add_ref, value_ref, gain_ref, q_ref, k_ref, v_ref, w_ref, out_ref, gain_grad_ref, acc_ref):
+    i = pl.program_id(0)
+    for j, r in enumerate((q_ref, k_ref, v_ref)):
+
+        @pl.when(i == j)
+        def _(j=j, r=r):
+            part = dot_nt(r[...], w_ref[...])
+            acc_ref[...] = part if j == 0 else acc_ref[...] + part
+
+    @pl.when(i == 2)
+    def _():
+        grad_in, grad_gain = norm_back(acc_ref[...], value_ref[...], gain_ref[...])
+        out_ref[...] = add_ref[...] + grad_in
+        gain_grad_ref[...] = grad_gain
+
+
+def project_back(grad_attended, x, gain, grad_query, grad_k, grad_v, w):
+    rows, width = x.shape
+    whole = pl.BlockSpec((rows, width), lambda i: (0, 0))
+    line = pl.BlockSpec((1, width), lambda i: (0, 0))
+    return pl.pallas_call(
+        project_back_kernel,
+        grid=(3,),
+        in_specs=[whole, whole, line, whole, whole, whole, pl.BlockSpec((width, width), lambda i: (0, i))],
+        out_specs=[whole, line],
+        out_shape=[jax.ShapeDtypeStruct((rows, width), jnp.float32), jax.ShapeDtypeStruct((1, width), jnp.float32)],
+        scratch_shapes=[pltpu.VMEM((rows, width), jnp.float32)],
+        compiler_params=pltpu.CompilerParams(vmem_limit_bytes=48 << 20),
+        cost_estimate=BRIEF,
+        name="project_back",
+    )(grad_attended, x, gain, grad_query, grad_k, grad_v, w)
 
 
 def gelu_pair(pre):
@@ -392,7 +477,7 @@
         ),
         out_shape=jax.ShapeDtypeStruct((at * 4 * depth, width), quads[0][0].dtype),
         compiler_params=pltpu.CompilerParams(vmem_limit_bytes=48 << 20),
-        cost_estimate=pl.CostEstimate(flops=0, bytes_accessed=16 * at * depth * width, transcendentals=0),
+        cost_estimate=BRIEF,
         name="assemble",
     )(table, *[r for q in quads for r in q])
 
@@ -422,44 +507,41 @@
     def send(self, piece, name):
         return Held(self.plan.exchange(piece.value, name))
 
+    def send_in_plane(self):
+        if self.pairs:
+            self.by_x, self.by_y, self.near_twin = [self.send(self.near, n) for n in ("s", "y", "core")]
+
     def a(self, main, following=None):
-        held = [self.near] + ([following.shard] if following else [])
-        main = tie(main, *held)
+        main = tie(main, self.near, *([following.shard] if following else []))
         if following:
             following.start()
-        if self.pairs:
-            self.by_x, self.by_y, self.near_twin = [self.send(self.near, n) for n in ("s", "y", "core")]
+        self.send_in_plane()
         return main
 
     def b(self, main):
-        if self.pairs:
-            main = tie(main, self.by_x, self.by_y, self.near_twin)
-            half = self.by_x.value.shape[0] // 2
-            self.low = Held(self.plan.exchange(self.by_y.value[:half], "s"))
-            self.high = Held(self.plan.exchange(self.by_x.value[half:], "y"))
-            self.x_twin, self.y_twin = self.send(self.by_x, "core"), self.send(self.by_y, "core")
-        return main
+        if not self.pairs:
+            return main
+        main = tie(main, self.by_x, self.by_y, self.near_twin)
+        half = self.by_x.value.shape[0] // 2
+        self.low = Held(self.plan.exchange(self.by_y.value[:half], "s"))
+        self.high = Held(self.plan.exchange(self.by_x.value[half:], "y"))
+        self.x_twin, self.y_twin = self.send(self.by_x, "core"), self.send(self.by_y, "core")
+        return tie(main, self.x_twin, self.y_twin)
 
     def c(self, main):
-        return tie(main, self.x_twin, self.y_twin) if self.pairs else main
-
-    def d(self, main):
-        if self.pairs:
-            main = tie(main, self.low, self.high)
-            self.low_twin, self.high_twin = self.send(self.low, "core"), self.send(self.high, "core")
-        return main
-
-    def e(self, main):
         if not self.pairs:
             return main, self.near.value
-        main = tie(main, self.low_twin, self.high_twin)
         plan = self.plan
+        main = tie(main, self.low, self.high)
+        twins = [self.send(p, "core") for p in (self.low, self.high)]
+        main = tie(main, *twins)
+        low_twin, high_twin = [t.value for t in twins]
         half = self.low.value.shape[0]
         by_y, y_twin = self.by_y.value, self.y_twin.value
         quads = [
             (self.near.value, self.near_twin.value, self.by_x.value, self.x_twin.value),
-            (by_y[:half], y_twin[:half], self.low.value, self.low_twin.value),
-            (by_y[half:], y_twin[half:], self.high.value, self.high_twin.value),
+            (by_y[:half], y_twin[:half], self.low.value, low_twin),
+            (by_y[half:], y_twin[half:], self.high.value, high_twin),
         ]
         z = jnp.arange(plan.nz, dtype=jnp.int32)
         order = jnp.concatenate([z * 2 + plan.y, z * 2 + (1 - plan.y)])
@@ -485,7 +567,7 @@
         self.part = None
 
     def one(self):
-        self.part = Held(self.product(self.rows // 2, self.rows))
+        self.part = Held(self.product(self.rows // 2, self.rows, None))
         return self.part
 
     def send_one(self):
@@ -495,9 +577,9 @@
         half = self.rows // 2
         if self.pairs:
             quarter = half // 2
-            self.part = Held(add_low(self.product(quarter, half), self.other.value[quarter:]))
+            self.part = Held(self.product(quarter, half, (self.other.value, quarter)))
         else:
-            self.part = Held(add_low(self.product(0, half), self.other.value))
+            self.part = Held(self.product(0, half, (self.other.value, 0)))
         return self.part
 
     def send_two(self):
@@ -510,7 +592,7 @@
     def near(self):
         if self.pairs:
             quarter = self.rows // 4
-            self.close_by = Held(add_low(self.product(0, quarter), self.other.value[:quarter]))
+            self.close_by = Held(self.product(0, quarter, (self.other.value, 0)))
             return self.close_by
         return self.far
 
@@ -540,29 +622,67 @@
         return self.piece
 
 
-def outer_grad_kernel(count, table_ref, *refs):
-    left = jnp.concatenate([r[...] for r in refs[:count]], axis=1)
-    refs[-1][...] = dot_tn(left, refs[count][...]).astype(refs[-1].dtype)
-
-
-def outer_grad(hidden, grad_low, table, start, stop):
-    rows, width = grad_low.shape
-    count = 4 if (stop - start) % 4 == 0 else 1
-    steps = (stop - start) // count
-    specs = [pl.BlockSpec((rows, TILE), functools.partial(lambda j, i, t: (0, t[start + i * count + j]), j)) for j in range(count)]
+def grad_kernel(lefts, starts, with_add, table_ref, *refs):
+    j = pl.program_id(1)
+    out = refs[-1]
+    at = 0
+    for (start, count), number in zip(starts, lefts):
+        left_refs, right = refs[at:at + number], refs[at + number]
+        at += number + 1
+
+        @pl.when(jnp.logical_and(j >= start, j < start + count))
+        def _(left_refs=left_refs, right=right):
+            left = left_refs[0][...] if len(left_refs) == 1 else jnp.concatenate([r[...] for r in left_refs], axis=1)
+            total = dot_tn(left, right[...])
+            if with_add:
+                total = total + refs[-2][...].astype(jnp.float32)
+            out[...] = total.astype(out.dtype)
+
+
+def grad_rows(pairs, start, stop, add=None, table=None):
+    depth = pairs[0][0].shape[0]
+    tile_n = 1024
+    count = stop - start
+    tile_m = min(512, count)
+    specs, operands, lefts, starts, at = [], [], [], [], 0
+
+    def column_map(first, begin, n):
+        return lambda i, j, t: (0, first + jnp.clip(j - begin, 0, n - 1))
+
+    for left, right, first, n in pairs:
+        if table is None:
+            block = start // tile_m
+            specs.append(pl.BlockSpec((depth, tile_m), lambda i, j, t, block=block: (0, block + i)))
+            operands.append(left)
+            lefts.append(1)
+        else:
+            per = tile_m // TILE
+            for k in range(per):
+                specs.append(pl.BlockSpec((depth, TILE), lambda i, j, t, k=k, per=per: (0, t[start // TILE + i * per + k])))
+                operands.append(left)
+            lefts.append(per)
+        specs.append(pl.BlockSpec((depth, tile_n), column_map(first, at, n)))
+        operands.append(right)
+        starts.append((at, n))
+        at += n
+    if add is not None:
+        base = add[1] // tile_m
+        specs.append(pl.BlockSpec((tile_m, tile_n), lambda i, j, t: (base + i, j)))
+        operands.append(add[0])
+    width = at * tile_n
     return pl.pallas_call(
-        functools.partial(outer_grad_kernel, count),
+        functools.partial(grad_kernel, lefts, starts, add is not None),
         grid_spec=pltpu.PrefetchScalarGridSpec(
             num_scalar_prefetch=1,
-            grid=(steps,),
-            in_specs=specs + [pl.BlockSpec((rows, width), lambda i, t: (0, 0))],
-            out_specs=pl.BlockSpec((count * TILE, width), lambda i, t: (i, 0)),
+            grid=(count // tile_m, at),
+            in_specs=specs,
+            out_specs=pl.BlockSpec((tile_m, tile_n), lambda i, j, t: (i, j)),
         ),
-        out_shape=jax.ShapeDtypeStruct(((stop - start) * TILE, width), jnp.bfloat16),
+        out_shape=jax.ShapeDtypeStruct((count, width), jnp.bfloat16),
         compiler_params=pltpu.CompilerParams(vmem_limit_bytes=32 << 20),
-        cost_estimate=pl.CostEstimate(flops=2 * rows * width * (stop - start) * TILE, bytes_accessed=2 * (stop - start) * TILE * (rows + width) + 2 * rows * width, transcendentals=0),
-        name="outer_grad",
-    )(table, *([hidden] * count), grad_low)
+        cost_estimate=BRIEF,
+        name="grad_rows",
+    )(jnp.zeros((1,), jnp.int32) if table is None else table, *operands)
 
 
 def project(x, gain, w_qkv):
@@ -587,86 +707,85 @@
         wide = hidden.shape[1]
         blocks = table[orders[1]]
 
-        def outer_rows(a, b, hidden=hidden, grad_low=grad_low, blocks=blocks, wide=wide):
+        def outer_rows(a, b, add, hidden=hidden, grad_low=grad_low, blocks=blocks, wide=wide):
             if wide // blocks.shape[0] == TILE:
-                return outer_grad(hidden, grad_low, blocks, a // TILE, b // TILE)
-            return plan.take_blocks(matmul_left(hidden, grad_low).astype(low), blocks)[a:b]
-
-        def rows_of(left, right):
-            return lambda a, b: matmul_left(left[:, a:b], right).astype(low)
+                return grad_rows([(hidden, grad_low, 0, 1)], a, b, add, blocks)
+            rows = plan.take_blocks(matmul_left(hidden, grad_low).astype(low), blocks)[a:b]
+            return rows if add is None else add_low(rows, add[0][add[1]:add[1] + b - a])
+
+        def rows_of(*pairs):
+            return lambda a, b, add: grad_rows(pairs, a, b, add)
 
         outer = Chain(plan, outer_rows, orders[1], wide)
-        late = [previous.outer.side, previous.inner.side] if previous else []
+        leaving = Held(output_half)
+        late = [previous.outer.side, previous.inner.side] if previous else [leaving]
         grad_out = tie(grad_out, outer.one(), *late)
         outer.send_one()
-        grad_pre = (matmul_back(grad_out.astype(low), w_outer) * slope.astype(f32)).astype(low)
-        grad_pre = tie(grad_pre, outer.other)
+        if not previous:
+            arrived = Held(plan.exchange(leaving.value, "s"))
+        grad_pre, grad_attended, attn_low, grad_mlp_gain = mlp_back(grad_out, attended, mlp_gain, w_outer, w_inner, slope)
+        late = [previous.qk.far, previous.ov.far] if previous else [arrived]
+        grad_pre = tie(grad_pre, outer.other, *late)
         left_m = matmul_rows(normed_mlp, perms[orders[0]]).astype(low)
-        inner = Chain(plan, rows_of(left_m, grad_pre), orders[0], width)
-        late = [previous.outer.close(), previous.inner.close()] if previous else []
+        inner = Chain(plan, rows_of((left_m, grad_pre, 0, wide // 1024)), orders[0], width)
+        late = []
+        if previous:
+            late = [part for c in (previous.qk, previous.ov) for part in (c.near(), c.three())]
+            late += [previous.outer.close(), previous.inner.close()]
         grad_pre = tie(grad_pre, outer.two(), inner.one(), *late)
         outer.send_two()
         inner.send_one()
         if previous:
-            previous.sum_mlp(plan)
-        grad_normed_mlp = matmul_back(grad_pre, w_inner)
-        grad_branch, grad_mlp_gain = norm_pull(grad_normed_mlp, attended, mlp_gain)
-        grad_attended = grad_out + grad_branch
-        late = [previous.qk.far, previous.ov.far] if previous else []
-        grad_attended = tie(grad_attended, inner.other, *late)
-        late = [part for c in (previous.qk, previous.ov) for part in (c.near(), c.three())] if previous else []
-        leaving = Held(output_half)
-        grad_attended = tie(grad_attended, inner.two(), *late, *([] if previous else [leaving]))
-        inner.send_two()
-        if not previous:
-            arrived = Held(plan.exchange(leaving.value, "s"))
-        if previous:
             previous.qk.send_three()
             previous.ov.send_three()
-        attn_low = grad_attended.astype(low)
+            previous.sum_mlp(plan)
+        late = [previous.qk.side, previous.ov.side] if previous else []
+        attn_low = tie(attn_low, inner.other, *late)
+        late = [previous.qk.close(), previous.ov.close()] if previous else []
+        attn_low = tie(attn_low, inner.two(), *late)
+        inner.send_two()
+        if previous:
+            previous.sum_attn(plan)
         grad_context = matmul_back(attn_low, w_output).astype(low)
+        ready = [outer.near(), inner.near()]
         left_c = matmul_rows(context, perms[orders[3]]).astype(low)
         left_n = {o: matmul_rows(normed, perms[o]).astype(low) for o in orders[2:]}
+        left_c, n_q, n_v = Held(left_c), Held(left_n[orders[2]]), Held(left_n[orders[3]])
+        grad_context = tie(grad_context, *ready, left_c, n_q, n_v)
+        left_c, left_n = left_c.value, {orders[2]: n_q.value, orders[3]: n_v.value}
         grad_query, dk, dv, diag = attn_bwd(pos, queries, grad_context, context, log_total, keys, values, bias, blk, 0, 1)
-        kv_parts = [jnp.concatenate([p, r], axis=1) for p, r in zip(dk, dv)]
-        late = [previous.qk.side, previous.ov.side, previous.inner_sum, previous.outer_sum] if previous else [arrived]
-        last_part = tie(kv_parts[-1], outer.far, inner.far, *late)
-        grad_kv = plan.reduce_keys(kv_parts[:-1] + [last_part]).astype(low)
-        late = [previous.qk.close(), previous.ov.close()] if previous else []
-        grad_kv = tie(grad_kv, outer.near(), outer.three(), inner.near(), inner.three(), *late)
+        late = [previous.mlp_sum] if previous else []
+        last = tie(dv[-1], outer.far, inner.far, *late)
+        grad_k = plan.reduce_keys(dk).astype(low)
+        grad_v = plan.reduce_keys(list(dv[:-1]) + [last]).astype(low)
+        grad_v = tie(grad_v, outer.three(), inner.three())
         outer.send_three()
         inner.send_three()
-        if previous:
-            previous.sum_attn(plan)
-        grad_qk = jnp.concatenate([grad_query, grad_kv[:, :width]], axis=1)
-        grad_v = grad_kv[:, width:]
-
-        def ov_rows(a, b, left_c=left_c, left_n=left_n[orders[3]], attn_low=attn_low, grad_v=grad_v):
-            return jnp.concatenate([matmul_left(left_c[:, a:b], attn_low).astype(low), matmul_left(left_n[:, a:b], grad_v).astype(low)], axis=1)
-
-        qk = Chain(plan, rows_of(left_n[orders[2]], grad_qk), orders[2], width)
-        ov = Chain(plan, ov_rows, orders[3], width)
-        grad_qk = tie(grad_qk, qk.one(), ov.one())
+        tiles = width // 1024
+        qk = Chain(plan, rows_of((left_n[orders[2]], grad_query, 0, tiles), (left_n[orders[2]], grad_k, 0, tiles)), orders[2], width)
+        ov = Chain(plan, rows_of((left_c, attn_low, 0, tiles), (left_n[orders[3]], grad_v, 0, tiles)), orders[3], width)
+        late = [previous.attn_sum] if previous else []
+        grad_v = tie(grad_v, qk.one(), ov.one(), *late)
         qk.send_one()
         ov.send_one()
-        grad_normed = matmul_back(grad_qk, w_qkv[:, :2 * width]) + matmul_back(grad_v, w_qkv[:, 2 * width:])
-        grad_flat, grad_attn_gain = norm_pull(grad_normed, x, attn_gain)
-        grad_out = tie(grad_attended + grad_flat, qk.other, ov.other)
+        grad_out, grad_attn_gain = project_back(grad_attended, x, attn_gain, grad_query, grad_k, grad_v, w_qkv)
+        grad_out = tie(grad_out, qk.other, ov.other)
         grad_out = tie(grad_out, qk.two(), ov.two())
         qk.send_two()
         ov.send_two()
         previous = LayerSums(outer, inner, qk, ov, grad_attn_gain, grad_mlp_gain, width)
         results.append(previous)
         diags.append(diag)
-    grad_out = tie(grad_out, outer.side, inner.side, results[0].attn_sum)
-    grad_out = tie(grad_out, outer.close(), inner.close(), qk.near(), ov.near())
+    grad_out = tie(grad_out, outer.side, inner.side)
+    outer.close()
+    inner.close()
     previous.sum_mlp(plan)
-    grad_out = tie(grad_out, qk.far, ov.far)
+    grad_out = tie(grad_out, qk.far, ov.far, qk.near(), ov.near())
     grad_out = tie(grad_out, qk.three(), ov.three())
     qk.send_three()
     ov.send_three()
     qk.close()
-    ov.close()
+    qk.piece.value = tie(qk.piece.value, ov.close(), previous.mlp_sum)
     previous.sum_attn(plan)
     return grad_out, results, diags, arrived.value
 
@@ -677,8 +796,11 @@
         self.attn_gain, self.mlp_gain, self.width = grad_attn_gain, grad_mlp_gain, width
 
     def sum_mlp(self, plan):
-        self.inner_sum = Held(plan.sum_z(self.inner.piece.value))
-        self.outer_sum = Held(plan.sum_z(self.outer.piece.value))
+        w = self.width
+        inner, outer = self.inner.piece.value, self.outer.piece.value
+        self.runs, self.depth = inner.shape[2] // w, inner.shape[1]
+        stacked = [inner[:, :, i * w:(i + 1) * w] for i in range(self.runs)]
+        self.mlp_sum = Held(plan.sum_z(jnp.concatenate(stacked + [outer], axis=1)))
 
     def sum_attn(self, plan):
         self.attn_sum = Held(plan.sum_z(jnp.concatenate([c.piece.value for c in (self.qk, self.ov)], axis=2)))
@@ -687,7 +809,10 @@
         w = self.width
         f32 = jnp.float32
         query, key, output, value = [self.attn_sum.value[:, i * w:(i + 1) * w].astype(f32) for i in range(4)]
-        return [self.attn_gain, query, key, value, output, self.mlp_gain, self.inner_sum.value.astype(f32), self.outer_sum.value.astype(f32)]
+        both = self.mlp_sum.value.astype(f32)
+        d = self.depth
+        inner = jnp.concatenate([both[i * d:(i + 1) * d] for i in range(self.runs)], axis=1)
+        return [self.attn_gain, query, key, value, output, self.mlp_gain, inner, both[self.runs * d:]]
 
 
 def body(sizes, inputs, cotangent, lengths, bucket_ids, *params):
@@ -723,66 +848,63 @@
     inner_1.start()
     x = attn_1.a(x, outer_1)
     x = attn_1.b(x)
-    x = attn_1.c(x)
     x = inner_1.a(x, attn_2)
-    x = attn_1.d(x)
-    x, first = attn_1.e(x)
-    smalls = first[:, 4 * width:].astype(f32)
-    gain = smalls[:, :4].T
-    whole_table = smalls[:, 4].reshape(-1, rows)[:, :bias_table.shape[0]].reshape(-1)
+    x, first = attn_1.c(x)
+    picks = jnp.eye(8, TILE, dtype=low)
+    smalls = matmul_back(picks, first[:, 4 * width:])
+    gain = smalls[:4]
+    whole_table = smalls[4].reshape(-1, rows)[:, :bias_table.shape[0]].reshape(-1)
     heads = width // DK
     buckets = whole_table.shape[0] // heads
     reversed_ids = jnp.concatenate([jnp.full((1,), -1, jnp.int32), bucket_ids[::-1]])
     indicator = (reversed_ids[None, :] == jnp.arange(buckets, dtype=jnp.int32)[:, None]).astype(low)
-    bias = Held(toeplitz_tiles(matmul_rows(whole_table.reshape(heads, buckets).astype(low), indicator)))
-    x = tie(x, bias)
-    bias = bias.value
+    vector = Held(matmul_rows(whole_table.reshape(heads, buckets).astype(low), indicator))
     x_one = x.astype(f32)
     normed_one, qkv = project(x_one, gain[0:1], first[:, :3 * width])
     qkv = inner_1.b(qkv)
+    qkv = outer_1.a(qkv, inner_2)
     kv = plan.gather_keys(qkv[:, width:])
-    qkv = inner_1.c(qkv)
-    qkv = outer_1.a(qkv, inner_2)
+    qkv = tie(qkv, vector)
+    bias = Held(toeplitz_tiles(vector.value))
+    qkv = tie(qkv, bias)
+    bias = bias.value
     queries_one = qkv[:, :width]
     keys_one, values_one = [p[:, :width] for p in kv], [p[:, width:] for p in kv]
     context_one, log_one = attn_fwd(pos, queries_one, keys_one, values_one, bias, blk)
-    context_one = inner_1.d(context_one)
-    context_one, w_inner_one = inner_1.e(context_one)
+    context_one, w_inner_one = inner_1.c(context_one)
+    context_one = outer_1.b(context_one)
+    context_one = attn_2.a(context_one, outer_2)
     attended_one = x_one + matmul_rows(context_one, first[:, 3 * width:4 * width])
-    attended_one = outer_1.b(attended_one)
     normed_mlp_one, hidden_one, slope_one = widen(attended_one, gain[1:2], w_inner_one)
-    hidden_one = outer_1.c(hidden_one)
-    hidden_one = attn_2.a(hidden_one, outer_2)
-    hidden_one = outer_1.d(hidden_one)
-    hidden_one, w_outer_one = outer_1.e(hidden_one)
+    slope_one = Held(slope_one)
+    hidden_one = tie(hidden_one, slope_one)
+    slope_one = slope_one.value
+    hidden_one, w_outer_one = outer_1.c(hidden_one)
+    hidden_one = attn_2.b(hidden_one)
+    hidden_one = inner_2.a(hidden_one)
     x_two = attended_one + matmul_rows(hidden_one, w_outer_one)
-    x_two = attn_2.b(x_two)
-    x_two = attn_2.c(x_two)
-    x_two = inner_2.a(x_two)
-    x_two = attn_2.d(x_two)
-    x_two, third = attn_2.e(x_two)
+    x_two, third = attn_2.c(x_two)
     normed_two, qkv = project(x_two, gain[2:3], third[:, :3 * width])
     qkv = inner_2.b(qkv)
+    qkv = outer_2.a(qkv)
     kv = plan.gather_keys(qkv[:, width:])
-    qkv = inner_2.c(qkv)
-    qkv = outer_2.a(qkv)
     queries_two = qkv[:, :width]
     keys_two, values_two = [p[:, :width] for p in kv], [p[:, width:] for p in kv]
     context_two, log_two = attn_fwd(pos, queries_two, keys_two, values_two, bias, blk)
-    context_two = inner_2.d(context_two)
-    context_two, w_inner_two = inner_2.e(context_two)
+    context_two, w_inner_two = inner_2.c(context_two)
+    context_two = outer_2.b(context_two)
     attended_two = x_two + matmul_rows(context_two, third[:, 3 * width:])
-    attended_two = outer_2.b(attended_two)
     normed_mlp_two, hidden_two, slope_two = widen(attended_two, gain[3:4], w_inner_two)
-    hidden_two = outer_2.c(hidden_two)
-    hidden_two = outer_2.d(hidden_two)
-    hidden_two, w_outer_two = outer_2.e(hidden_two)
+    slope_two = Held(slope_two)
+    hidden_two = tie(hidden_two, slope_two)
+    slope_two = slope_two.value
+    hidden_two, w_outer_two = outer_2.c(hidden_two)
     final = attended_two + matmul_rows(hidden_two, w_outer_two)
     output_rows = (final * row_valid).astype(low)
     grad_out = cotangent.astype(f32) * row_valid
 
-    weights_one = (gain[0:1], first[:, :3 * width], first[:, 3 * width:4 * width], gain[1:2], w_inner_one, w_outer_one)
-    weights_two = (gain[2:3], third[:, :3 * width], third[:, 3 * width:], gain[3:4], w_inner_two, w_outer_two)
+    weights_one = (gain[0:1], first, first[:, 3 * width:4 * width], gain[1:2], w_inner_one, w_outer_one)
+    weights_two = (gain[2:3], third, third[:, 3 * width:], gain[3:4], w_inner_two, w_outer_two)
     saved_one = (x_one, normed_one, queries_one, keys_one, values_one, context_one, log_one, attended_one, normed_mlp_one, hidden_one, slope_one)
     saved_two = (x_two, normed_two, queries_two, keys_two, values_two, context_two, log_two, attended_two, normed_mlp_two, hidden_two, slope_two)
 
@@ -800,7 +922,7 @@
     input_grad = plan.from_sequences(grad_state.astype(low))
 
     grad_table = lax.dot_general(diags[0] + diags[1], indicator.astype(f32), (((1,), (1,)), ((), ())), precision=HIGH_PRECISION)
-    vectors = jnp.concatenate([grads_one[0], grads_one[5], grads_two[0], grads_two[5], grad_table.reshape(-1)])
+    vectors = jnp.concatenate([grads_one[0][0], grads_one[5][0], grads_two[0][0], grads_two[5][0], grad_table.reshape(-1)])
     held = Held(vectors)
     grad_state = tie(grad_state, held)
     vectors = plan.sum_vector(held.value)

time: 815 us -> 778 us (0.955)
  matrix products: 196 us -> 96.2 us
  Pallas kernels: 188 us -> 284 us
  other arithmetic: 88 us -> 57.7 us
  waiting for transfers between devices: 194 us -> 167 us
  local copies, waits for them, and re-layouts: 61.8 us -> 84.7 us
    pallas_call x6 -> x28, Pallas kernels: 18.2 us -> 117 us  [the longest x24 66.1 us: grad_rows(): pl.pallas_call(functools.partial(grad_kernel, lefts, starts, add is not N...]
    dot_general x10 -> x3, matrix products: 69.1 us -> 10.4 us  [matmul_back(): lax.dot_general(left, right, (((1,), (1,)), ((), ())), preferred_element_...]
    dot_general x24 -> x0, matrix products: 53.9 us -> none  [matmul_left(): lax.dot_general(left, right, (((0,), (0,)), ((), ())), preferred_element_...]
    ppermute x86 -> x88, waiting for transfers between devices: 158 us -> 125 us  [exchange(): return lax.ppermute(piece, name, SWAP)]
    unnamed x288 -> x316, local copies, waits for them, and re-layouts: 14.8 us -> 37 us
    convert_element_type x20 -> x16, other arithmetic: 51.2 us -> 33.5 us  [add_low(): return total.astype(jnp.bfloat16)]
    dot_general x17, matrix products: 73.2 us -> 85.6 us  [matmul_rows(): return jnp.dot(left, right, preferred_element_type=jnp.float32)]
    ppermute x5, waiting for transfers between devices: 4.56 us -> 13.7 us  [sum_vector(): lax.ppermute(vector, name, [(i, i ^ step) for i in range(size)])]
  transfers between devices with their start and end apart: 103 -> 103, of which waited for: 36 -> 50; matrix products, arithmetic and copies ran while one was open for 36% -> 23% of each run, Pallas kernels for 22% -> 33%
where the time goes in v3:
time: 778 us; the launch traced here: 767 us
  Pallas kernels  284 us (37%)
  waiting for transfers between devices  167 us (21%)
  matrix products  96.2 us (12%)
  local copies, waits for them, and re-layouts  84.7 us (11%)
  starting transfers between devices  60.9 us (8%)
  other arithmetic  57.7 us (7%)
  between operations  16.6 us (2%)
    ppermute x88, waiting for transfers between devices, exchange(): return lax.ppermute(piece, name, SWAP)  125 us
    dot_general x17, matrix products, matmul_rows(): return jnp.dot(left, right, preferred_element_type=jnp.float32)  85.6 us
    pallas_call x2, Pallas kernels, attn_bwd(): pl.pallas_call(functools.partial(attn_bwd_kernel, parts, chunk, blk), gri...  71.1 us
    pallas_call x24, Pallas kernels, grad_rows(): pl.pallas_call(functools.partial(grad_kernel, lefts, starts, add is not N...  66.1 us
    ppermute x88, starting transfers between devices, exchange(): return lax.ppermute(piece, name, SWAP)  59 us
    pallas_call x6, Pallas kernels, assemble(): pl.pallas_call(functools.partial(assemble_kernel, steps, depth), grid_spe...  45.5 us
    pallas_call x2, Pallas kernels, attn_fwd(): pl.pallas_call(functools.partial(attn_fwd_kernel, parts, chunk, blk), gri...  39.2 us
    unnamed x316, local copies, waits for them, and re-layouts  37 us
  transfers between devices with their start and end apart: 103, of which 50 were waited for; matrix products, arithmetic and copies ran while one was open for 23% of the time, Pallas kernels for 33%

profile of v3, /device:TPU:0, one launch (start us, length us, event | category | flops | bytes accessed | tf_op | source)
XLA Modules:
  0.0 766.8 jit_solution(13210026161809507084)
XLA Ops:
  17.3 11.9 %collective-permute-done = bf16[256,1024]{1,0:T(8,128)(2,1)S(1)} collective-permute-done((bf16[256,1024]{1,0:T(8,128)(2,1)S(1)}, bf16[256,1024]{1,0:T(8,128)(2,1)S(1)}, u32[]{:S(2)}, u32[]{:S(2)}) %collective-permute-start) | collective-permute-done | bytes 524320 | tf_op jit(solution)/shard_map/ppermute | solution.py:395
  30.2 14.0 %all-gather.7.cloned.1.call-done.refs_0_ = bf16[128,4224]{1,0:T(8,128)(2,1)} async-done(((bf16[32,4224]{1,0:T(8,128)(2,1)}), bf16[128,4224]{1,0:T(8,128)(2,1)}) %all-gather.7.cloned.1.call-update) | async-done | bytes 1081360 | tf_op jit(solution)/shard_map/all_gather | solution.py:505
  47.3 22.7 %collective-permute-done.1.refs_2_ = bf16[128,4224]{1,0:T(8,128)(2,1)} collective-permute-done((bf16[128,4224]{1,0:T(8,128)(2,1)}, bf16[128,4224]{1,0:T(8,128)(2,1)}, u32[]{:S(2)}, u32[]{:S(2)}) %collective-permute-start.1) | collective-permute-done | bytes 1081376 | tf_op jit(solution)/shard_map/ppermute | solution.py:395
  80.4 10.0 %collective-permute-done.6.refs_6_ = bf16[64,4224]{1,0:T(8,128)(2,1)S(1)} collective-permute-done((bf16[64,4224]{1,0:T(8,128)(2,1)S(1)}, bf16[64,4224]{1,0:T(8,128)(2,1)S(1)}, u32[]{:S(2)}, u32[]{:S(2)}) %collective-permute-start.6) | collective-permute-done | bytes 540704 | tf_op jit(solution)/shard_map/ppermute | solution.py:395
  102.8 7.7 %fusion.20 = bf16[512,3072]{1,0:T(8,128)(2,1)} fusion(bf16[1024,4224]{1,0:T(8,128)(2,1)} %assemble.6.w_ref, bf16[512,1024]{1,0:T(8,128)(2,1)S(1)} %copy-done.101, f32[1024]{0:T(1024)S(1)} %bitcast.69, f32[512]{0:T(512)S(1)} %add_rsqrt_fusion.3), kind=kOutput, calls=%fused_computation.48 | convolution fusion | flops 3224895488 | bytes 10491904 | tf_op jit(solution)/shard_map/dot_general | solution.py:239
  131.0 10.9 %toeplitz.1.refs_4_ = bf16[16,15,128,128]{3,2,1,0:T(8,128)(2,1)} custom-call(f32[16,1,2048]{2,1,0:T(1,128)} %reshape.119.u_ref), custom_call_target="tpu_custom_call" | custom-call | flops 1024 | bytes 1024 | tf_op jit(solution)/shard_map/toeplitz/pallas_call | solution.py:29
  148.8 19.8 %attn_fwd.2 = (bf16[512,1024]{1,0:T(8,128)(2,1)S(1)}, f32[8,2,512]{2,1,0:T(2,128)S(1)}) custom-call(s32[7]{0:T(128)S(1)} %stack.74.pos_ref, bf16[512,1024]{1,0:T(8,128)(2,1)S(1)} %slice.378.q_ref, bf16[512,1024]{1,0:T(8,128)(2,1)S(1)} %get-tuple-element.505.refs_0_, bf16[512,1024]{1,0:T(8,128)(2,1)S(1)} %get-tuple-element.509.refs_1_, ...), custom_call_target="tpu_custom_call" | custom-call | flops 1024 | bytes 1024 | tf_op jit(solution)/shard_map/attn_fwd/pallas_call | solution.py:115
  171.6 8.1 %assemble.7.inner_ref = bf16[1024,4096]{1,0:T(8,128)(2,1)} custom-call(s32[10]{0:T(128)S(1)} %pad_add_fusion.1.table_ref, bf16[128,4096]{1,0:T(8,128)(2,1)S(1)} %copy-done.82, bf16[128,4096]{1,0:T(8,128)(2,1)} %copy-done.118, bf16[128,4096]{1,0:T(8,128)(2,1)} %copy-done.105, bf16[128,4096]{1,0:T(8,128)(2,1)} %copy-done.122, ...), custom_call_target="tpu_custom_call" | custom-call | flops 1024 | bytes 1024 | tf_op jit(solution)/shard_map/assemble/pallas_call | solution.py:470
  192.0 15.4 %fusion.7 = (bf16[512,4096]{1,0:T(8,128)(2,1)}, bf16[512,4096]{1,0:T(8,128)(2,1)}) fusion(bf16[1024,4096]{1,0:T(8,128)(2,1)} %assemble.7.inner_ref, f32[512,1024]{1,0:T(8,128)S(1)} %get-tuple-element.569.value_ref, f32[1024]{0:T(1024)S(1)} %bitcast.72, f32[512]{0:T(512)S(1)} %add_rsqrt_fusion.2), kind=kOutput, calls=%fused_computation.15 | convolution fusion | flops 4334288896 | bytes 18880512 | tf_op jit(solution)/shard_map/dot_general | solution.py:239
  210.6 8.1 %assemble.8.outer_ref = bf16[4096,1024]{1,0:T(8,128)(2,1)} custom-call(s32[10]{0:T(128)S(1)} %pad_add_fusion.1.table_ref, bf16[512,1024]{1,0:T(8,128)(2,1)S(1)} %copy-done.78, bf16[512,1024]{1,0:T(8,128)(2,1)} %copy-done.121, bf16[512,1024]{1,0:T(8,128)(2,1)} %collective-permute-done.20.refs_2_, bf16[512,1024]{1,0:T(8,128)(2,1)} %collective-permute-done.23.refs_3_, ...), custom_call_target="tpu_custom_call" | custom-call | flops 1024 | bytes 1024 | tf_op jit(solution)/shard_map/assemble/pallas_call | solution.py:470
  230.1 9.7 %convolution_add_fusion.value_ref = f32[512,1024]{1,0:T(8,128)S(1)} fusion(f32[512,1024]{1,0:T(8,128)} %copy-done.113, bf16[512,4096]{1,0:T(8,128)(2,1)} %get-tuple-element.325.refs_0_.refs_1_.refs_2_.refs_3_, bf16[4096,1024]{1,0:T(8,128)(2,1)} %assemble.8.outer_ref), kind=kOutput, calls=%fused_computation.97 | convolution fusion | flops 4295491584 | bytes 16777216 | tf_op jit(solution)/shard_map/dot_general | solution.py:239
  252.7 7.9 %fusion.23 = bf16[512,3072]{1,0:T(8,128)(2,1)} fusion(bf16[512,1024]{1,0:T(8,128)(2,1)S(1)} %multiply_convert_fusion.4, bf16[1024,4096]{1,0:T(8,128)(2,1)} %assemble.9.w_ref), kind=kOutput, calls=%fused_computation.49 | convolution fusion | flops 3222798336 | bytes 10485760 | tf_op jit(solution)/shard_map/dot_general | solution.py:239
  277.2 19.5 %attn_fwd.3 = (bf16[512,1024]{1,0:T(8,128)(2,1)S(1)}, f32[8,2,512]{2,1,0:T(2,128)S(1)}) custom-call(s32[7]{0:T(128)S(1)} %stack.74.pos_ref, bf16[512,1024]{1,0:T(8,128)(2,1)S(1)} %get-tuple-element.503.q_ref, bf16[512,1024]{1,0:T(8,128)(2,1)S(1)} %get-tuple-element.502.refs_0_, bf16[512,1024]{1,0:T(8,128)(2,1)S(1)} %get-tuple-element.507.refs_1_, ...), custom_call_target="tpu_custom_call" | custom-call | flops 1024 | bytes 1024 | tf_op jit(solution)/shard_map/attn_fwd/pallas_call | solution.py:115
  320.5 11.4 %fusion.15 = (bf16[512,4096]{1,0:T(8,128)(2,1)}, bf16[512,4096]{1,0:T(8,128)(2,1)S(1)}) fusion(bf16[1024,4096]{1,0:T(8,128)(2,1)S(1)} %copy-done.99, f32[512,1024]{1,0:T(8,128)S(1)} %get-tuple-element.571.value_ref, f32[1024]{0:T(1024)S(1)} %bitcast.74, f32[512]{0:T(512)S(1)} %add_rsqrt_fusion), kind=kOutput, calls=%fused_computation.23 | convolution fusion | flops 4334288896 | bytes 18880512 | tf_op jit(solution)/shard_map/dot_general | solution.py:239
  348.4 7.9 %multiply_convert_fusion.2 = bf16[512,1024]{1,0:T(8,128)(2,1)S(1)} fusion(f32[512,1024]{1,0:T(8,128)S(1)} %get-tuple-element.571.value_ref, bf16[512,4096]{1,0:T(8,128)(2,1)S(1)} %get-tuple-element.372.refs_0_.refs_1_.refs_2_.refs_3_, bf16[4096,1024]{1,0:T(8,128)(2,1)} %assemble.11.outer_ref, f32[512]{0:T(512)S(1)} %fusion.71), kind=kOutput, calls=%fused_computation.78 | convolution fusion | flops 4296540160 | bytes 15730688 | tf_op jit(solution)/shard_map/dot_general | solution.py:239
  365.4 17.8 %mlp_back.2 = (bf16[512,4096]{1,0:T(8,128)(2,1)}, f32[512,1024]{1,0:T(8,128)S(1)}, bf16[512,1024]{1,0:T(8,128)(2,1)S(1)}, f32[1,1024]{1,0:T(1,128)S(1)}) custom-call(f32[512,1024]{1,0:T(8,128)S(1)} %copy-done.62, f32[512,1024]{1,0:T(8,128)} %copy-done.115, f32[1,1024]{1,0:T(1,128)S(1)} %get-tuple-element.560.gain_ref, ...), custom_call_target="tpu_custom_call" | custom-call | flops 1024 | bytes 1024 | tf_op jit(solution)/shard_map/mlp_back/pallas_call | solution.py:289
  415.8 35.4 %attn_bwd.2 = (bf16[512,1024]{1,0:T(8,128)(2,1)S(1)}, bf16[512,1024]{1,0:T(8,128)(2,1)S(1)}, bf16[512,1024]{1,0:T(8,128)(2,1)S(1)}, bf16[512,1024]{1,0:T(8,128)(...) custom-call(s32[7]{0:T(128)S(1)} %copy-done.96, bf16[512,1024]{1,0:T(8,128)(2,1)} %copy-done.26, ...), custom_call_target="tpu_custom_call" | custom-call | flops 1024 | bytes 1024 | tf_op jit(solution)/shard_map/attn_bwd/pallas_call | solution.py:218
  467.8 8.0 %project_back.2 = (f32[512,1024]{1,0:T(8,128)S(1)}, f32[1,1024]{1,0:T(1,128)S(1)}) custom-call(f32[512,1024]{1,0:T(8,128)} %copy-done.70, f32[512,1024]{1,0:T(8,128)} %copy-done.100, f32[1,1024]{1,0:T(1,128)S(1)} %copy-done.90, bf16[512,1024]{1,0:T(8,128)(2,1)S(1)} %get-tuple-element.390.refs_1_.q_ref, ...), custom_call_target="tpu_custom_call" | custom-call | flops 1024 | bytes 1024 | tf_op jit(solution)/shard_map/project_back/pallas_call | solution.py:334
  504.4 17.6 %mlp_back.3 = (bf16[512,4096]{1,0:T(8,128)(2,1)}, f32[512,1024]{1,0:T(8,128)S(1)}, bf16[512,1024]{1,0:T(8,128)(2,1)S(1)}, f32[1,1024]{1,0:T(1,128)S(1)}) custom-call(f32[512,1024]{1,0:T(8,128)S(1)} %get-tuple-element.416.grad_ref, f32[512,1024]{1,0:T(8,128)} %copy-done.113, f32[1,1024]{1,0:T(1,128)S(1)} %copy-done.94, bf16[4096,1024]{1,0:T(8,128)(2,1)} %assemble.8.outer_ref, ...), custom_call_target="tpu_custom_call" | custom-call | flops 1024 | bytes 1024 | tf_op jit(solution)/shard_map/mlp_back/pallas_call | solution.py:289
  549.8 7.5 collective-permute-done.73
  586.1 35.7 %attn_bwd.3 = (bf16[512,1024]{1,0:T(8,128)(2,1)S(1)}, bf16[512,1024]{1,0:T(8,128)(2,1)S(1)}, bf16[512,1024]{1,0:T(8,128)(2,1)}, bf16[512,1024]{1,0:T(8,128)(2,1)...) custom-call(s32[7]{0:T(128)S(1)} %copy-done.97, bf16[512,1024]{1,0:T(8,128)(2,1)} %copy-done.20, ...), custom_call_target="tpu_custom_call" | custom-call | flops 1024 | bytes 1024 | tf_op jit(solution)/shard_map/attn_bwd/pallas_call | solution.py:218
  643.0 7.9 %reduce-scatter.7.cloned.1.call-done = bf16[1,32,4096]{2,1,0:T(8,128)(2,1)} async-done(((bf16[4,32,4096]{2,1,0:T(8,128)(2,1)}), bf16[1,32,4096]{2,1,0:T(8,128)(2,1)}) %reduce-scatter.7.cloned.1.call-update) | async-done | bytes 262160 | tf_op jit(solution)/shard_map/reduce_scatter | solution.py:400
  658.4 7.6 project_back.3
  696.3 13.5 %collective-permute-done.83 = bf16[256,2048]{1,0:T(8,128)(2,1)} collective-permute-done((bf16[256,2048]{1,0:T(8,128)(2,1)}, bf16[256,2048]{1,0:T(8,128)(2,1)}, u32[]{:S(2)}, u32[]{:S(2)}) %collective-permute-start.83) | collective-permute-done | bytes 1048608 | tf_op jit(solution)/shard_map/ppermute | solution.py:395
  (677 shorter events, 414.2 us)
Async XLA Ops:
  7.2 37.1 %all-gather.7.cloned.1.call-start = ((), (), s32[]{:S(2)}) async-start(), calls=%async_computation.4 | async-start | bytes 1351680 | tf_op jit(solution)/shard_map/all_gather | solution.py:505
  12.9 65.4 %all-gather.9.cloned.1.call-start = ((), (), s32[]{:S(2)}) async-start(), calls=%async_computation.5 | async-start | bytes 1310720 | tf_op jit(solution)/shard_map/all_gather | solution.py:505
  47.2 71.4 %all-gather.11.cloned.1.call-start = ((), (), s32[]{:S(2)}) async-start(), calls=%async_computation.6 | async-start | bytes 1310720 | tf_op jit(solution)/shard_map/all_gather | solution.py:505
  78.2 109.0 %all-gather.13.cloned.1.call-start = ((), (), s32[]{:S(2)}) async-start(), calls=%async_computation.7 | async-start | bytes 1310720 | tf_op jit(solution)/shard_map/all_gather | solution.py:505
  78.3 34.2 %collective-permute-start.10 = (bf16[128,4096]{1,0:T(8,128)(2,1)}, bf16[128,4096]{1,0:T(8,128)(2,1)S(1)}, u32[]{:S(2)}, u32[]{:S(2)}) collective-permute-start(bf16[128,4096]{1,0:T(8,128)(2,1)} %all-gather.9.cloned.1.call-done.refs_0_), channel_id=1, source_target_pairs={{0,2},{2,0},{1,3},{3,1},{4,6},{6,4},{5,7},{7,5},{8,10},{10,8},{9,1... | collective-permute-start | bytes 3145736 | tf_op jit(solution)/shard_map/ppermute | solution.py:395
  123.6 104.8 %all-gather.15.cloned.1.call-start = ((), (), s32[]{:S(2)}) async-start(), calls=%async_computation.8 | async-start | bytes 1310720 | tf_op jit(solution)/shard_map/all_gather | solution.py:505
  126.2 42.5 %collective-permute-start.16 = (bf16[64,4096]{1,0:T(8,128)(2,1)S(1)}, bf16[64,4096]{1,0:T(8,128)(2,1)}, u32[]{:S(2)}, u32[]{:S(2)}) collective-permute-start(bf16[64,4096]{1,0:T(8,128)(2,1)S(1)} %get-tuple-element.539.refs_4_), channel_id=1, source_target_pairs={{0,2},{2,0},{1,3},{3,1},{4,6},{6,4},{5,7},{7,5},{8,10},{10,8},{9,1... | collective-permute-start | bytes 1572872 | tf_op jit(solution)/shard_map/ppermute | solution.py:395
  127.3 41.3 %collective-permute-start.17 = (bf16[64,4096]{1,0:T(8,128)(2,1)}, bf16[64,4096]{1,0:T(8,128)(2,1)}, u32[]{:S(2)}, u32[]{:S(2)}) collective-permute-start(bf16[64,4096]{1,0:T(8,128)(2,1)} %slice.385), channel_id=1, source_target_pairs={{0,4},{4,0},{1,5},{5,1},{2,6},{6,2},{3,7},{7,3},{8,12},{12,8},{9,1... | collective-permute-start | bytes 1572872 | tf_op jit(solution)/shard_map/ppermute | solution.py:395
  129.5 50.1 %collective-permute-start.20 = (bf16[512,1024]{1,0:T(8,128)(2,1)S(1)}, bf16[512,1024]{1,0:T(8,128)(2,1)}, u32[]{:S(2)}, u32[]{:S(2)}) collective-permute-start(bf16[512,1024]{1,0:T(8,128)(2,1)S(1)} %copy-done.78), channel_id=1, source_target_pairs={{0,2},{2,0},{1,3},{3,1},{4,6},{6,4},{5,7},{7,5},{8,10},{10,8},{9,1... | collective-permute-start | bytes 3145736 | tf_op jit(solution)/shard_map/ppermute | solution.py:395
  130.5 49.2 %collective-permute-start.21 = (bf16[512,1024]{1,0:T(8,128)(2,1)S(1)}, bf16[512,1024]{1,0:T(8,128)(2,1)}, u32[]{:S(2)}, u32[]{:S(2)}) collective-permute-start(bf16[512,1024]{1,0:T(8,128)(2,1)S(1)} %copy-done.78), channel_id=1, source_target_pairs={{0,4},{4,0},{1,5},{5,1},{2,6},{6,2},{3,7},{7,3},{8,12},{12,8},{9,1... | collective-permute-start | bytes 3145736 | tf_op jit(solution)/shard_map/ppermute | solution.py:395
  145.4 34.3 %collective-permute-start.22 = (bf16[512,1024]{1,0:T(8,128)(2,1)S(1)}, bf16[512,1024]{1,0:T(8,128)(2,1)S(1)}, u32[]{:S(2)}, u32[]{:S(2)}) collective-permute-start(bf16[512,1024]{1,0:T(8,128)(2,1)S(1)} %copy-done.78), channel_id=1, source_target_pairs={{0,1},{1,0},{2,3},{3,2},{4,5},{5,4},{6,7},{7,6},{8,9},{9,8},{10,11... | collective-permute-start | bytes 3145736 | tf_op jit(solution)/shard_map/ppermute | solution.py:395
  181.2 86.4 %all-gather.17.cloned.1.call-start = ((), (), s32[]{:S(2)}) async-start(), calls=%async_computation.9 | async-start | bytes 1310720 | tf_op jit(solution)/shard_map/all_gather | solution.py:505
  187.2 34.0 %collective-permute-start.29 = (bf16[128,4096]{1,0:T(8,128)(2,1)}, bf16[128,4096]{1,0:T(8,128)(2,1)}, u32[]{:S(2)}, u32[]{:S(2)}) collective-permute-start(bf16[128,4096]{1,0:T(8,128)(2,1)} %all-gather.13.cloned.1.call-done.refs_0_), channel_id=1, source_target_pairs={{0,2},{2,0},{1,3},{3,1},{4,6},{6,4},{5,7},{7,5},{8,10},{10,8},{9,1... | collective-permute-start | bytes 3145736 | tf_op jit(solution)/shard_map/ppermute | solution.py:395
  188.2 33.9 %collective-permute-start.30 = (bf16[128,4096]{1,0:T(8,128)(2,1)}, bf16[128,4096]{1,0:T(8,128)(2,1)}, u32[]{:S(2)}, u32[]{:S(2)}) collective-permute-start(bf16[128,4096]{1,0:T(8,128)(2,1)} %all-gather.13.cloned.1.call-done.refs_0_), channel_id=1, source_target_pairs={{0,4},{4,0},{1,5},{5,1},{2,6},{6,2},{3,7},{7,3},{8,12},{12,8},{9,1... | collective-permute-start | bytes 3145736 | tf_op jit(solution)/shard_map/ppermute | solution.py:395
  222.7 409.4 %reduce-scatter.5.cloned.1.call-start = ((), (), s32[]{:S(2)}) async-start(), calls=%async_computation.10 | async-start | bytes 2621440 | tf_op jit(solution)/shard_map/reduce_scatter | solution.py:400
  273.7 34.2 %collective-permute-start.48 = (bf16[512,1024]{1,0:T(8,128)(2,1)S(1)}, bf16[512,1024]{1,0:T(8,128)(2,1)S(1)}, u32[]{:S(2)}, u32[]{:S(2)}) collective-permute-start(bf16[512,1024]{1,0:T(8,128)(2,1)S(1)} %copy-done.79), channel_id=1, source_target_pairs={{0,2},{2,0},{1,3},{3,1},{4,6},{6,4},{5,7},{7,5},{8,10},{10,8},{9,1... | collective-permute-start | bytes 3145736 | tf_op jit(solution)/shard_map/ppermute | solution.py:395
  274.7 34.0 %collective-permute-start.49 = (bf16[512,1024]{1,0:T(8,128)(2,1)S(1)}, bf16[512,1024]{1,0:T(8,128)(2,1)}, u32[]{:S(2)}, u32[]{:S(2)}) collective-permute-start(bf16[512,1024]{1,0:T(8,128)(2,1)S(1)} %copy-done.79), channel_id=1, source_target_pairs={{0,4},{4,0},{1,5},{5,1},{2,6},{6,2},{3,7},{7,3},{8,12},{12,8},{9,1... | collective-permute-start | bytes 3145736 | tf_op jit(solution)/shard_map/ppermute | solution.py:395
  395.8 60.4 %collective-permute-start.62 = (bf16[1024,1024]{1,0:T(8,128)(2,1)}, bf16[1024,1024]{1,0:T(8,128)(2,1)}, u32[]{:S(2)}, u32[]{:S(2)}) collective-permute-start(bf16[1024,1024]{1,0:T(8,128)(2,1)} %grad_rows.25), channel_id=1, source_target_pairs={{0,4},{4,0},{1,5},{5,1},{2,6},{6,2},{3,7},{7,3},{8,12},{12,8},{9,1... | collective-permute-start | bytes 6291464 | tf_op jit(solution)/shard_map/ppermute | solution.py:395
  401.8 54.4 %collective-permute-start.63 = (bf16[256,4096]{1,0:T(8,128)(2,1)}, bf16[256,4096]{1,0:T(8,128)(2,1)}, u32[]{:S(2)}, u32[]{:S(2)}) collective-permute-start(bf16[256,4096]{1,0:T(8,128)(2,1)} %grad_rows.27), channel_id=1, source_target_pairs={{0,2},{2,0},{1,3},{3,1},{4,6},{6,4},{5,7},{7,5},{8,10},{10,8},{9,1... | collective-permute-start | bytes 6291464 | tf_op jit(solution)/shard_map/ppermute | solution.py:395
  544.3 87.9 %collective-permute-start.76 = (bf16[1024,1024]{1,0:T(8,128)(2,1)}, bf16[1024,1024]{1,0:T(8,128)(2,1)}, u32[]{:S(2)}, u32[]{:S(2)}) collective-permute-start(bf16[1024,1024]{1,0:T(8,128)(2,1)} %grad_rows.35), channel_id=1, source_target_pairs={{0,4},{4,0},{1,5},{5,1},{2,6},{6,2},{3,7},{7,3},{8,12},{12,8},{9,1... | collective-permute-start | bytes 6291464 | tf_op jit(solution)/shard_map/ppermute | solution.py:395
  549.8 101.1 %reduce-scatter.7.cloned.1.call-start = ((), (), s32[]{:S(2)}) async-start(), calls=%async_computation.11 | async-start | bytes 1310720 | tf_op jit(solution)/shard_map/reduce_scatter | solution.py:400
  569.5 62.6 %collective-permute-start.77 = (bf16[256,4096]{1,0:T(8,128)(2,1)}, bf16[256,4096]{1,0:T(8,128)(2,1)}, u32[]{:S(2)}, u32[]{:S(2)}) collective-permute-start(bf16[256,4096]{1,0:T(8,128)(2,1)} %grad_rows.39), channel_id=1, source_target_pairs={{0,2},{2,0},{1,3},{3,1},{4,6},{6,4},{5,7},{7,5},{8,10},{10,8},{9,1... | collective-permute-start | bytes 6291464 | tf_op jit(solution)/shard_map/ppermute | solution.py:395
  625.0 105.5 %reduce-scatter.9.cloned.1.call-start = ((), (), s32[]{:S(2)}) async-start(), calls=%async_computation.12 | async-start | bytes 2621440 | tf_op jit(solution)/shard_map/reduce_scatter | solution.py:400
  685.4 72.3 %reduce-scatter.11.cloned.1.call-start = ((), (), s32[]{:S(2)}) async-start(), calls=%async_computation.13 | async-start | bytes 1310720 | tf_op jit(solution)/shard_map/reduce_scatter | solution.py:400
  (228 other events, 3154.6 us)
Sparse Core Ops, SparseCore 0:
  13.0 31.1 all-gather.6
  47.3 25.8 all-gather.8
  78.3 26.8 all-gather.10
  123.8 27.3 all-gather.12
  181.3 27.2 all-gather.14
  222.8 27.2 all-gather.16
  549.9 42.2 reduce-scatter.4
  625.2 25.6 reduce-scatter.6
  685.5 42.4 reduce-scatter.8
  732.8 24.8 reduce-scatter.10

commit v4 on v3

--- a/solution.py
+++ b/solution.py
@@ -228,7 +228,7 @@
         + [jax.ShapeDtypeStruct((rows, width), jnp.bfloat16)] * (2 * parts)
         + [jax.ShapeDtypeStruct((heads // 2, 2, (span + 1) * TILE), jnp.float32)],
         compiler_params=pltpu.CompilerParams(vmem_limit_bytes=48 << 20),
-        cost_estimate=BRIEF,
+        cost_estimate=pl.CostEstimate(flops=40 * q_rows * keys * width, bytes_accessed=8 * keys * width + 8 * q_rows * width, transcendentals=heads * q_rows * keys),
         name="attn_bwd",
     )(pos, q, do, o, lse, *ks, *vs, bias)
     dq, dks, dvs, d = out[0], out[1:1 + parts], out[1 + parts:1 + 2 * parts], out[-1]
@@ -283,7 +283,7 @@
 def mlp_back(grad_out, attended, gain, w_outer, w_inner, slope):
     rows, width = grad_out.shape
     wide = w_outer.shape[0]
-    tile = 512
+    tile = min(1024, wide)
     whole = pl.BlockSpec((rows, width), lambda i: (0, 0))
     line = pl.BlockSpec((1, width), lambda i: (0, 0))
     return pl.pallas_call(
@@ -322,7 +322,7 @@
 
     @pl.when(i == 2)
     def _():
-        grad_in, grad_gain = norm_back(acc_ref[...], value_ref[...], gain_ref[...])
+        grad_in, grad_gain = norm_back(acc_ref[...], value_ref[...].astype(jnp.float32), gain_ref[...])
         out_ref[...] = add_ref[...] + grad_in
         gain_grad_ref[...] = grad_gain
 
@@ -430,7 +430,7 @@
 
     def reduce_keys(self, parts):
         if self.m == 1:
-            return parts[0].astype(jnp.float32) + self.exchange(parts[1], "core").astype(jnp.float32)
+            return add_rows(parts[0].shape[0], (parts[0], 0), (self.exchange(parts[1], "core"), 0))
         return lax.psum_scatter(parts[0], ("q", "core"), scatter_dimension=0, tiled=True).astype(jnp.float32)
 
     def positions(self, length, blk):
@@ -528,13 +528,14 @@
         self.x_twin, self.y_twin = self.send(self.by_x, "core"), self.send(self.by_y, "core")
         return tie(main, self.x_twin, self.y_twin)
 
-    def c(self, main):
+    def c(self, main, between=None):
         if not self.pairs:
-            return main, self.near.value
+            return (between(main) if between else main), self.near.value
         plan = self.plan
         main = tie(main, self.low, self.high)
         twins = [self.send(p, "core") for p in (self.low, self.high)]
         main = tie(main, *twins)
+        main = between(main) if between else main
         low_twin, high_twin = [t.value for t in twins]
         half = self.low.value.shape[0]
         by_y, y_twin = self.by_y.value, self.y_twin.value
@@ -551,6 +552,28 @@
         return main, whole.value
 
 
+def add_kernel(*refs):
+    total = refs[0][...].astype(jnp.float32)
+    for r in refs[1:-1]:
+        total = total + r[...].astype(jnp.float32)
+    refs[-1][...] = total.astype(refs[-1].dtype)
+
+
+def add_rows(count, *terms):
+    width = terms[0][0].shape[1]
+    tile = count // 2
+    return pl.pallas_call(
+        add_kernel,
+        grid=(2,),
+        in_specs=[pl.BlockSpec((tile, width), lambda i, base=first // tile: (base + i, 0)) for _, first in terms],
+        out_specs=pl.BlockSpec((tile, width), lambda i: (i, 0)),
+        out_shape=jax.ShapeDtypeStruct((count, width), jnp.bfloat16),
+        compiler_params=pltpu.CompilerParams(vmem_limit_bytes=32 << 20),
+        cost_estimate=BRIEF,
+        name="add_rows",
+    )(*[array for array, _ in terms])
+
+
 def add_low(*terms):
     total = terms[0].astype(jnp.float32)
     for t in terms[1:]:
@@ -594,12 +617,13 @@
             quarter = self.rows // 4
             self.close_by = Held(self.product(0, quarter, (self.other.value, 0)))
             return self.close_by
-        return self.far
+        self.close_by = self.far
+        return self.close_by
 
     def three(self):
         if self.pairs:
             eighth = self.rows // 8
-            self.part = Held(add_low(self.close_by.value[eighth:], self.far.value[eighth:]))
+            self.part = Held(add_rows(eighth, (self.close_by.value, eighth), (self.far.value, eighth)))
         else:
             self.part = self.far
         return self.part
@@ -615,7 +639,7 @@
         nz = self.plan.nz
         if self.pairs:
             eighth = self.rows // 8
-            total = add_low(self.close_by.value[:eighth], self.far.value[:eighth], self.side.value)
+            total = add_rows(eighth, (self.close_by.value, 0), (self.far.value, 0), (self.side.value, 0))
         else:
             total = self.side.value
         self.piece = Held(total.reshape(nz, total.shape[0] // nz, -1))
@@ -758,25 +782,25 @@
         last = tie(dv[-1], outer.far, inner.far, *late)
         grad_k = plan.reduce_keys(dk).astype(low)
         grad_v = plan.reduce_keys(list(dv[:-1]) + [last]).astype(low)
-        grad_v = tie(grad_v, outer.three(), inner.three())
+        k_held = Held(grad_k)
+        grad_v = tie(grad_v, k_held, outer.three(), inner.three())
+        grad_k = k_held.value
         outer.send_three()
         inner.send_three()
         tiles = width // 1024
         qk = Chain(plan, rows_of((left_n[orders[2]], grad_query, 0, tiles), (left_n[orders[2]], grad_k, 0, tiles)), orders[2], width)
         ov = Chain(plan, rows_of((left_c, attn_low, 0, tiles), (left_n[orders[3]], grad_v, 0, tiles)), orders[3], width)
-        late = [previous.attn_sum] if previous else []
-        grad_v = tie(grad_v, qk.one(), ov.one(), *late)
+        grad_v = tie(grad_v, qk.one(), ov.one())
         qk.send_one()
         ov.send_one()
         grad_out, grad_attn_gain = project_back(grad_attended, x, attn_gain, grad_query, grad_k, grad_v, w_qkv)
         grad_out = tie(grad_out, qk.other, ov.other)
-        grad_out = tie(grad_out, qk.two(), ov.two())
+        grad_out = tie(grad_out, qk.two(), ov.two(), outer.close_by, inner.close_by)
         qk.send_two()
         ov.send_two()
         previous = LayerSums(outer, inner, qk, ov, grad_attn_gain, grad_mlp_gain, width)
         results.append(previous)
         diags.append(diag)
-    grad_out = tie(grad_out, outer.side, inner.side)
     outer.close()
     inner.close()
     previous.sum_mlp(plan)
@@ -785,7 +809,7 @@
     qk.send_three()
     ov.send_three()
     qk.close()
-    qk.piece.value = tie(qk.piece.value, ov.close(), previous.mlp_sum)
+    qk.piece.value = tie(qk.piece.value, ov.close(), previous.mlp_sum, results[0].attn_sum)
     previous.sum_attn(plan)
     return grad_out, results, diags, arrived.value
 
@@ -846,6 +870,9 @@
     cotangent = plan.to_sequences(cotangent)
     x = tie(x, inner_1.shard)
     inner_1.start()
+    held = Held(cotangent)
+    x = tie(x, held)
+    cotangent = held.value
     x = attn_1.a(x, outer_1)
     x = attn_1.b(x)
     x = inner_1.a(x, attn_2)
@@ -871,9 +898,7 @@
     queries_one = qkv[:, :width]
     keys_one, values_one = [p[:, :width] for p in kv], [p[:, width:] for p in kv]
     context_one, log_one = attn_fwd(pos, queries_one, keys_one, values_one, bias, blk)
-    context_one, w_inner_one = inner_1.c(context_one)
-    context_one = outer_1.b(context_one)
-    context_one = attn_2.a(context_one, outer_2)
+    context_one, w_inner_one = inner_1.c(context_one, lambda main: attn_2.a(outer_1.b(main), outer_2))
     attended_one = x_one + matmul_rows(context_one, first[:, 3 * width:4 * width])
     normed_mlp_one, hidden_one, slope_one = widen(attended_one, gain[1:2], w_inner_one)
     slope_one = Held(slope_one)
@@ -905,7 +930,7 @@
 
     weights_one = (gain[0:1], first, first[:, 3 * width:4 * width], gain[1:2], w_inner_one, w_outer_one)
     weights_two = (gain[2:3], third, third[:, 3 * width:], gain[3:4], w_inner_two, w_outer_two)
-    saved_one = (x_one, normed_one, queries_one, keys_one, values_one, context_one, log_one, attended_one, normed_mlp_one, hidden_one, slope_one)
+    saved_one = (x, normed_one, queries_one, keys_one, values_one, context_one, log_one, attended_one, normed_mlp_one, hidden_one, slope_one)
     saved_two = (x_two, normed_two, queries_two, keys_two, values_two, context_two, log_two, attended_two, normed_mlp_two, hidden_two, slope_two)
 
     xy, yx = ("x", "y"), ("y", "x")

time: 778 us -> 746 us (0.959)
  other arithmetic: 57.7 us -> 17.6 us
  Pallas kernels: 284 us -> 320 us
  waiting for transfers between devices: 167 us -> 135 us
  local copies, waits for them, and re-layouts: 84.7 us -> 92.5 us
    convert_element_type x21 -> x0, other arithmetic: 40.7 us -> none  [the longest x16 33.5 us: add_low(): return total.astype(jnp.bfloat16)]
    pallas_call x0 -> x20, Pallas kernels: none -> 25.5 us  [add_rows(): pl.pallas_call(add_kernel, grid=(2,), in_specs=[pl.BlockSpec((tile, width...]
    ppermute x88, waiting for transfers between devices: 125 us -> 109 us  [exchange(): return lax.ppermute(piece, name, SWAP)]
    all_gather x6, waiting for transfers between devices: 14 us -> 2.78 us  [start(): self.near = Held(lax.all_gather(self.shard.value, axes, axis=0, tiled=True))]
    pallas_call x24, Pallas kernels: 66.1 us -> 77 us  [grad_rows(): pl.pallas_call(functools.partial(grad_kernel, lefts, starts, add is not N...]
    reduce_scatter x4, waiting for transfers between devices: 14.5 us -> 5.27 us  [sum_z(): return lax.psum_scatter(piece, 'z', scatter_dimension=0, tiled=False)]
    unnamed x316 -> x314, local copies, waits for them, and re-layouts: 37 us -> 41 us
  transfers between devices with their start and end apart: 103 -> 103, of which waited for: 50 -> 42; matrix products, arithmetic and copies ran while one was open for 23% -> 21% of each run, Pallas kernels for 33% -> 37%
where the time goes in v4:
time: 746 us; the launch traced here: 736 us
  Pallas kernels  320 us (43%)
  waiting for transfers between devices  135 us (18%)
  matrix products  95 us (13%)
  local copies, waits for them, and re-layouts  92.5 us (12%)
  starting transfers between devices  59.6 us (8%)
  other arithmetic  17.6 us (2%)
  between operations  16.6 us (2%)
    ppermute x88, waiting for transfers between devices, exchange(): return lax.ppermute(piece, name, SWAP)  109 us
    dot_general x17, matrix products, matmul_rows(): return jnp.dot(left, right, preferred_element_type=jnp.float32)  86 us
    pallas_call x24, Pallas kernels, grad_rows(): pl.pallas_call(functools.partial(grad_kernel, lefts, starts, add is not N...  77 us
    pallas_call x2, Pallas kernels, attn_bwd(): pl.pallas_call(functools.partial(attn_bwd_kernel, parts, chunk, blk), gri...  71.1 us
    ppermute x88, starting transfers between devices, exchange(): return lax.ppermute(piece, name, SWAP)  55.7 us
    pallas_call x6, Pallas kernels, assemble(): pl.pallas_call(functools.partial(assemble_kernel, steps, depth), grid_spe...  47 us
    unnamed x314, local copies, waits for them, and re-layouts  41 us
    pallas_call x2, Pallas kernels, attn_fwd(): pl.pallas_call(functools.partial(attn_fwd_kernel, parts, chunk, blk), gri...  38.9 us
  transfers between devices with their start and end apart: 103, of which 42 were waited for; matrix products, arithmetic and copies ran while one was open for 21% of the time, Pallas kernels for 37%

profile of v4, /device:TPU:0, one launch (start us, length us, event | category | flops | bytes accessed | tf_op | source)
XLA Modules:
  0.0 735.9 jit_solution(6629443811403677634)
XLA Ops:
  18.6 11.3 %collective-permute-done = bf16[256,1024]{1,0:T(8,128)(2,1)S(1)} collective-permute-done((bf16[256,1024]{1,0:T(8,128)(2,1)S(1)}, bf16[256,1024]{1,0:T(8,128)(2,1)S(1)}, u32[]{:S(2)}, u32[]{:S(2)}) %collective-permute-start) | collective-permute-done | bytes 524320 | tf_op jit(solution)/shard_map/ppermute | solution.py:395
  30.0 10.3 %collective-permute-done.1 = bf16[256,1024]{1,0:T(8,128)(2,1)S(1)} collective-permute-done((bf16[256,1024]{1,0:T(8,128)(2,1)S(1)}, bf16[256,1024]{1,0:T(8,128)(2,1)S(1)}, u32[]{:S(2)}, u32[]{:S(2)}) %collective-permute-start.1) | collective-permute-done | bytes 524320 | tf_op jit(solution)/shard_map/ppermute | solution.py:395
  47.2 22.7 %collective-permute-done.2.refs_2_ = bf16[128,4224]{1,0:T(8,128)(2,1)} collective-permute-done((bf16[128,4224]{1,0:T(8,128)(2,1)}, bf16[128,4224]{1,0:T(8,128)(2,1)}, u32[]{:S(2)}, u32[]{:S(2)}) %collective-permute-start.2) | collective-permute-done | bytes 1081376 | tf_op jit(solution)/shard_map/ppermute | solution.py:395
  80.4 10.1 %collective-permute-done.7.refs_6_ = bf16[64,4224]{1,0:T(8,128)(2,1)} collective-permute-done((bf16[64,4224]{1,0:T(8,128)(2,1)S(1)}, bf16[64,4224]{1,0:T(8,128)(2,1)}, u32[]{:S(2)}, u32[]{:S(2)}) %collective-permute-start.7) | collective-permute-done | bytes 540704 | tf_op jit(solution)/shard_map/ppermute | solution.py:395
  94.2 8.2 %assemble.6.w_ref = bf16[1024,4224]{1,0:T(8,128)(2,1)} custom-call(s32[10]{0:T(128)S(1)} %pad_add_fusion.1.table_ref, bf16[128,4224]{1,0:T(8,128)(2,1)S(1)} %copy-done.78, bf16[128,4224]{1,0:T(8,128)(2,1)} %copy-done.119, bf16[128,4224]{1,0:T(8,128)(2,1)} %collective-permute-done.2.refs_2_, bf16[128,4224]{1,0:T(8,128)(2,1)} %collective-permute-done.5.refs_3_, ...), custom_call_target="tpu_custom_call" | custom-call | flops 1024 | bytes 1024 | tf_op jit(solution)/shard_map/assemble/pallas_call | solution.py:470
  103.9 7.7 %fusion.20 = bf16[512,3072]{1,0:T(8,128)(2,1)} fusion(bf16[1024,4224]{1,0:T(8,128)(2,1)} %assemble.6.w_ref, bf16[512,1024]{1,0:T(8,128)(2,1)S(1)} %pad_maximum_fusion.value_ref, f32[1024]{0:T(1024)S(1)} %bitcast.83, f32[512]{0:T(512)S(1)} %add_rsqrt_fusion.3), kind=kOutput, calls=%fused_computation.48 | convolution fusion | flops 3224895488 | bytes 10491904 | tf_op jit(solution)/shard_map/dot_general | solution.py:239
  131.3 10.9 %toeplitz.1.refs_4_ = bf16[16,15,128,128]{3,2,1,0:T(8,128)(2,1)} custom-call(f32[16,1,2048]{2,1,0:T(1,128)} %reshape.119.u_ref), custom_call_target="tpu_custom_call" | custom-call | flops 1024 | bytes 1024 | tf_op jit(solution)/shard_map/toeplitz/pallas_call | solution.py:29
  149.0 19.5 %attn_fwd.2 = (bf16[512,1024]{1,0:T(8,128)(2,1)S(1)}, f32[8,2,512]{2,1,0:T(2,128)S(1)}) custom-call(s32[7]{0:T(128)S(1)} %stack.74.pos_ref, bf16[512,1024]{1,0:T(8,128)(2,1)S(1)} %slice.282.q_ref, bf16[512,1024]{1,0:T(8,128)(2,1)S(1)} %get-tuple-element.515.refs_0_, bf16[512,1024]{1,0:T(8,128)(2,1)S(1)} %get-tuple-element.519.refs_1_, ...), custom_call_target="tpu_custom_call" | custom-call | flops 1024 | bytes 1024 | tf_op jit(solution)/shard_map/attn_fwd/pallas_call | solution.py:115
  180.2 8.7 %assemble.7.inner_ref = bf16[1024,4096]{1,0:T(8,128)(2,1)} custom-call(s32[10]{0:T(128)S(1)} %pad_add_fusion.1.table_ref, bf16[128,4096]{1,0:T(8,128)(2,1)S(1)} %copy-done.82, bf16[128,4096]{1,0:T(8,128)(2,1)} %copy-done.120, bf16[128,4096]{1,0:T(8,128)(2,1)} %copy-done.109, bf16[128,4096]{1,0:T(8,128)(2,1)} %copy-done.121, ...), custom_call_target="tpu_custom_call" | custom-call | flops 1024 | bytes 1024 | tf_op jit(solution)/shard_map/assemble/pallas_call | solution.py:470
  194.6 11.3 %fusion.7 = (bf16[512,4096]{1,0:T(8,128)(2,1)}, bf16[512,4096]{1,0:T(8,128)(2,1)}) fusion(bf16[1024,4096]{1,0:T(8,128)(2,1)S(1)} %copy-done.104, f32[512,1024]{1,0:T(8,128)S(1)} %get-tuple-element.579.value_ref, f32[1024]{0:T(1024)S(1)} %bitcast.86, f32[512]{0:T(512)S(1)} %add_rsqrt_fusion.2), kind=kOutput, calls=%fused_computation.15 | convolution fusion | flops 4334288896 | bytes 18880512 | tf_op jit(solution)/shard_map/dot_general | solution.py:239
  208.8 8.1 %assemble.8.outer_ref = bf16[4096,1024]{1,0:T(8,128)(2,1)} custom-call(s32[10]{0:T(128)S(1)} %pad_add_fusion.1.table_ref, bf16[512,1024]{1,0:T(8,128)(2,1)S(1)} %copy-done.80, bf16[512,1024]{1,0:T(8,128)(2,1)} %collective-permute-done.23.refs_1_, bf16[512,1024]{1,0:T(8,128)(2,1)} %collective-permute-done.21.refs_2_, ...), custom_call_target="tpu_custom_call" | custom-call | flops 1024 | bytes 1024 | tf_op jit(solution)/shard_map/assemble/pallas_call | solution.py:470
  224.9 9.7 %convolution_add_fusion.value_ref = f32[512,1024]{1,0:T(8,128)S(1)} fusion(f32[512,1024]{1,0:T(8,128)} %copy-done.115, bf16[512,4096]{1,0:T(8,128)(2,1)} %get-tuple-element.331.refs_0_.refs_1_.refs_2_.refs_3_, bf16[4096,1024]{1,0:T(8,128)(2,1)} %assemble.8.outer_ref), kind=kOutput, calls=%fused_computation.88 | convolution fusion | flops 4295491584 | bytes 16777216 | tf_op jit(solution)/shard_map/dot_general | solution.py:239
  247.6 7.9 %fusion.23 = bf16[512,3072]{1,0:T(8,128)(2,1)} fusion(bf16[512,1024]{1,0:T(8,128)(2,1)S(1)} %multiply_convert_fusion.4, bf16[1024,4096]{1,0:T(8,128)(2,1)} %assemble.9.w_ref), kind=kOutput, calls=%fused_computation.49 | convolution fusion | flops 3222798336 | bytes 10485760 | tf_op jit(solution)/shard_map/dot_general | solution.py:239
  272.2 19.5 %attn_fwd.3 = (bf16[512,1024]{1,0:T(8,128)(2,1)S(1)}, f32[8,2,512]{2,1,0:T(2,128)S(1)}) custom-call(s32[7]{0:T(128)S(1)} %stack.74.pos_ref, bf16[512,1024]{1,0:T(8,128)(2,1)S(1)} %get-tuple-element.513.q_ref, bf16[512,1024]{1,0:T(8,128)(2,1)S(1)} %get-tuple-element.512.refs_0_, bf16[512,1024]{1,0:T(8,128)(2,1)S(1)} %get-tuple-element.517.refs_1_, ...), custom_call_target="tpu_custom_call" | custom-call | flops 1024 | bytes 1024 | tf_op jit(solution)/shard_map/attn_fwd/pallas_call | solution.py:115
  313.3 11.4 %fusion.15 = (bf16[512,4096]{1,0:T(8,128)(2,1)}, bf16[512,4096]{1,0:T(8,128)(2,1)S(1)}) fusion(bf16[1024,4096]{1,0:T(8,128)(2,1)S(1)} %copy-done.105, f32[512,1024]{1,0:T(8,128)S(1)} %get-tuple-element.581.value_ref, f32[1024]{0:T(1024)S(1)} %bitcast.88, f32[512]{0:T(512)S(1)} %add_rsqrt_fusion), kind=kOutput, calls=%fused_computation.23 | convolution fusion | flops 4334288896 | bytes 18880512 | tf_op jit(solution)/shard_map/dot_general | solution.py:239
  335.4 7.9 %multiply_convert_fusion.2 = bf16[512,1024]{1,0:T(8,128)(2,1)S(1)} fusion(f32[512,1024]{1,0:T(8,128)S(1)} %get-tuple-element.581.value_ref, bf16[512,4096]{1,0:T(8,128)(2,1)S(1)} %get-tuple-element.378.refs_0_.refs_1_.refs_2_.refs_3_, bf16[4096,1024]{1,0:T(8,128)(2,1)} %assemble.11.outer_ref, f32[512]{0:T(512)S(1)} %fusion.74), kind=kOutput, calls=%fused_computation.72 | convolution fusion | flops 4296540160 | bytes 15730688 | tf_op jit(solution)/shard_map/dot_general | solution.py:239
  355.5 16.3 %mlp_back.2 = (bf16[512,4096]{1,0:T(8,128)(2,1)}, f32[512,1024]{1,0:T(8,128)S(1)}, bf16[512,1024]{1,0:T(8,128)(2,1)S(1)}, f32[1,1024]{1,0:T(1,128)S(1)}) custom-call(f32[512,1024]{1,0:T(8,128)S(1)} %copy-done.61, f32[512,1024]{1,0:T(8,128)} %copy-done.117, f32[1,1024]{1,0:T(1,128)S(1)} %get-tuple-element.570.gain_ref, ...), custom_call_target="tpu_custom_call" | custom-call | flops 1024 | bytes 1024 | tf_op jit(solution)/shard_map/mlp_back/pallas_call | solution.py:289
  403.5 35.4 %attn_bwd.2 = (bf16[512,1024]{1,0:T(8,128)(2,1)S(1)}, bf16[512,1024]{1,0:T(8,128)(2,1)S(1)}, bf16[512,1024]{1,0:T(8,128)(2,1)S(1)}, bf16[512,1024]{1,0:T(8,128)(...) custom-call(s32[7]{0:T(128)S(1)} %copy-done.98, bf16[512,1024]{1,0:T(8,128)(2,1)} %copy-done.68, ...), custom_call_target="tpu_custom_call" | custom-call | flops 21474836480 | bytes 12582912 | tf_op jit(solution)/shard_map/attn_bwd/pallas_call | solution.py:218
  454.9 8.0 %project_back.2 = (f32[512,1024]{1,0:T(8,128)S(1)}, f32[1,1024]{1,0:T(1,128)S(1)}) custom-call(f32[512,1024]{1,0:T(8,128)} %copy-done.70, f32[512,1024]{1,0:T(8,128)} %copy-done.106, f32[1,1024]{1,0:T(1,128)S(1)} %copy-done.92, bf16[512,1024]{1,0:T(8,128)(2,1)S(1)} %get-tuple-element.397.refs_1_.q_ref, bf16[512,1024]{1,0:T(8,128)(2,1)S(1)} %add_rows.21.refs_3_.k_ref, ...), custom_call_target="tpu_custom_call" | custom-call | flops 1024 | bytes 1024 | tf_op jit(solution)/shard_map/project_back/pallas_call | solution.py:334
  491.0 16.5 %mlp_back.3 = (bf16[512,4096]{1,0:T(8,128)(2,1)}, f32[512,1024]{1,0:T(8,128)S(1)}, bf16[512,1024]{1,0:T(8,128)(2,1)S(1)}, f32[1,1024]{1,0:T(1,128)S(1)}) custom-call(f32[512,1024]{1,0:T(8,128)S(1)} %get-tuple-element.424.grad_ref, f32[512,1024]{1,0:T(8,128)} %copy-done.115, f32[1,1024]{1,0:T(1,128)S(1)} %copy-done.96, bf16[4096,1024]{1,0:T(8,128)(2,1)} %assemble.8.outer_ref, ...), custom_call_target="tpu_custom_call" | custom-call | flops 1024 | bytes 1024 | tf_op jit(solution)/shard_map/mlp_back/pallas_call | solution.py:289
  564.2 35.7 %attn_bwd.3 = (bf16[512,1024]{1,0:T(8,128)(2,1)S(1)}, bf16[512,1024]{1,0:T(8,128)(2,1)S(1)}, bf16[512,1024]{1,0:T(8,128)(2,1)}, bf16[512,1024]{1,0:T(8,128)(2,1)...) custom-call(s32[7]{0:T(128)S(1)} %copy-done.99, bf16[512,1024]{1,0:T(8,128)(2,1)} %copy-done.62, ...), custom_call_target="tpu_custom_call" | custom-call | flops 21474836480 | bytes 12582912 | tf_op jit(solution)/shard_map/attn_bwd/pallas_call | solution.py:218
  626.4 8.5 %project_back.3 = (f32[512,1024]{1,0:T(8,128)}, f32[1,1024]{1,0:T(1,128)S(1)}) custom-call(f32[512,1024]{1,0:T(8,128)} %copy-done.71, bf16[512,1024]{1,0:T(8,128)(2,1)S(1)} %copy-done.28, f32[1,1024]{1,0:T(1,128)S(1)} %copy-done.94, bf16[512,1024]{1,0:T(8,128)(2,1)S(1)} %copy-done.17, bf16[512,1024]{1,0:T(8,128)(2,1)S(1)} %add_rows.31.refs_3_.k_ref, ...), custom_call_target="tpu_custom_call" | custom-call | flops 1024 | bytes 1024 | tf_op jit(solution)/shard_map/project_back/pallas_call | solution.py:334
  664.0 14.7 %collective-permute-done.81.refs_1_ = bf16[256,2048]{1,0:T(8,128)(2,1)} collective-permute-done((bf16[256,2048]{1,0:T(8,128)(2,1)}, bf16[256,2048]{1,0:T(8,128)(2,1)}, u32[]{:S(2)}, u32[]{:S(2)}) %collective-permute-start.81) | collective-permute-done | bytes 1048608 | tf_op jit(solution)/shard_map/ppermute | solution.py:395
  707.0 9.6 %collective-permute-done.88 = f32[4608]{0:T(1024)S(1)} collective-permute-done((f32[4608]{0:T(1024)S(1)}, f32[4608]{0:T(1024)S(1)}, u32[]{:S(2)}, u32[]{:S(2)}) %collective-permute-start.88) | collective-permute-done | bytes 18464 | tf_op jit(solution)/shard_map/ppermute | solution.py:409
  (675 shorter events, 389.2 us)
Async XLA Ops:
  7.2 37.0 %all-gather.7.cloned.1.call-start = ((), (), s32[]{:S(2)}) async-start(), calls=%async_computation.4 | async-start | bytes 1351680 | tf_op jit(solution)/shard_map/all_gather | solution.py:505
  12.9 65.4 %all-gather.9.cloned.1.call-start = ((), (), s32[]{:S(2)}) async-start(), calls=%async_computation.5 | async-start | bytes 1310720 | tf_op jit(solution)/shard_map/all_gather | solution.py:505
  47.2 70.4 %all-gather.11.cloned.1.call-start = ((), (), s32[]{:S(2)}) async-start(), calls=%async_computation.6 | async-start | bytes 1310720 | tf_op jit(solution)/shard_map/all_gather | solution.py:505
  78.2 110.7 %all-gather.13.cloned.1.call-start = ((), (), s32[]{:S(2)}) async-start(), calls=%async_computation.7 | async-start | bytes 1310720 | tf_op jit(solution)/shard_map/all_gather | solution.py:505
  78.3 34.2 %collective-permute-start.11 = (bf16[128,4096]{1,0:T(8,128)(2,1)}, bf16[128,4096]{1,0:T(8,128)(2,1)S(1)}, u32[]{:S(2)}, u32[]{:S(2)}) collective-permute-start(bf16[128,4096]{1,0:T(8,128)(2,1)} %all-gather.9.cloned.1.call-done.refs_0_), channel_id=1, source_target_pairs={{0,2},{2,0},{1,3},{3,1},{4,6},{6,4},{5,7},{7,5},{8,10},{10,8},{9,1... | collective-permute-start | bytes 3145736 | tf_op jit(solution)/shard_map/ppermute | solution.py:395
  122.9 99.8 %all-gather.15.cloned.1.call-start = ((), (), s32[]{:S(2)}) async-start(), calls=%async_computation.8 | async-start | bytes 1310720 | tf_op jit(solution)/shard_map/all_gather | solution.py:505
  126.4 43.1 %collective-permute-start.17 = (bf16[64,4096]{1,0:T(8,128)(2,1)S(1)}, bf16[64,4096]{1,0:T(8,128)(2,1)}, u32[]{:S(2)}, u32[]{:S(2)}) collective-permute-start(bf16[64,4096]{1,0:T(8,128)(2,1)S(1)} %get-tuple-element.549.refs_4_), channel_id=1, source_target_pairs={{0,2},{2,0},{1,3},{3,1},{4,6},{6,4},{5,7},{7,5},{8,10},{10,8},{9,1... | collective-permute-start | bytes 1572872 | tf_op jit(solution)/shard_map/ppermute | solution.py:395
  127.5 42.0 %collective-permute-start.18 = (bf16[64,4096]{1,0:T(8,128)(2,1)}, bf16[64,4096]{1,0:T(8,128)(2,1)}, u32[]{:S(2)}, u32[]{:S(2)}) collective-permute-start(bf16[64,4096]{1,0:T(8,128)(2,1)} %slice.289), channel_id=1, source_target_pairs={{0,4},{4,0},{1,5},{5,1},{2,6},{6,2},{3,7},{7,3},{8,12},{12,8},{9,1... | collective-permute-start | bytes 1572872 | tf_op jit(solution)/shard_map/ppermute | solution.py:395
  129.7 42.8 %collective-permute-start.21 = (bf16[512,1024]{1,0:T(8,128)(2,1)S(1)}, bf16[512,1024]{1,0:T(8,128)(2,1)}, u32[]{:S(2)}, u32[]{:S(2)}) collective-permute-start(bf16[512,1024]{1,0:T(8,128)(2,1)S(1)} %copy-done.79), channel_id=1, source_target_pairs={{0,2},{2,0},{1,3},{3,1},{4,6},{6,4},{5,7},{7,5},{8,10},{10,8},{9,1... | collective-permute-start | bytes 3145736 | tf_op jit(solution)/shard_map/ppermute | solution.py:395
  130.7 41.8 %collective-permute-start.22 = (bf16[512,1024]{1,0:T(8,128)(2,1)S(1)}, bf16[512,1024]{1,0:T(8,128)(2,1)}, u32[]{:S(2)}, u32[]{:S(2)}) collective-permute-start(bf16[512,1024]{1,0:T(8,128)(2,1)S(1)} %copy-done.79), channel_id=1, source_target_pairs={{0,4},{4,0},{1,5},{5,1},{2,6},{6,2},{3,7},{7,3},{8,12},{12,8},{9,1... | collective-permute-start | bytes 3145736 | tf_op jit(solution)/shard_map/ppermute | solution.py:395
  170.0 92.6 %all-gather.17.cloned.1.call-start = ((), (), s32[]{:S(2)}) async-start(), calls=%async_computation.9 | async-start | bytes 1310720 | tf_op jit(solution)/shard_map/all_gather | solution.py:505
  217.5 386.7 %reduce-scatter.5.cloned.1.call-start = ((), (), s32[]{:S(2)}) async-start(), calls=%async_computation.10 | async-start | bytes 2621440 | tf_op jit(solution)/shard_map/reduce_scatter | solution.py:400
  222.7 34.5 %collective-permute-start.39 = (bf16[128,4096]{1,0:T(8,128)(2,1)}, bf16[128,4096]{1,0:T(8,128)(2,1)S(1)}, u32[]{:S(2)}, u32[]{:S(2)}) collective-permute-start(bf16[128,4096]{1,0:T(8,128)(2,1)} %all-gather.15.cloned.1.call-done.refs_0_), channel_id=1, source_target_pairs={{0,2},{2,0},{1,3},{3,1},{4,6},{6,4},{5,7},{7,5},{8,10},{10,8},{9,1... | collective-permute-start | bytes 3145736 | tf_op jit(solution)/shard_map/ppermute | solution.py:395
  223.8 34.5 %collective-permute-start.40 = (bf16[128,4096]{1,0:T(8,128)(2,1)}, bf16[128,4096]{1,0:T(8,128)(2,1)S(1)}, u32[]{:S(2)}, u32[]{:S(2)}) collective-permute-start(bf16[128,4096]{1,0:T(8,128)(2,1)} %all-gather.15.cloned.1.call-done.refs_0_), channel_id=1, source_target_pairs={{0,4},{4,0},{1,5},{5,1},{2,6},{6,2},{3,7},{7,3},{8,12},{12,8},{9,1... | collective-permute-start | bytes 3145736 | tf_op jit(solution)/shard_map/ppermute | solution.py:395
  268.3 34.6 %collective-permute-start.49 = (bf16[512,1024]{1,0:T(8,128)(2,1)S(1)}, bf16[512,1024]{1,0:T(8,128)(2,1)S(1)}, u32[]{:S(2)}, u32[]{:S(2)}) collective-permute-start(bf16[512,1024]{1,0:T(8,128)(2,1)S(1)} %copy-done.83), channel_id=1, source_target_pairs={{0,2},{2,0},{1,3},{3,1},{4,6},{6,4},{5,7},{7,5},{8,10},{10,8},{9,1... | collective-permute-start | bytes 3145736 | tf_op jit(solution)/shard_map/ppermute | solution.py:395
  269.3 34.4 %collective-permute-start.50 = (bf16[512,1024]{1,0:T(8,128)(2,1)S(1)}, bf16[512,1024]{1,0:T(8,128)(2,1)}, u32[]{:S(2)}, u32[]{:S(2)}) collective-permute-start(bf16[512,1024]{1,0:T(8,128)(2,1)S(1)} %copy-done.83), channel_id=1, source_target_pairs={{0,4},{4,0},{1,5},{5,1},{2,6},{6,2},{3,7},{7,3},{8,12},{12,8},{9,1... | collective-permute-start | bytes 3145736 | tf_op jit(solution)/shard_map/ppermute | solution.py:395
  391.5 48.2 %collective-permute-start.61 = (bf16[1024,1024]{1,0:T(8,128)(2,1)}, bf16[1024,1024]{1,0:T(8,128)(2,1)S(1)}, u32[]{:S(2)}, u32[]{:S(2)}) collective-permute-start(bf16[1024,1024]{1,0:T(8,128)(2,1)} %grad_rows.25), channel_id=1, source_target_pairs={{0,4},{4,0},{1,5},{5,1},{2,6},{6,2},{3,7},{7,3},{8,12},{12,8},{9,1... | collective-permute-start | bytes 6291464 | tf_op jit(solution)/shard_map/ppermute | solution.py:395
  396.1 47.9 %collective-permute-start.62 = (bf16[256,4096]{1,0:T(8,128)(2,1)}, bf16[256,4096]{1,0:T(8,128)(2,1)}, u32[]{:S(2)}, u32[]{:S(2)}) collective-permute-start(bf16[256,4096]{1,0:T(8,128)(2,1)} %grad_rows.27), channel_id=1, source_target_pairs={{0,2},{2,0},{1,3},{3,1},{4,6},{6,4},{5,7},{7,5},{8,10},{10,8},{9,1... | collective-permute-start | bytes 6291464 | tf_op jit(solution)/shard_map/ppermute | solution.py:395
  479.4 33.7 %collective-permute-start.69 = (bf16[2048,1024]{1,0:T(8,128)(2,1)}, bf16[2048,1024]{1,0:T(8,128)(2,1)}, u32[]{:S(2)}, u32[]{:S(2)}) collective-permute-start(bf16[2048,1024]{1,0:T(8,128)(2,1)} %grad_rows.34), channel_id=1, source_target_pairs={{0,1},{1,0},{2,3},{3,2},{4,5},{5,4},{6,7},{7,6},{8,9},{9,8},{10,11... | collective-permute-start | bytes 12582920 | tf_op jit(solution)/shard_map/ppermute | solution.py:395
  534.0 165.2 %reduce-scatter.9.cloned.1.call-start = ((), (), s32[]{:S(2)}) async-start(), calls=%async_computation.12 | async-start | bytes 1310720 | tf_op jit(solution)/shard_map/reduce_scatter | solution.py:400
  544.1 58.7 %collective-permute-start.75 = (bf16[1024,1024]{1,0:T(8,128)(2,1)S(1)}, bf16[1024,1024]{1,0:T(8,128)(2,1)S(1)}, u32[]{:S(2)}, u32[]{:S(2)}) collective-permute-start(bf16[1024,1024]{1,0:T(8,128)(2,1)S(1)} %copy-done.77), channel_id=1, source_target_pairs={{0,4},{4,0},{1,5},{5,1},{2,6},{6,2},{3,7},{7,3},{8,12},{12,8},{9,1... | collective-permute-start | bytes 6291464 | tf_op jit(solution)/shard_map/ppermute | solution.py:395
  554.0 50.3 %collective-permute-start.76 = (bf16[256,4096]{1,0:T(8,128)(2,1)}, bf16[256,4096]{1,0:T(8,128)(2,1)}, u32[]{:S(2)}, u32[]{:S(2)}) collective-permute-start(bf16[256,4096]{1,0:T(8,128)(2,1)} %grad_rows.39), channel_id=1, source_target_pairs={{0,2},{2,0},{1,3},{3,1},{4,6},{6,4},{5,7},{7,5},{8,10},{10,8},{9,1... | collective-permute-start | bytes 6291464 | tf_op jit(solution)/shard_map/ppermute | solution.py:395
  623.9 75.3 %reduce-scatter.7.cloned.1.call-start = ((), (), s32[]{:S(2)}) async-start(), calls=%async_computation.11 | async-start | bytes 2621440 | tf_op jit(solution)/shard_map/reduce_scatter | solution.py:400
  654.0 72.9 %reduce-scatter.11.cloned.1.call-start = ((), (), s32[]{:S(2)}) async-start(), calls=%async_computation.13 | async-start | bytes 1310720 | tf_op jit(solution)/shard_map/reduce_scatter | solution.py:400
  (227 other events, 3023.5 us)
Sparse Core Ops, SparseCore 0:
  13.0 31.1 all-gather.6
  47.3 25.8 all-gather.8
  78.3 26.8 all-gather.10
  123.0 27.3 all-gather.12
  170.2 27.3 all-gather.14
  217.6 26.7 all-gather.16
  534.1 42.6 reduce-scatter.4
  624.1 26.0 reduce-scatter.8
  654.1 43.7 reduce-scatter.6
  700.5 26.3 reduce-scatter.10

commit v5 on v4

--- a/solution.py
+++ b/solution.py
@@ -18,10 +18,11 @@
 
 
 def toeplitz_kernel(span, u_ref, t_ref):
+    rolled = jnp.broadcast_to(u_ref[0], (TILE, u_ref.shape[2]))
+    rolled = pltpu.roll(rolled, 0, 1, stride=1, stride_axis=0)
     for e in range(span):
-        base = TILE * (span - 1 - e)
-        w = jnp.broadcast_to(u_ref[0, :, base:base + 2 * TILE], (TILE, 2 * TILE))
-        t_ref[0, e] = pltpu.roll(w, TILE, 1, stride=1, stride_axis=0)[:, :TILE].astype(t_ref.dtype)
+        base = TILE * (span - e)
+        t_ref[0, e] = rolled[:, base:base + TILE].astype(t_ref.dtype)
 
 def toeplitz_tiles(u):
     heads, width = u.shape
@@ -518,7 +519,7 @@
         self.send_in_plane()
         return main
 
-    def b(self, main):
+    def b(self, main, *fill):
         if not self.pairs:
             return main
         main = tie(main, self.by_x, self.by_y, self.near_twin)
@@ -526,15 +527,15 @@
         self.low = Held(self.plan.exchange(self.by_y.value[:half], "s"))
         self.high = Held(self.plan.exchange(self.by_x.value[half:], "y"))
         self.x_twin, self.y_twin = self.send(self.by_x, "core"), self.send(self.by_y, "core")
-        return tie(main, self.x_twin, self.y_twin)
-
-    def c(self, main, between=None):
+        return tie(main, self.x_twin, self.y_twin, *fill)
+
+    def c(self, main, between=None, fill=()):
         if not self.pairs:
             return (between(main) if between else main), self.near.value
         plan = self.plan
         main = tie(main, self.low, self.high)
         twins = [self.send(p, "core") for p in (self.low, self.high)]
-        main = tie(main, *twins)
+        main = tie(main, *twins, *fill)
         main = between(main) if between else main
         low_twin, high_twin = [t.value for t in twins]
         half = self.low.value.shape[0]
@@ -719,13 +720,13 @@
     return (normed_mlp,) + gelu_pair(matmul_rows(normed_mlp, w_inner))
 
 
-def backward(plan, grad_out, layers, pos, bias, blk, perms, table, output_half):
+def backward(plan, grad_out, layers, pos, bias, blk, table, output_half):
     low, f32 = jnp.bfloat16, jnp.float32
     previous = None
     results, diags = [], []
     for weights, saved, orders in layers:
         attn_gain, w_qkv, w_output, mlp_gain, w_inner, w_outer = weights
-        x, normed, queries, keys, values, context, log_total, attended, normed_mlp, hidden, slope = saved
+        x, queries, keys, values, context, log_total, attended, hidden, slope, left_m, left_c, n_qk, n_v = saved
         width = x.shape[1]
         grad_low = grad_out.astype(low)
         wide = hidden.shape[1]
@@ -750,7 +751,6 @@
         grad_pre, grad_attended, attn_low, grad_mlp_gain = mlp_back(grad_out, attended, mlp_gain, w_outer, w_inner, slope)
         late = [previous.qk.far, previous.ov.far] if previous else [arrived]
         grad_pre = tie(grad_pre, outer.other, *late)
-        left_m = matmul_rows(normed_mlp, perms[orders[0]]).astype(low)
         inner = Chain(plan, rows_of((left_m, grad_pre, 0, wide // 1024)), orders[0], width)
         late = []
         if previous:
@@ -763,20 +763,16 @@
             previous.qk.send_three()
             previous.ov.send_three()
             previous.sum_mlp(plan)
-        late = [previous.qk.side, previous.ov.side] if previous else []
-        attn_low = tie(attn_low, inner.other, *late)
-        late = [previous.qk.close(), previous.ov.close()] if previous else []
-        attn_low = tie(attn_low, inner.two(), *late)
+        attn_low = tie(attn_low, inner.other)
+        attn_low = tie(attn_low, inner.two())
         inner.send_two()
-        if previous:
-            previous.sum_attn(plan)
         grad_context = matmul_back(attn_low, w_output).astype(low)
         ready = [outer.near(), inner.near()]
-        left_c = matmul_rows(context, perms[orders[3]]).astype(low)
-        left_n = {o: matmul_rows(normed, perms[o]).astype(low) for o in orders[2:]}
-        left_c, n_q, n_v = Held(left_c), Held(left_n[orders[2]]), Held(left_n[orders[3]])
-        grad_context = tie(grad_context, *ready, left_c, n_q, n_v)
-        left_c, left_n = left_c.value, {orders[2]: n_q.value, orders[3]: n_v.value}
+        late = [previous.qk.side, previous.ov.side] if previous else []
+        grad_context = tie(grad_context, *ready, *late)
+        if previous:
+            grad_context = tie(grad_context, previous.qk.close(), previous.ov.close())
+            previous.sum_attn(plan)
         grad_query, dk, dv, diag = attn_bwd(pos, queries, grad_context, context, log_total, keys, values, bias, blk, 0, 1)
         late = [previous.mlp_sum] if previous else []
         last = tie(dv[-1], outer.far, inner.far, *late)
@@ -788,8 +784,8 @@
         outer.send_three()
         inner.send_three()
         tiles = width // 1024
-        qk = Chain(plan, rows_of((left_n[orders[2]], grad_query, 0, tiles), (left_n[orders[2]], grad_k, 0, tiles)), orders[2], width)
-        ov = Chain(plan, rows_of((left_c, attn_low, 0, tiles), (left_n[orders[3]], grad_v, 0, tiles)), orders[3], width)
+        qk = Chain(plan, rows_of((n_qk, grad_query, 0, tiles), (n_qk, grad_k, 0, tiles)), orders[2], width)
+        ov = Chain(plan, rows_of((left_c, attn_low, 0, tiles), (n_v, grad_v, 0, tiles)), orders[3], width)
         grad_v = tie(grad_v, qk.one(), ov.one())
         qk.send_one()
         ov.send_one()
@@ -855,6 +851,12 @@
     row = jnp.arange(blk, dtype=jnp.int32)
     row_pos = jnp.concatenate([row + pos[1] * TILE, row + pos[2] * TILE])
     row_valid = (row_pos < length).astype(f32)[:, None]
+
+    xy, yx = ("x", "y"), ("y", "x")
+    perms = {o: plan.permutation(o, width) for o in (xy, yx)}
+
+    def permuted(rows_low, order):
+        return Held(matmul_rows(rows_low, perms[order]).astype(low))
 
     shards = (
         jnp.concatenate([one[1], one[2], one[3], one[4], small], axis=1),
@@ -898,14 +900,17 @@
     queries_one = qkv[:, :width]
     keys_one, values_one = [p[:, :width] for p in kv], [p[:, width:] for p in kv]
     context_one, log_one = attn_fwd(pos, queries_one, keys_one, values_one, bias, blk)
-    context_one, w_inner_one = inner_1.c(context_one, lambda main: attn_2.a(outer_1.b(main), outer_2))
+    n_yx_one, n_xy_one = permuted(normed_one, yx), permuted(normed_one, xy)
+    context_one, w_inner_one = inner_1.c(context_one, lambda main: attn_2.a(outer_1.b(main, n_xy_one), outer_2), [n_yx_one])
+    c_one = permuted(context_one, xy)
     attended_one = x_one + matmul_rows(context_one, first[:, 3 * width:4 * width])
     normed_mlp_one, hidden_one, slope_one = widen(attended_one, gain[1:2], w_inner_one)
     slope_one = Held(slope_one)
     hidden_one = tie(hidden_one, slope_one)
     slope_one = slope_one.value
-    hidden_one, w_outer_one = outer_1.c(hidden_one)
-    hidden_one = attn_2.b(hidden_one)
+    m_one = permuted(normed_mlp_one, xy)
+    hidden_one, w_outer_one = outer_1.c(hidden_one, None, [c_one])
+    hidden_one = attn_2.b(hidden_one, m_one)
     hidden_one = inner_2.a(hidden_one)
     x_two = attended_one + matmul_rows(hidden_one, w_outer_one)
     x_two, third = attn_2.c(x_two)
@@ -916,32 +921,33 @@
     queries_two = qkv[:, :width]
     keys_two, values_two = [p[:, :width] for p in kv], [p[:, width:] for p in kv]
     context_two, log_two = attn_fwd(pos, queries_two, keys_two, values_two, bias, blk)
-    context_two, w_inner_two = inner_2.c(context_two)
-    context_two = outer_2.b(context_two)
+    n_yx_two, n_xy_two = permuted(normed_two, yx), permuted(normed_two, xy)
+    context_two, w_inner_two = inner_2.c(context_two, None, [n_yx_two])
+    context_two = outer_2.b(context_two, n_xy_two)
+    c_two = permuted(context_two, xy)
     attended_two = x_two + matmul_rows(context_two, third[:, 3 * width:])
     normed_mlp_two, hidden_two, slope_two = widen(attended_two, gain[3:4], w_inner_two)
     slope_two = Held(slope_two)
     hidden_two = tie(hidden_two, slope_two)
     slope_two = slope_two.value
-    hidden_two, w_outer_two = outer_2.c(hidden_two)
+    hidden_two, w_outer_two = outer_2.c(hidden_two, None, [c_two])
+    m_two = permuted(normed_mlp_two, xy)
     final = attended_two + matmul_rows(hidden_two, w_outer_two)
     output_rows = (final * row_valid).astype(low)
     grad_out = cotangent.astype(f32) * row_valid
 
     weights_one = (gain[0:1], first, first[:, 3 * width:4 * width], gain[1:2], w_inner_one, w_outer_one)
     weights_two = (gain[2:3], third, third[:, 3 * width:], gain[3:4], w_inner_two, w_outer_two)
-    saved_one = (x, normed_one, queries_one, keys_one, values_one, context_one, log_one, attended_one, normed_mlp_one, hidden_one, slope_one)
-    saved_two = (x_two, normed_two, queries_two, keys_two, values_two, context_two, log_two, attended_two, normed_mlp_two, hidden_two, slope_two)
-
-    xy, yx = ("x", "y"), ("y", "x")
-    perms = {o: plan.permutation(o, width) for o in (xy, yx)}
+    saved_one = (x, queries_one, keys_one, values_one, context_one, log_one, attended_one, hidden_one, slope_one, m_one.value, c_one.value, n_yx_one.value, n_xy_one.value)
+    saved_two = (x_two, queries_two, keys_two, values_two, context_two, log_two, attended_two, hidden_two, slope_two, m_two.value, c_two.value, n_yx_two.value, n_xy_two.value)
+
     depth = one[7].shape[0]
     step = TILE if depth % TILE == 0 else depth
-    blocks = jnp.arange(saved_one[9].shape[1] // step, dtype=jnp.int32)
+    blocks = jnp.arange(hidden_one.shape[1] // step, dtype=jnp.int32)
     per = depth // step
     table = {o: plan.block_of(o, blocks // per) * per + blocks % per for o in (xy, yx)}
     layers = [(weights_two, saved_two, (xy, yx, yx, xy)), (weights_one, saved_one, (xy, yx, yx, xy))]
-    grad_state, sums, diags, arrived = backward(plan, grad_out, layers, pos, bias, blk, perms, table, output_rows[blk:])
+    grad_state, sums, diags, arrived = backward(plan, grad_out, layers, pos, bias, blk, table, output_rows[blk:])
     output = plan.in_order(output_rows[:blk], arrived)
     grads_two, grads_one = sums[0].grads(), sums[1].grads()
     input_grad = plan.from_sequences(grad_state.astype(low))

time: 746 us -> 743 us (level)
  waiting for transfers between devices: 135 us -> 127 us
    ppermute x88, waiting for transfers between devices: 109 us -> 101 us  [exchange(): return lax.ppermute(piece, name, SWAP)]
    unnamed x314 -> x286, local copies, waits for them, and re-layouts: 41 us -> 43.9 us
  transfers between devices with their start and end apart: 103 -> 103, of which waited for: 42 -> 36; matrix products, arithmetic and copies ran while one was open for 21% -> 21% of each run, Pallas kernels for 37% -> 38%
where the time goes in v5:
time: 743 us; the launch traced here: 731 us
  Pallas kernels  319 us (43%)
  waiting for transfers between devices  127 us (17%)
  local copies, waits for them, and re-layouts  97.7 us (13%)
  matrix products  92.5 us (12%)
  starting transfers between devices  61.4 us (8%)
  other arithmetic  17.4 us (2%)
  between operations  16.4 us (2%)
    ppermute x88, waiting for transfers between devices, exchange(): return lax.ppermute(piece, name, SWAP)  101 us
    dot_general x17, matrix products, matmul_rows(): return jnp.dot(left, right, preferred_element_type=jnp.float32)  83.4 us
    pallas_call x24, Pallas kernels, grad_rows(): pl.pallas_call(functools.partial(grad_kernel, lefts, starts, add is not N...  76.6 us
    pallas_call x2, Pallas kernels, attn_bwd(): pl.pallas_call(functools.partial(attn_bwd_kernel, parts, chunk, blk), gri...  71.1 us
    ppermute x88, starting transfers between devices, exchange(): return lax.ppermute(piece, name, SWAP)  55.3 us
    pallas_call x6, Pallas kernels, assemble(): pl.pallas_call(functools.partial(assemble_kernel, steps, depth), grid_spe...  48 us
    unnamed x286, local copies, waits for them, and re-layouts  43.9 us
    pallas_call x2, Pallas kernels, attn_fwd(): pl.pallas_call(functools.partial(attn_fwd_kernel, parts, chunk, blk), gri...  38.9 us
  transfers between devices with their start and end apart: 103, of which 36 were waited for; matrix products, arithmetic and copies ran while one was open for 21% of the time, Pallas kernels for 38%

profile of v5, /device:TPU:0, one launch (start us, length us, event | category | flops | bytes accessed | tf_op | source)
XLA Modules:
  0.0 731.2 jit_solution(18176272629451105704)
XLA Ops:
  18.6 11.3 %collective-permute-done = bf16[256,1024]{1,0:T(8,128)(2,1)S(1)} collective-permute-done((bf16[256,1024]{1,0:T(8,128)(2,1)S(1)}, bf16[256,1024]{1,0:T(8,128)(2,1)S(1)}, u32[]{:S(2)}, u32[]{:S(2)}) %collective-permute-start) | collective-permute-done | bytes 524320 | tf_op jit(solution)/shard_map/ppermute | solution.py:396
  30.0 10.3 %collective-permute-done.1 = bf16[256,1024]{1,0:T(8,128)(2,1)S(1)} collective-permute-done((bf16[256,1024]{1,0:T(8,128)(2,1)S(1)}, bf16[256,1024]{1,0:T(8,128)(2,1)S(1)}, u32[]{:S(2)}, u32[]{:S(2)}) %collective-permute-start.1) | collective-permute-done | bytes 524320 | tf_op jit(solution)/shard_map/ppermute | solution.py:396
  47.2 22.7 %collective-permute-done.2.refs_2_ = bf16[128,4224]{1,0:T(8,128)(2,1)} collective-permute-done((bf16[128,4224]{1,0:T(8,128)(2,1)}, bf16[128,4224]{1,0:T(8,128)(2,1)}, u32[]{:S(2)}, u32[]{:S(2)}) %collective-permute-start.2) | collective-permute-done | bytes 1081376 | tf_op jit(solution)/shard_map/ppermute | solution.py:396
  80.4 10.0 %collective-permute-done.7.refs_6_ = bf16[64,4224]{1,0:T(8,128)(2,1)S(1)} collective-permute-done((bf16[64,4224]{1,0:T(8,128)(2,1)S(1)}, bf16[64,4224]{1,0:T(8,128)(2,1)S(1)}, u32[]{:S(2)}, u32[]{:S(2)}) %collective-permute-start.7) | collective-permute-done | bytes 540704 | tf_op jit(solution)/shard_map/ppermute | solution.py:396
  95.4 8.0 %assemble.6.w_ref = bf16[1024,4224]{1,0:T(8,128)(2,1)} custom-call(s32[10]{0:T(128)S(1)} %pad_add_fusion.1.table_ref, bf16[128,4224]{1,0:T(8,128)(2,1)S(1)} %copy-done.75, bf16[128,4224]{1,0:T(8,128)(2,1)} %copy-done.113, bf16[128,4224]{1,0:T(8,128)(2,1)} %collective-permute-done.2.refs_2_, bf16[128,4224]{1,0:T(8,128)(2,1)} %collective-permute-done.5.refs_3_, ...), custom_call_target="tpu_custom_call" | custom-call | flops 1024 | bytes 1024 | tf_op jit(solution)/shard_map/assemble/pallas_call | solution.py:471
  131.2 10.2 %toeplitz.1.refs_4_ = bf16[16,15,128,128]{3,2,1,0:T(8,128)(2,1)} custom-call(f32[16,1,2048]{2,1,0:T(1,128)} %reshape.119.u_ref), custom_call_target="tpu_custom_call" | custom-call | flops 1024 | bytes 1024 | tf_op jit(solution)/shard_map/toeplitz/pallas_call | solution.py:30
  148.3 19.5 %attn_fwd.2 = (bf16[512,1024]{1,0:T(8,128)(2,1)S(1)}, f32[8,2,512]{2,1,0:T(2,128)S(1)}) custom-call(s32[7]{0:T(128)S(1)} %stack.74.pos_ref, bf16[512,1024]{1,0:T(8,128)(2,1)S(1)} %slice.282.q_ref, bf16[512,1024]{1,0:T(8,128)(2,1)S(1)} %get-tuple-element.519.refs_0_, bf16[512,1024]{1,0:T(8,128)(2,1)S(1)} %get-tuple-element.523.refs_1_, ...), custom_call_target="tpu_custom_call" | custom-call | flops 1024 | bytes 1024 | tf_op jit(solution)/shard_map/attn_fwd/pallas_call | solution.py:116
  180.9 8.7 %assemble.7.inner_ref = bf16[1024,4096]{1,0:T(8,128)(2,1)} custom-call(s32[10]{0:T(128)S(1)} %pad_add_fusion.1.table_ref, bf16[128,4096]{1,0:T(8,128)(2,1)S(1)} %copy-done.77, bf16[128,4096]{1,0:T(8,128)(2,1)} %collective-permute-done.13.refs_1_, bf16[128,4096]{1,0:T(8,128)(2,1)} %collective-permute-done.11.refs_2_, bf16[128,4096]{1,0:T(8,128)(2,1)} %copy-done.114, ...), custom_call_target="tpu_custom_call" | custom-call | flops 1024 | bytes 1024 | tf_op jit(solution)/shard_map/assemble/pallas_call | solution.py:471
  194.8 11.3 %fusion.7 = (bf16[512,4096]{1,0:T(8,128)(2,1)}, bf16[512,4096]{1,0:T(8,128)(2,1)}) fusion(bf16[1024,4096]{1,0:T(8,128)(2,1)S(1)} %copy-done.101, f32[512,1024]{1,0:T(8,128)S(1)} %get-tuple-element.583.value_ref, f32[1024]{0:T(1024)S(1)} %bitcast.86, f32[512]{0:T(512)S(1)} %add_rsqrt_fusion.2), kind=kOutput, calls=%fused_computation.15 | convolution fusion | flops 4334288896 | bytes 18880512 | tf_op jit(solution)/shard_map/dot_general | solution.py:240
  211.1 8.8 %assemble.8.outer_ref = bf16[4096,1024]{1,0:T(8,128)(2,1)} custom-call(s32[10]{0:T(128)S(1)} %pad_add_fusion.1.table_ref, bf16[512,1024]{1,0:T(8,128)(2,1)} %all-gather.11.cloned.1.call-done.refs_0_, bf16[512,1024]{1,0:T(8,128)(2,1)} %collective-permute-done.23.refs_1_, bf16[512,1024]{1,0:T(8,128)(2,1)} %collective-permute-done.21.refs_2_, ...), custom_call_target="tpu_custom_call" | custom-call | flops 1024 | bytes 1024 | tf_op jit(solution)/shard_map/assemble/pallas_call | solution.py:471
  230.4 9.7 %convolution_add_fusion.value_ref = f32[512,1024]{1,0:T(8,128)S(1)} fusion(f32[512,1024]{1,0:T(8,128)} %copy-done.109, bf16[512,4096]{1,0:T(8,128)(2,1)} %get-tuple-element.333.refs_0_.refs_1_.refs_2_.refs_3_, bf16[4096,1024]{1,0:T(8,128)(2,1)} %assemble.8.outer_ref), kind=kOutput, calls=%fused_computation.88 | convolution fusion | flops 4295491584 | bytes 16777216 | tf_op jit(solution)/shard_map/dot_general | solution.py:240
  245.4 8.3 %assemble.9.w_ref = bf16[1024,4096]{1,0:T(8,128)(2,1)} custom-call(s32[10]{0:T(128)S(1)} %pad_add_fusion.1.table_ref, bf16[128,4096]{1,0:T(8,128)(2,1)S(1)} %copy-done.78, bf16[128,4096]{1,0:T(8,128)(2,1)} %copy-done.115, bf16[128,4096]{1,0:T(8,128)(2,1)} %collective-permute-done.30.refs_2_, bf16[128,4096]{1,0:T(8,128)(2,1)} %collective-permute-done.33.refs_3_, ...), custom_call_target="tpu_custom_call" | custom-call | flops 1024 | bytes 1024 | tf_op jit(solution)/shard_map/assemble/pallas_call | solution.py:471
  254.2 8.0 %fusion.23 = bf16[512,3072]{1,0:T(8,128)(2,1)} fusion(bf16[512,1024]{1,0:T(8,128)(2,1)S(1)} %multiply_convert_fusion.4, bf16[1024,4096]{1,0:T(8,128)(2,1)} %assemble.9.w_ref), kind=kOutput, calls=%fused_computation.49 | convolution fusion | flops 3222798336 | bytes 10485760 | tf_op jit(solution)/shard_map/dot_general | solution.py:240
  281.4 19.5 %attn_fwd.3 = (bf16[512,1024]{1,0:T(8,128)(2,1)S(1)}, f32[8,2,512]{2,1,0:T(2,128)S(1)}) custom-call(s32[7]{0:T(128)S(1)} %stack.74.pos_ref, bf16[512,1024]{1,0:T(8,128)(2,1)S(1)} %get-tuple-element.517.q_ref, bf16[512,1024]{1,0:T(8,128)(2,1)S(1)} %get-tuple-element.516.refs_0_, bf16[512,1024]{1,0:T(8,128)(2,1)S(1)} %get-tuple-element.521.refs_1_, ...), custom_call_target="tpu_custom_call" | custom-call | flops 1024 | bytes 1024 | tf_op jit(solution)/shard_map/attn_fwd/pallas_call | solution.py:116
  324.7 11.7 %fusion.15 = (bf16[512,4096]{1,0:T(8,128)(2,1)}, bf16[512,4096]{1,0:T(8,128)(2,1)S(1)}) fusion(bf16[1024,4096]{1,0:T(8,128)(2,1)S(1)} %copy-done.102, f32[512,1024]{1,0:T(8,128)S(1)} %get-tuple-element.585.value_ref, f32[1024]{0:T(1024)S(1)} %bitcast.88, f32[512]{0:T(512)S(1)} %add_rsqrt_fusion), kind=kOutput, calls=%fused_computation.23 | convolution fusion | flops 4334288896 | bytes 18880512 | tf_op jit(solution)/shard_map/dot_general | solution.py:240
  347.2 8.4 %multiply_convert_fusion.2 = bf16[512,1024]{1,0:T(8,128)(2,1)S(1)} fusion(f32[512,1024]{1,0:T(8,128)} %copy-done.111, bf16[512,4096]{1,0:T(8,128)(2,1)S(1)} %get-tuple-element.380.refs_0_.refs_1_.refs_2_.refs_3_, bf16[4096,1024]{1,0:T(8,128)(2,1)} %assemble.11.outer_ref, f32[512]{0:T(512)S(1)} %fusion.74), kind=kOutput, calls=%fused_computation.72 | convolution fusion | flops 4296540160 | bytes 15730688 | tf_op jit(solution)/shard_map/dot_general | solution.py:240
  364.5 16.3 %mlp_back.2 = (bf16[512,4096]{1,0:T(8,128)(2,1)}, f32[512,1024]{1,0:T(8,128)S(1)}, bf16[512,1024]{1,0:T(8,128)(2,1)S(1)}, f32[1,1024]{1,0:T(1,128)S(1)}) custom-call(f32[512,1024]{1,0:T(8,128)S(1)} %copy-done.57, f32[512,1024]{1,0:T(8,128)} %copy-done.111, f32[1,1024]{1,0:T(1,128)S(1)} %copy-done.94, bf16[4096,1024]{1,0:T(8,128)(2,1)} %assemble.11.outer_ref, ...), custom_call_target="tpu_custom_call" | custom-call | flops 1024 | bytes 1024 | tf_op jit(solution)/shard_map/mlp_back/pallas_call | solution.py:290
  408.5 35.4 %attn_bwd.2 = (bf16[512,1024]{1,0:T(8,128)(2,1)S(1)}, bf16[512,1024]{1,0:T(8,128)(2,1)S(1)}, bf16[512,1024]{1,0:T(8,128)(2,1)S(1)}, bf16[512,1024]{1,0:T(8,128)(...) custom-call(s32[7]{0:T(128)S(1)} %copy-done.96, bf16[512,1024]{1,0:T(8,128)(2,1)} %copy-done.64, ...), custom_call_target="tpu_custom_call" | custom-call | flops 21474836480 | bytes 12582912 | tf_op jit(solution)/shard_map/attn_bwd/pallas_call | solution.py:219
  460.6 8.0 %project_back.2 = (f32[512,1024]{1,0:T(8,128)S(1)}, f32[1,1024]{1,0:T(1,128)S(1)}) custom-call(f32[512,1024]{1,0:T(8,128)} %copy-done.66, f32[512,1024]{1,0:T(8,128)} %copy-done.103, f32[1,1024]{1,0:T(1,128)S(1)} %copy-done.89, bf16[512,1024]{1,0:T(8,128)(2,1)S(1)} %get-tuple-element.399.refs_1_.q_ref, bf16[512,1024]{1,0:T(8,128)(2,1)S(1)} %add_rows.21.refs_3_.k_ref, ...), custom_call_target="tpu_custom_call" | custom-call | flops 1024 | bytes 1024 | tf_op jit(solution)/shard_map/project_back/pallas_call | solution.py:335
  490.9 16.6 %mlp_back.3 = (bf16[512,4096]{1,0:T(8,128)(2,1)}, f32[512,1024]{1,0:T(8,128)S(1)}, bf16[512,1024]{1,0:T(8,128)(2,1)S(1)}, f32[1,1024]{1,0:T(1,128)S(1)}) custom-call(f32[512,1024]{1,0:T(8,128)S(1)} %get-tuple-element.426.grad_ref, f32[512,1024]{1,0:T(8,128)} %copy-done.109, f32[1,1024]{1,0:T(1,128)S(1)} %copy-done.93, bf16[4096,1024]{1,0:T(8,128)(2,1)} %assemble.8.outer_ref, ...), custom_call_target="tpu_custom_call" | custom-call | flops 1024 | bytes 1024 | tf_op jit(solution)/shard_map/mlp_back/pallas_call | solution.py:290
  559.3 35.7 %attn_bwd.3 = (bf16[512,1024]{1,0:T(8,128)(2,1)S(1)}, bf16[512,1024]{1,0:T(8,128)(2,1)S(1)}, bf16[512,1024]{1,0:T(8,128)(2,1)}, bf16[512,1024]{1,0:T(8,128)(2,1)...) custom-call(s32[7]{0:T(128)S(1)} %copy-done.96, bf16[512,1024]{1,0:T(8,128)(2,1)} %copy-done.58, ...), custom_call_target="tpu_custom_call" | custom-call | flops 21474836480 | bytes 12582912 | tf_op jit(solution)/shard_map/attn_bwd/pallas_call | solution.py:219
  622.0 8.6 %project_back.3 = (f32[512,1024]{1,0:T(8,128)}, f32[1,1024]{1,0:T(1,128)S(1)}) custom-call(f32[512,1024]{1,0:T(8,128)} %copy-done.68, bf16[512,1024]{1,0:T(8,128)(2,1)S(1)} %copy-done.23, f32[1,1024]{1,0:T(1,128)S(1)} %copy-done.91, bf16[512,1024]{1,0:T(8,128)(2,1)S(1)} %copy-done.16, bf16[512,1024]{1,0:T(8,128)(2,1)S(1)} %add_rows.31.refs_3_.k_ref, ...), custom_call_target="tpu_custom_call" | custom-call | flops 1024 | bytes 1024 | tf_op jit(solution)/shard_map/project_back/pallas_call | solution.py:335
  659.6 14.1 %collective-permute-done.81.refs_1_ = bf16[256,2048]{1,0:T(8,128)(2,1)} collective-permute-done((bf16[256,2048]{1,0:T(8,128)(2,1)}, bf16[256,2048]{1,0:T(8,128)(2,1)}, u32[]{:S(2)}, u32[]{:S(2)}) %collective-permute-start.81) | collective-permute-done | bytes 1048608 | tf_op jit(solution)/shard_map/ppermute | solution.py:396
  703.5 7.9 %collective-permute-done.88 = f32[4608]{0:T(1024)S(1)} collective-permute-done((f32[4608]{0:T(1024)S(1)}, f32[4608]{0:T(1024)S(1)}, u32[]{:S(2)}, u32[]{:S(2)}) %collective-permute-start.88) | collective-permute-done | bytes 18464 | tf_op jit(solution)/shard_map/ppermute | solution.py:410
  (647 shorter events, 385.9 us)
Async XLA Ops:
  7.2 37.0 %all-gather.7.cloned.1.call-start = ((), (), s32[]{:S(2)}) async-start(), calls=%async_computation.4 | async-start | bytes 1351680 | tf_op jit(solution)/shard_map/all_gather | solution.py:506
  12.9 65.4 %all-gather.9.cloned.1.call-start = ((), (), s32[]{:S(2)}) async-start(), calls=%async_computation.5 | async-start | bytes 1310720 | tf_op jit(solution)/shard_map/all_gather | solution.py:506
  47.2 70.5 %all-gather.11.cloned.1.call-start = ((), (), s32[]{:S(2)}) async-start(), calls=%async_computation.6 | async-start | bytes 1310720 | tf_op jit(solution)/shard_map/all_gather | solution.py:506
  78.2 111.5 %all-gather.13.cloned.1.call-start = ((), (), s32[]{:S(2)}) async-start(), calls=%async_computation.7 | async-start | bytes 1310720 | tf_op jit(solution)/shard_map/all_gather | solution.py:506
  78.3 34.9 %collective-permute-start.11 = (bf16[128,4096]{1,0:T(8,128)(2,1)}, bf16[128,4096]{1,0:T(8,128)(2,1)}, u32[]{:S(2)}, u32[]{:S(2)}) collective-permute-start(bf16[128,4096]{1,0:T(8,128)(2,1)} %all-gather.9.cloned.1.call-done.refs_0_), channel_id=1, source_target_pairs={{0,2},{2,0},{1,3},{3,1},{4,6},{6,4},{5,7},{7,5},{8,10},{10,8},{9,1... | collective-permute-start | bytes 3145736 | tf_op jit(solution)/shard_map/ppermute | solution.py:396
  115.4 113.2 %all-gather.15.cloned.1.call-start = ((), (), s32[]{:S(2)}) async-start(), calls=%async_computation.8 | async-start | bytes 1310720 | tf_op jit(solution)/shard_map/all_gather | solution.py:506
  126.4 42.4 %collective-permute-start.17 = (bf16[64,4096]{1,0:T(8,128)(2,1)S(1)}, bf16[64,4096]{1,0:T(8,128)(2,1)}, u32[]{:S(2)}, u32[]{:S(2)}) collective-permute-start(bf16[64,4096]{1,0:T(8,128)(2,1)S(1)} %get-tuple-element.553.refs_4_), channel_id=1, source_target_pairs={{0,2},{2,0},{1,3},{3,1},{4,6},{6,4},{5,7},{7,5},{8,10},{10,8},{9,1... | collective-permute-start | bytes 1572872 | tf_op jit(solution)/shard_map/ppermute | solution.py:396
  127.9 40.8 %collective-permute-start.18 = (bf16[64,4096]{1,0:T(8,128)(2,1)}, bf16[64,4096]{1,0:T(8,128)(2,1)}, u32[]{:S(2)}, u32[]{:S(2)}) collective-permute-start(bf16[64,4096]{1,0:T(8,128)(2,1)} %slice.289), channel_id=1, source_target_pairs={{0,4},{4,0},{1,5},{5,1},{2,6},{6,2},{3,7},{7,3},{8,12},{12,8},{9,1... | collective-permute-start | bytes 1572872 | tf_op jit(solution)/shard_map/ppermute | solution.py:396
  130.1 42.0 %collective-permute-start.21 = (bf16[512,1024]{1,0:T(8,128)(2,1)}, bf16[512,1024]{1,0:T(8,128)(2,1)}, u32[]{:S(2)}, u32[]{:S(2)}) collective-permute-start(bf16[512,1024]{1,0:T(8,128)(2,1)} %all-gather.11.cloned.1.call-done.refs_0_), channel_id=1, source_target_pairs={{0,2},{2,0},{1,3},{3,1},{4,6},{6,4},{5,7},{7,5},{8,10},{10,8},{9,1... | collective-permute-start | bytes 3145736 | tf_op jit(solution)/shard_map/ppermute | solution.py:396
  130.6 41.5 %collective-permute-start.22 = (bf16[512,1024]{1,0:T(8,128)(2,1)}, bf16[512,1024]{1,0:T(8,128)(2,1)}, u32[]{:S(2)}, u32[]{:S(2)}) collective-permute-start(bf16[512,1024]{1,0:T(8,128)(2,1)} %all-gather.11.cloned.1.call-done.refs_0_), channel_id=1, source_target_pairs={{0,4},{4,0},{1,5},{5,1},{2,6},{6,2},{3,7},{7,3},{8,12},{12,8},{9,1... | collective-permute-start | bytes 3145736 | tf_op jit(solution)/shard_map/ppermute | solution.py:396
  171.8 96.8 %all-gather.17.cloned.1.call-start = ((), (), s32[]{:S(2)}) async-start(), calls=%async_computation.9 | async-start | bytes 1310720 | tf_op jit(solution)/shard_map/all_gather | solution.py:506
  223.0 376.3 %reduce-scatter.5.cloned.1.call-start = ((), (), s32[]{:S(2)}) async-start(), calls=%async_computation.10 | async-start | bytes 2621440 | tf_op jit(solution)/shard_map/reduce_scatter | solution.py:401
  228.6 34.2 %collective-permute-start.39 = (bf16[128,4096]{1,0:T(8,128)(2,1)}, bf16[128,4096]{1,0:T(8,128)(2,1)}, u32[]{:S(2)}, u32[]{:S(2)}) collective-permute-start(bf16[128,4096]{1,0:T(8,128)(2,1)} %all-gather.15.cloned.1.call-done.refs_0_), channel_id=1, source_target_pairs={{0,2},{2,0},{1,3},{3,1},{4,6},{6,4},{5,7},{7,5},{8,10},{10,8},{9,1... | collective-permute-start | bytes 3145736 | tf_op jit(solution)/shard_map/ppermute | solution.py:396
  229.6 34.5 %collective-permute-start.40 = (bf16[128,4096]{1,0:T(8,128)(2,1)}, bf16[128,4096]{1,0:T(8,128)(2,1)}, u32[]{:S(2)}, u32[]{:S(2)}) collective-permute-start(bf16[128,4096]{1,0:T(8,128)(2,1)} %all-gather.15.cloned.1.call-done.refs_0_), channel_id=1, source_target_pairs={{0,4},{4,0},{1,5},{5,1},{2,6},{6,2},{3,7},{7,3},{8,12},{12,8},{9,1... | collective-permute-start | bytes 3145736 | tf_op jit(solution)/shard_map/ppermute | solution.py:396
  230.4 33.7 %collective-permute-start.41 = (bf16[128,4096]{1,0:T(8,128)(2,1)}, bf16[128,4096]{1,0:T(8,128)(2,1)}, u32[]{:S(2)}, u32[]{:S(2)}) collective-permute-start(bf16[128,4096]{1,0:T(8,128)(2,1)} %all-gather.15.cloned.1.call-done.refs_0_), channel_id=1, source_target_pairs={{0,1},{1,0},{2,3},{3,2},{4,5},{5,4},{6,7},{7,6},{8,9},{9,8},{10,11... | collective-permute-start | bytes 3145736 | tf_op jit(solution)/shard_map/ppermute | solution.py:396
  277.3 34.9 %collective-permute-start.49 = (bf16[512,1024]{1,0:T(8,128)(2,1)S(1)}, bf16[512,1024]{1,0:T(8,128)(2,1)}, u32[]{:S(2)}, u32[]{:S(2)}) collective-permute-start(bf16[512,1024]{1,0:T(8,128)(2,1)S(1)} %copy-done.79), channel_id=1, source_target_pairs={{0,2},{2,0},{1,3},{3,1},{4,6},{6,4},{5,7},{7,5},{8,10},{10,8},{9,1... | collective-permute-start | bytes 3145736 | tf_op jit(solution)/shard_map/ppermute | solution.py:396
  278.8 33.8 %collective-permute-start.50 = (bf16[512,1024]{1,0:T(8,128)(2,1)S(1)}, bf16[512,1024]{1,0:T(8,128)(2,1)}, u32[]{:S(2)}, u32[]{:S(2)}) collective-permute-start(bf16[512,1024]{1,0:T(8,128)(2,1)S(1)} %copy-done.79), channel_id=1, source_target_pairs={{0,4},{4,0},{1,5},{5,1},{2,6},{6,2},{3,7},{7,3},{8,12},{12,8},{9,1... | collective-permute-start | bytes 3145736 | tf_op jit(solution)/shard_map/ppermute | solution.py:396
  395.4 48.6 %collective-permute-start.61 = (bf16[1024,1024]{1,0:T(8,128)(2,1)S(1)}, bf16[1024,1024]{1,0:T(8,128)(2,1)S(1)}, u32[]{:S(2)}, u32[]{:S(2)}) collective-permute-start(bf16[1024,1024]{1,0:T(8,128)(2,1)S(1)} %grad_rows.25), channel_id=1, source_target_pairs={{0,4},{4,0},{1,5},{5,1},{2,6},{6,2},{3,7},{7,3},{8,12},{12,8},{9,1... | collective-permute-start | bytes 6291464 | tf_op jit(solution)/shard_map/ppermute | solution.py:396
  401.0 48.0 %collective-permute-start.62 = (bf16[256,4096]{1,0:T(8,128)(2,1)}, bf16[256,4096]{1,0:T(8,128)(2,1)}, u32[]{:S(2)}, u32[]{:S(2)}) collective-permute-start(bf16[256,4096]{1,0:T(8,128)(2,1)} %grad_rows.27), channel_id=1, source_target_pairs={{0,2},{2,0},{1,3},{3,1},{4,6},{6,4},{5,7},{7,5},{8,10},{10,8},{9,1... | collective-permute-start | bytes 6291464 | tf_op jit(solution)/shard_map/ppermute | solution.py:396
  529.3 166.4 %reduce-scatter.9.cloned.1.call-start = ((), (), s32[]{:S(2)}) async-start(), calls=%async_computation.12 | async-start | bytes 1310720 | tf_op jit(solution)/shard_map/reduce_scatter | solution.py:401
  539.5 58.5 %collective-permute-start.75 = (bf16[1024,1024]{1,0:T(8,128)(2,1)S(1)}, bf16[1024,1024]{1,0:T(8,128)(2,1)S(1)}, u32[]{:S(2)}, u32[]{:S(2)}) collective-permute-start(bf16[1024,1024]{1,0:T(8,128)(2,1)S(1)} %copy-done.74), channel_id=1, source_target_pairs={{0,4},{4,0},{1,5},{5,1},{2,6},{6,2},{3,7},{7,3},{8,12},{12,8},{9,1... | collective-permute-start | bytes 6291464 | tf_op jit(solution)/shard_map/ppermute | solution.py:396
  544.9 54.4 %collective-permute-start.76 = (bf16[256,4096]{1,0:T(8,128)(2,1)}, bf16[256,4096]{1,0:T(8,128)(2,1)}, u32[]{:S(2)}, u32[]{:S(2)}) collective-permute-start(bf16[256,4096]{1,0:T(8,128)(2,1)} %grad_rows.39), channel_id=1, source_target_pairs={{0,2},{2,0},{1,3},{3,1},{4,6},{6,4},{5,7},{7,5},{8,10},{10,8},{9,1... | collective-permute-start | bytes 6291464 | tf_op jit(solution)/shard_map/ppermute | solution.py:396
  619.5 76.2 %reduce-scatter.7.cloned.1.call-start = ((), (), s32[]{:S(2)}) async-start(), calls=%async_computation.11 | async-start | bytes 2621440 | tf_op jit(solution)/shard_map/reduce_scatter | solution.py:401
  648.9 73.5 %reduce-scatter.11.cloned.1.call-start = ((), (), s32[]{:S(2)}) async-start(), calls=%async_computation.13 | async-start | bytes 1310720 | tf_op jit(solution)/shard_map/reduce_scatter | solution.py:401
  (213 other events, 2789.2 us)
Sparse Core Ops, SparseCore 0:
  13.0 31.1 all-gather.6
  47.3 25.8 all-gather.8
  78.3 26.8 all-gather.10
  115.5 27.5 all-gather.12
  171.9 27.6 all-gather.14
  223.1 27.1 all-gather.16
  529.4 42.8 reduce-scatter.4
  619.7 25.4 reduce-scatter.8
  649.1 43.4 reduce-scatter.6
  696.9 25.5 reduce-scatter.10

commit v6 on v5

--- a/solution.py
+++ b/solution.py
@@ -123,7 +123,7 @@
             scratch_shapes=[pltpu.VMEM((keys, q_rows), jnp.float32)],
         ),
         out_shape=[jax.ShapeDtypeStruct((q_rows, width), jnp.bfloat16), jax.ShapeDtypeStruct((heads // 2, 2, q_rows), jnp.float32)],
-        compiler_params=pltpu.CompilerParams(vmem_limit_bytes=48 << 20),
+        compiler_params=pltpu.CompilerParams(vmem_limit_bytes=60 << 20),
         cost_estimate=BRIEF,
         name="attn_fwd",
     )(pos, q, *ks, *vs, bias)
@@ -228,7 +228,7 @@
         out_shape=[jax.ShapeDtypeStruct((q_rows, width), jnp.bfloat16)]
         + [jax.ShapeDtypeStruct((rows, width), jnp.bfloat16)] * (2 * parts)
         + [jax.ShapeDtypeStruct((heads // 2, 2, (span + 1) * TILE), jnp.float32)],
-        compiler_params=pltpu.CompilerParams(vmem_limit_bytes=48 << 20),
+        compiler_params=pltpu.CompilerParams(vmem_limit_bytes=60 << 20),
         cost_estimate=pl.CostEstimate(flops=40 * q_rows * keys * width, bytes_accessed=8 * keys * width + 8 * q_rows * width, transcendentals=heads * q_rows * keys),
         name="attn_bwd",
     )(pos, q, do, o, lse, *ks, *vs, bias)
@@ -306,7 +306,7 @@
             jax.ShapeDtypeStruct((1, width), jnp.float32),
         ],
         scratch_shapes=[pltpu.VMEM((rows, width), jnp.float32), pltpu.VMEM((rows, width), jnp.bfloat16)],
-        compiler_params=pltpu.CompilerParams(vmem_limit_bytes=48 << 20),
+        compiler_params=pltpu.CompilerParams(vmem_limit_bytes=60 << 20),
         cost_estimate=BRIEF,
         name="mlp_back",
     )(grad_out, attended, gain, w_outer, w_inner, slope)
@@ -339,7 +339,7 @@
         out_specs=[whole, line],
         out_shape=[jax.ShapeDtypeStruct((rows, width), jnp.float32), jax.ShapeDtypeStruct((1, width), jnp.float32)],
         scratch_shapes=[pltpu.VMEM((rows, width), jnp.float32)],
-        compiler_params=pltpu.CompilerParams(vmem_limit_bytes=48 << 20),
+        compiler_params=pltpu.CompilerParams(vmem_limit_bytes=60 << 20),
         cost_estimate=BRIEF,
         name="project_back",
     )(grad_attended, x, gain, grad_query, grad_k, grad_v, w)
@@ -477,7 +477,7 @@
             out_specs=pl.BlockSpec((4 * depth, width), lambda i, t: (t[2 + i], 0)),
         ),
         out_shape=jax.ShapeDtypeStruct((at * 4 * depth, width), quads[0][0].dtype),
-        compiler_params=pltpu.CompilerParams(vmem_limit_bytes=48 << 20),
+        compiler_params=pltpu.CompilerParams(vmem_limit_bytes=60 << 20),
         cost_estimate=BRIEF,
         name="assemble",
     )(table, *[r for q in quads for r in q])
@@ -569,7 +569,7 @@
         in_specs=[pl.BlockSpec((tile, width), lambda i, base=first // tile: (base + i, 0)) for _, first in terms],
         out_specs=pl.BlockSpec((tile, width), lambda i: (i, 0)),
         out_shape=jax.ShapeDtypeStruct((count, width), jnp.bfloat16),
-        compiler_params=pltpu.CompilerParams(vmem_limit_bytes=32 << 20),
+        compiler_params=pltpu.CompilerParams(vmem_limit_bytes=60 << 20),
         cost_estimate=BRIEF,
         name="add_rows",
     )(*[array for array, _ in terms])
@@ -704,7 +704,7 @@
             out_specs=pl.BlockSpec((tile_m, tile_n), lambda i, j, t: (i, j)),
         ),
         out_shape=jax.ShapeDtypeStruct((count, width), jnp.bfloat16),
-        compiler_params=pltpu.CompilerParams(vmem_limit_bytes=32 << 20),
+        compiler_params=pltpu.CompilerParams(vmem_limit_bytes=60 << 20),
         cost_estimate=BRIEF,
         name="grad_rows",
     )(jnp.zeros((1,), jnp.int32) if table is None else table, *operands)

time: 743 us -> 806 us (1.085)
  Pallas kernels: 319 us -> 404 us
  local copies, waits for them, and re-layouts: 97.7 us -> 81 us
  waiting for transfers between devices: 127 us -> 114 us
    pallas_call x24, Pallas kernels: 76.6 us -> 119 us  [grad_rows(): pl.pallas_call(functools.partial(grad_kernel, lefts, starts, add is not N...]
    pallas_call x20, Pallas kernels: 24.5 us -> 48.3 us  [add_rows(): pl.pallas_call(add_kernel, grid=(2,), in_specs=[pl.BlockSpec((tile, width...]
    unnamed x286 -> x188, local copies, waits for them, and re-layouts: 43.9 us -> 20.6 us
    pallas_call x6, Pallas kernels: 48 us -> 63.4 us  [assemble(): pl.pallas_call(functools.partial(assemble_kernel, steps, depth), grid_spe...]
    ppermute x88, waiting for transfers between devices: 101 us -> 87.8 us  [exchange(): return lax.ppermute(piece, name, SWAP)]
  transfers between devices with their start and end apart: 103 -> 103, of which waited for: 36 -> 28; matrix products, arithmetic and copies ran while one was open for 21% -> 21% of each run, Pallas kernels for 38% -> 42%
where the time goes in v6:
time: 806 us; the launch traced here: 793 us
  Pallas kernels  404 us (50%)
  waiting for transfers between devices  114 us (14%)
  matrix products  97 us (12%)
  local copies, waits for them, and re-layouts  81 us (10%)
  starting transfers between devices  62.4 us (8%)
  other arithmetic  20.3 us (3%)
  between operations  15.5 us (2%)
    pallas_call x24, Pallas kernels, grad_rows(): pl.pallas_call(functools.partial(grad_kernel, lefts, starts, add is not N...  119 us
    dot_general x17, matrix products, matmul_rows(): return jnp.dot(left, right, preferred_element_type=jnp.float32)  88 us
    ppermute x88, waiting for transfers between devices, exchange(): return lax.ppermute(piece, name, SWAP)  87.8 us
    pallas_call x2, Pallas kernels, attn_bwd(): pl.pallas_call(functools.partial(attn_bwd_kernel, parts, chunk, blk), gri...  69.9 us
    pallas_call x6, Pallas kernels, assemble(): pl.pallas_call(functools.partial(assemble_kernel, steps, depth), grid_spe...  63.4 us
    ppermute x88, starting transfers between devices, exchange(): return lax.ppermute(piece, name, SWAP)  56.8 us
    pallas_call x20, Pallas kernels, add_rows(): pl.pallas_call(add_kernel, grid=(2,), in_specs=[pl.BlockSpec((tile, width...  48.3 us
    pallas_call x2, Pallas kernels, attn_fwd(): pl.pallas_call(functools.partial(attn_fwd_kernel, parts, chunk, blk), gri...  36.8 us
  transfers between devices with their start and end apart: 103, of which 28 were waited for; matrix products, arithmetic and copies ran while one was open for 21% of the time, Pallas kernels for 42%

profile of v6, /device:TPU:0, one launch (start us, length us, event | category | flops | bytes accessed | tf_op | source)
XLA Modules:
  0.0 793.3 jit_solution(16690225990216681413)
XLA Ops:
  18.6 11.3 %collective-permute-done = bf16[256,1024]{1,0:T(8,128)(2,1)S(1)} collective-permute-done((bf16[256,1024]{1,0:T(8,128)(2,1)S(1)}, bf16[256,1024]{1,0:T(8,128)(2,1)S(1)}, u32[]{:S(2)}, u32[]{:S(2)}) %collective-permute-start) | collective-permute-done | bytes 524320 | tf_op jit(solution)/shard_map/ppermute | solution.py:396
  30.0 10.3 %collective-permute-done.1 = bf16[256,1024]{1,0:T(8,128)(2,1)S(1)} collective-permute-done((bf16[256,1024]{1,0:T(8,128)(2,1)S(1)}, bf16[256,1024]{1,0:T(8,128)(2,1)S(1)}, u32[]{:S(2)}, u32[]{:S(2)}) %collective-permute-start.1) | collective-permute-done | bytes 524320 | tf_op jit(solution)/shard_map/ppermute | solution.py:396
  47.2 22.6 %collective-permute-done.2.refs_2_ = bf16[128,4224]{1,0:T(8,128)(2,1)S(1)} collective-permute-done((bf16[128,4224]{1,0:T(8,128)(2,1)}, bf16[128,4224]{1,0:T(8,128)(2,1)S(1)}, u32[]{:S(2)}, u32[]{:S(2)}) %collective-permute-start.2) | collective-permute-done | bytes 1081376 | tf_op jit(solution)/shard_map/ppermute | solution.py:396
  80.3 9.9 %collective-permute-done.7.refs_6_ = bf16[64,4224]{1,0:T(8,128)(2,1)} collective-permute-done((bf16[64,4224]{1,0:T(8,128)(2,1)}, bf16[64,4224]{1,0:T(8,128)(2,1)}, u32[]{:S(2)}, u32[]{:S(2)}) %collective-permute-start.7) | collective-permute-done | bytes 540704 | tf_op jit(solution)/shard_map/ppermute | solution.py:396
  94.5 10.6 %assemble.6.w_ref = bf16[1024,4224]{1,0:T(8,128)(2,1)} custom-call(s32[10]{0:T(128)} %pad_add_fusion.1.table_ref, bf16[128,4224]{1,0:T(8,128)(2,1)} %all-gather.7.cloned.1.call-done.refs_0_, bf16[128,4224]{1,0:T(8,128)(2,1)} %copy-done.37, bf16[128,4224]{1,0:T(8,128)(2,1)} %copy-done.20, bf16[128,4224]{1,0:T(8,128)(2,1)} %collective-permute-done.5.refs_3_, ...), custom_call_target="tpu_custom_call" | custom-call | flops 1024 | bytes 1024 | tf_op jit(solution)/shard_map/assemble/pallas_call | solution.py:471
  133.4 10.2 %toeplitz.1.refs_4_ = bf16[16,15,128,128]{3,2,1,0:T(8,128)(2,1)} custom-call(f32[16,1,2048]{2,1,0:T(1,128)} %reshape.119.u_ref), custom_call_target="tpu_custom_call" | custom-call | flops 1024 | bytes 1024 | tf_op jit(solution)/shard_map/toeplitz/pallas_call | solution.py:30
  152.0 18.4 %attn_fwd.2 = (bf16[512,1024]{1,0:T(8,128)(2,1)}, f32[8,2,512]{2,1,0:T(2,128)}) custom-call(s32[7]{0:T(128)} %stack.74.pos_ref, bf16[512,1024]{1,0:T(8,128)(2,1)} %slice.282.q_ref, bf16[512,1024]{1,0:T(8,128)(2,1)} %get-tuple-element.519.refs_0_, bf16[512,1024]{1,0:T(8,128)(2,1)} %get-tuple-element.523.refs_1_, ...), custom_call_target="tpu_custom_call" | custom-call | flops 1024 | bytes 1024 | tf_op jit(solution)/shard_map/attn_fwd/pallas_call | solution.py:116
  183.4 10.3 %assemble.7.inner_ref = bf16[1024,4096]{1,0:T(8,128)(2,1)} custom-call(s32[10]{0:T(128)} %pad_add_fusion.1.table_ref, bf16[128,4096]{1,0:T(8,128)(2,1)} %all-gather.9.cloned.1.call-done.refs_0_, bf16[128,4096]{1,0:T(8,128)(2,1)} %collective-permute-done.13.refs_1_, bf16[128,4096]{1,0:T(8,128)(2,1)} %copy-done.21, bf16[128,4096]{1,0:T(8,128)(2,1)} %copy-done.38, ...), custom_call_target="tpu_custom_call" | custom-call | flops 1024 | bytes 1024 | tf_op jit(solution)/shard_map/assemble/pallas_call | solution.py:471
  199.8 11.5 %fusion.7 = (bf16[512,4096]{1,0:T(8,128)(2,1)}, bf16[512,4096]{1,0:T(8,128)(2,1)}) fusion(bf16[1024,4096]{1,0:T(8,128)(2,1)S(1)} %copy-done, f32[512,1024]{1,0:T(8,128)S(1)} %get-tuple-element.583.value_ref, f32[1024]{0:T(1024)S(1)} %bitcast.93, f32[512]{0:T(512)S(1)} %add_rsqrt_fusion.2), kind=kOutput, calls=%fused_computation.15 | convolution fusion | flops 4334288896 | bytes 18880512 | tf_op jit(solution)/shard_map/dot_general | solution.py:240
  218.3 10.5 %assemble.8.outer_ref = bf16[4096,1024]{1,0:T(8,128)(2,1)} custom-call(s32[10]{0:T(128)} %pad_add_fusion.1.table_ref, bf16[512,1024]{1,0:T(8,128)(2,1)} %all-gather.11.cloned.1.call-done.refs_0_, bf16[512,1024]{1,0:T(8,128)(2,1)} %collective-permute-done.23.refs_1_, bf16[512,1024]{1,0:T(8,128)(2,1)} %copy-done.22, bf16[512,1024]{1,0:T(8,128)(2,1)} %copy-done.39, ...), custom_call_target="tpu_custom_call" | custom-call | flops 1024 | bytes 1024 | tf_op jit(solution)/shard_map/assemble/pallas_call | solution.py:471
  239.2 9.7 %convolution_add_fusion.value_ref = f32[512,1024]{1,0:T(8,128)S(1)} fusion(f32[512,1024]{1,0:T(8,128)} %copy-done.33, bf16[512,4096]{1,0:T(8,128)(2,1)} %get-tuple-element.333.refs_0_.refs_1_.refs_2_.refs_3_, bf16[4096,1024]{1,0:T(8,128)(2,1)} %assemble.8.outer_ref), kind=kOutput, calls=%fused_computation.88 | convolution fusion | flops 4295491584 | bytes 16777216 | tf_op jit(solution)/shard_map/dot_general | solution.py:240
  255.0 11.0 %assemble.9.w_ref = bf16[1024,4096]{1,0:T(8,128)(2,1)} custom-call(s32[10]{0:T(128)} %pad_add_fusion.1.table_ref, bf16[128,4096]{1,0:T(8,128)(2,1)} %all-gather.13.cloned.1.call-done.refs_0_, bf16[128,4096]{1,0:T(8,128)(2,1)} %collective-permute-done.32.refs_1_, bf16[128,4096]{1,0:T(8,128)(2,1)} %copy-done.23, ...), custom_call_target="tpu_custom_call" | custom-call | flops 1024 | bytes 1024 | tf_op jit(solution)/shard_map/assemble/pallas_call | solution.py:471
  295.5 18.4 %attn_fwd.3 = (bf16[512,1024]{1,0:T(8,128)(2,1)}, f32[8,2,512]{2,1,0:T(2,128)}) custom-call(s32[7]{0:T(128)} %stack.74.pos_ref, bf16[512,1024]{1,0:T(8,128)(2,1)} %get-tuple-element.517.q_ref, bf16[512,1024]{1,0:T(8,128)(2,1)} %get-tuple-element.516.refs_0_, bf16[512,1024]{1,0:T(8,128)(2,1)} %get-tuple-element.521.refs_1_, ...), custom_call_target="tpu_custom_call" | custom-call | flops 1024 | bytes 1024 | tf_op jit(solution)/shard_map/attn_fwd/pallas_call | solution.py:116
  317.7 10.4 %assemble.10.inner_ref = bf16[1024,4096]{1,0:T(8,128)(2,1)} custom-call(s32[10]{0:T(128)} %pad_add_fusion.1.table_ref, bf16[128,4096]{1,0:T(8,128)(2,1)} %all-gather.15.cloned.1.call-done.refs_0_, bf16[128,4096]{1,0:T(8,128)(2,1)} %collective-permute-done.41.refs_1_, bf16[128,4096]{1,0:T(8,128)(2,1)} %collective-permute-done.39.refs_2_, ...), custom_call_target="tpu_custom_call" | custom-call | flops 1024 | bytes 1024 | tf_op jit(solution)/shard_map/assemble/pallas_call | solution.py:471
  341.3 11.6 %fusion.15 = (bf16[512,4096]{1,0:T(8,128)(2,1)}, bf16[512,4096]{1,0:T(8,128)(2,1)}) fusion(bf16[1024,4096]{1,0:T(8,128)(2,1)S(1)} %copy-done.1, f32[512,1024]{1,0:T(8,128)S(1)} %get-tuple-element.585.value_ref, f32[1024]{0:T(1024)S(1)} %bitcast.95, f32[512]{0:T(512)S(1)} %add_rsqrt_fusion), kind=kOutput, calls=%fused_computation.23 | convolution fusion | flops 4334288896 | bytes 18880512 | tf_op jit(solution)/shard_map/dot_general | solution.py:240
  358.7 10.5 %assemble.11.outer_ref = bf16[4096,1024]{1,0:T(8,128)(2,1)} custom-call(s32[10]{0:T(128)} %pad_add_fusion.1.table_ref, bf16[512,1024]{1,0:T(8,128)(2,1)} %all-gather.17.cloned.1.call-done.refs_0_, bf16[512,1024]{1,0:T(8,128)(2,1)} %collective-permute-done.51.refs_1_, bf16[512,1024]{1,0:T(8,128)(2,1)} %copy-done.24, bf16[512,1024]{1,0:T(8,128)(2,1)} %copy-done.40, ...), custom_call_target="tpu_custom_call" | custom-call | flops 1024 | bytes 1024 | tf_op jit(solution)/shard_map/assemble/pallas_call | solution.py:471
  390.0 18.5 %mlp_back.2 = (bf16[512,4096]{1,0:T(8,128)(2,1)}, f32[512,1024]{1,0:T(8,128)}, bf16[512,1024]{1,0:T(8,128)(2,1)}, f32[1,1024]{1,0:T(1,128)}) custom-call(f32[512,1024]{1,0:T(8,128)} %get-tuple-element.383.grad_ref, f32[512,1024]{1,0:T(8,128)} %copy-done.35, f32[1,1024]{1,0:T(1,128)} %get-tuple-element.574.gain_ref, bf16[4096,1024]{1,0:T(8,128)(2,1)} %assemble.11.outer_ref, ...), custom_call_target="tpu_custom_call" | custom-call | flops 1024 | bytes 1024 | tf_op jit(solution)/shard_map/mlp_back/pallas_call | solution.py:290
  443.7 35.0 %attn_bwd.2 = (bf16[512,1024]{1,0:T(8,128)(2,1)}, bf16[512,1024]{1,0:T(8,128)(2,1)}, bf16[512,1024]{1,0:T(8,128)(2,1)}, bf16[512,1024]{1,0:T(8,128)(2,1)}, bf16[...) custom-call(s32[7]{0:T(128)} %stack.74.pos_ref, bf16[512,1024]{1,0:T(8,128)(2,1)} %get-tuple-element.517.q_ref, ...), custom_call_target="tpu_custom_call" | custom-call | flops 21474836480 | bytes 12582912 | tf_op jit(solution)/shard_map/attn_bwd/pallas_call | solution.py:219
  504.1 9.9 %project_back.2 = (f32[512,1024]{1,0:T(8,128)}, f32[1,1024]{1,0:T(1,128)}) custom-call(f32[512,1024]{1,0:T(8,128)} %get-tuple-element.389.add_ref, f32[512,1024]{1,0:T(8,128)} %copy-done.2, f32[1,1024]{1,0:T(1,128)} %get-tuple-element.575.gain_ref, bf16[512,1024]{1,0:T(8,128)(2,1)} %get-tuple-element.399.refs_1_.q_ref, ...), custom_call_target="tpu_custom_call" | custom-call | flops 1024 | bytes 1024 | tf_op jit(solution)/shard_map/project_back/pallas_call | solution.py:335
  541.1 17.9 %mlp_back.3 = (bf16[512,4096]{1,0:T(8,128)(2,1)}, f32[512,1024]{1,0:T(8,128)}, bf16[512,1024]{1,0:T(8,128)(2,1)}, f32[1,1024]{1,0:T(1,128)}) custom-call(f32[512,1024]{1,0:T(8,128)} %get-tuple-element.426.grad_ref, f32[512,1024]{1,0:T(8,128)} %copy-done.33, f32[1,1024]{1,0:T(1,128)} %copy-done.75, bf16[4096,1024]{1,0:T(8,128)(2,1)} %assemble.8.outer_ref, ...), custom_call_target="tpu_custom_call" | custom-call | flops 1024 | bytes 1024 | tf_op jit(solution)/shard_map/mlp_back/pallas_call | solution.py:290
  614.3 35.0 %attn_bwd.3 = (bf16[512,1024]{1,0:T(8,128)(2,1)}, bf16[512,1024]{1,0:T(8,128)(2,1)}, bf16[512,1024]{1,0:T(8,128)(2,1)}, bf16[512,1024]{1,0:T(8,128)(2,1)}, bf16[...) custom-call(s32[7]{0:T(128)} %stack.74.pos_ref, bf16[512,1024]{1,0:T(8,128)(2,1)} %slice.282.q_ref, ...), custom_call_target="tpu_custom_call" | custom-call | flops 21474836480 | bytes 12582912 | tf_op jit(solution)/shard_map/attn_bwd/pallas_call | solution.py:219
  675.6 10.0 %project_back.3 = (f32[512,1024]{1,0:T(8,128)}, f32[1,1024]{1,0:T(1,128)}) custom-call(f32[512,1024]{1,0:T(8,128)} %get-tuple-element.428.add_ref, bf16[512,1024]{1,0:T(8,128)(2,1)} %copy-done.3, f32[1,1024]{1,0:T(1,128)} %copy-done.74, bf16[512,1024]{1,0:T(8,128)(2,1)} %get-tuple-element.456.refs_1_.q_ref, bf16[512,1024]{1,0:T(8,128)(2,1)} %add_rows.31.refs_3_.k_ref, ...), custom_call_target="tpu_custom_call" | custom-call | flops 1024 | bytes 1024 | tf_op jit(solution)/shard_map/project_back/pallas_call | solution.py:335
  716.6 14.6 %collective-permute-done.81.refs_1_ = bf16[256,2048]{1,0:T(8,128)(2,1)S(1)} collective-permute-done((bf16[256,2048]{1,0:T(8,128)(2,1)}, bf16[256,2048]{1,0:T(8,128)(2,1)S(1)}, u32[]{:S(2)}, u32[]{:S(2)}) %collective-permute-start.81) | collective-permute-done | bytes 1048608 | tf_op jit(solution)/shard_map/ppermute | solution.py:396
  762.7 10.2 %collective-permute-done.88 = f32[4608]{0:T(1024)S(1)} collective-permute-done((f32[4608]{0:T(1024)S(1)}, f32[4608]{0:T(1024)S(1)}, u32[]{:S(2)}, u32[]{:S(2)}) %collective-permute-start.88) | collective-permute-done | bytes 18464 | tf_op jit(solution)/shard_map/ppermute | solution.py:410
  (549 shorter events, 429.6 us)
Async XLA Ops:
  7.2 37.0 %all-gather.7.cloned.1.call-start = ((), (), s32[]{:S(2)}) async-start(), calls=%async_computation.4 | async-start | bytes 1351680 | tf_op jit(solution)/shard_map/all_gather | solution.py:506
  12.9 65.4 %all-gather.9.cloned.1.call-start = ((), (), s32[]{:S(2)}) async-start(), calls=%async_computation.5 | async-start | bytes 1310720 | tf_op jit(solution)/shard_map/all_gather | solution.py:506
  47.2 72.3 %all-gather.11.cloned.1.call-start = ((), (), s32[]{:S(2)}) async-start(), calls=%async_computation.6 | async-start | bytes 1310720 | tf_op jit(solution)/shard_map/all_gather | solution.py:506
  78.1 116.6 %all-gather.13.cloned.1.call-start = ((), (), s32[]{:S(2)}) async-start(), calls=%async_computation.7 | async-start | bytes 1310720 | tf_op jit(solution)/shard_map/all_gather | solution.py:506
  78.2 36.7 %collective-permute-start.11 = (bf16[128,4096]{1,0:T(8,128)(2,1)}, bf16[128,4096]{1,0:T(8,128)(2,1)S(1)}, u32[]{:S(2)}, u32[]{:S(2)}) collective-permute-start(bf16[128,4096]{1,0:T(8,128)(2,1)} %all-gather.9.cloned.1.call-done.refs_0_), channel_id=1, source_target_pairs={{0,2},{2,0},{1,3},{3,1},{4,6},{6,4},{5,7},{7,5},{8,10},{10,8},{9,1... | collective-permute-start | bytes 3145736 | tf_op jit(solution)/shard_map/ppermute | solution.py:396
  117.6 119.6 %all-gather.15.cloned.1.call-start = ((), (), s32[]{:S(2)}) async-start(), calls=%async_computation.8 | async-start | bytes 1310720 | tf_op jit(solution)/shard_map/all_gather | solution.py:506
  128.6 41.8 %collective-permute-start.17 = (bf16[64,4096]{1,0:T(8,128)(2,1)S(1)}, bf16[64,4096]{1,0:T(8,128)(2,1)S(1)}, u32[]{:S(2)}, u32[]{:S(2)}) collective-permute-start(bf16[64,4096]{1,0:T(8,128)(2,1)S(1)} %get-tuple-element.553.refs_4_), channel_id=1, source_target_pairs={{0,2},{2,0},{1,3},{3,1},{4,6},{6,4},{5,7},{7,5},{8,10},{10,8},{9,1... | collective-permute-start | bytes 1572872 | tf_op jit(solution)/shard_map/ppermute | solution.py:396
  130.0 40.3 %collective-permute-start.18 = (bf16[64,4096]{1,0:T(8,128)(2,1)}, bf16[64,4096]{1,0:T(8,128)(2,1)}, u32[]{:S(2)}, u32[]{:S(2)}) collective-permute-start(bf16[64,4096]{1,0:T(8,128)(2,1)} %slice.289), channel_id=1, source_target_pairs={{0,4},{4,0},{1,5},{5,1},{2,6},{6,2},{3,7},{7,3},{8,12},{12,8},{9,1... | collective-permute-start | bytes 1572872 | tf_op jit(solution)/shard_map/ppermute | solution.py:396
  132.2 41.7 %collective-permute-start.21 = (bf16[512,1024]{1,0:T(8,128)(2,1)}, bf16[512,1024]{1,0:T(8,128)(2,1)S(1)}, u32[]{:S(2)}, u32[]{:S(2)}) collective-permute-start(bf16[512,1024]{1,0:T(8,128)(2,1)} %all-gather.11.cloned.1.call-done.refs_0_), channel_id=1, source_target_pairs={{0,2},{2,0},{1,3},{3,1},{4,6},{6,4},{5,7},{7,5},{8,10},{10,8},{9,1... | collective-permute-start | bytes 3145736 | tf_op jit(solution)/shard_map/ppermute | solution.py:396
  132.7 41.2 %collective-permute-start.22 = (bf16[512,1024]{1,0:T(8,128)(2,1)}, bf16[512,1024]{1,0:T(8,128)(2,1)}, u32[]{:S(2)}, u32[]{:S(2)}) collective-permute-start(bf16[512,1024]{1,0:T(8,128)(2,1)} %all-gather.11.cloned.1.call-done.refs_0_), channel_id=1, source_target_pairs={{0,4},{4,0},{1,5},{5,1},{2,6},{6,2},{3,7},{7,3},{8,12},{12,8},{9,1... | collective-permute-start | bytes 3145736 | tf_op jit(solution)/shard_map/ppermute | solution.py:396
  173.5 105.5 %all-gather.17.cloned.1.call-start = ((), (), s32[]{:S(2)}) async-start(), calls=%async_computation.9 | async-start | bytes 1310720 | tf_op jit(solution)/shard_map/all_gather | solution.py:506
  231.9 417.5 %reduce-scatter.5.cloned.1.call-start = ((), (), s32[]{:S(2)}) async-start(), calls=%async_computation.10 | async-start | bytes 2621440 | tf_op jit(solution)/shard_map/reduce_scatter | solution.py:401
  237.2 37.2 %collective-permute-start.39 = (bf16[128,4096]{1,0:T(8,128)(2,1)}, bf16[128,4096]{1,0:T(8,128)(2,1)}, u32[]{:S(2)}, u32[]{:S(2)}) collective-permute-start(bf16[128,4096]{1,0:T(8,128)(2,1)} %all-gather.15.cloned.1.call-done.refs_0_), channel_id=1, source_target_pairs={{0,2},{2,0},{1,3},{3,1},{4,6},{6,4},{5,7},{7,5},{8,10},{10,8},{9,1... | collective-permute-start | bytes 3145736 | tf_op jit(solution)/shard_map/ppermute | solution.py:396
  238.3 36.1 %collective-permute-start.40 = (bf16[128,4096]{1,0:T(8,128)(2,1)}, bf16[128,4096]{1,0:T(8,128)(2,1)}, u32[]{:S(2)}, u32[]{:S(2)}) collective-permute-start(bf16[128,4096]{1,0:T(8,128)(2,1)} %all-gather.15.cloned.1.call-done.refs_0_), channel_id=1, source_target_pairs={{0,4},{4,0},{1,5},{5,1},{2,6},{6,2},{3,7},{7,3},{8,12},{12,8},{9,1... | collective-permute-start | bytes 3145736 | tf_op jit(solution)/shard_map/ppermute | solution.py:396
  239.2 35.3 %collective-permute-start.41 = (bf16[128,4096]{1,0:T(8,128)(2,1)}, bf16[128,4096]{1,0:T(8,128)(2,1)}, u32[]{:S(2)}, u32[]{:S(2)}) collective-permute-start(bf16[128,4096]{1,0:T(8,128)(2,1)} %all-gather.15.cloned.1.call-done.refs_0_), channel_id=1, source_target_pairs={{0,1},{1,0},{2,3},{3,2},{4,5},{5,4},{6,7},{7,6},{8,9},{9,8},{10,11... | collective-permute-start | bytes 3145736 | tf_op jit(solution)/shard_map/ppermute | solution.py:396
  290.4 37.7 %collective-permute-start.49 = (bf16[512,1024]{1,0:T(8,128)(2,1)}, bf16[512,1024]{1,0:T(8,128)(2,1)S(1)}, u32[]{:S(2)}, u32[]{:S(2)}) collective-permute-start(bf16[512,1024]{1,0:T(8,128)(2,1)} %all-gather.17.cloned.1.call-done.refs_0_), channel_id=1, source_target_pairs={{0,2},{2,0},{1,3},{3,1},{4,6},{6,4},{5,7},{7,5},{8,10},{10,8},{9,1... | collective-permute-start | bytes 3145736 | tf_op jit(solution)/shard_map/ppermute | solution.py:396
  291.3 36.7 %collective-permute-start.50 = (bf16[512,1024]{1,0:T(8,128)(2,1)}, bf16[512,1024]{1,0:T(8,128)(2,1)}, u32[]{:S(2)}, u32[]{:S(2)}) collective-permute-start(bf16[512,1024]{1,0:T(8,128)(2,1)} %all-gather.17.cloned.1.call-done.refs_0_), channel_id=1, source_target_pairs={{0,4},{4,0},{1,5},{5,1},{2,6},{6,2},{3,7},{7,3},{8,12},{12,8},{9,1... | collective-permute-start | bytes 3145736 | tf_op jit(solution)/shard_map/ppermute | solution.py:396
  425.3 53.5 %collective-permute-start.61 = (bf16[1024,1024]{1,0:T(8,128)(2,1)}, bf16[1024,1024]{1,0:T(8,128)(2,1)S(1)}, u32[]{:S(2)}, u32[]{:S(2)}) collective-permute-start(bf16[1024,1024]{1,0:T(8,128)(2,1)} %grad_rows.25), channel_id=1, source_target_pairs={{0,4},{4,0},{1,5},{5,1},{2,6},{6,2},{3,7},{7,3},{8,12},{12,8},{9,1... | collective-permute-start | bytes 6291464 | tf_op jit(solution)/shard_map/ppermute | solution.py:396
  433.2 48.0 %collective-permute-start.62 = (bf16[256,4096]{1,0:T(8,128)(2,1)}, bf16[256,4096]{1,0:T(8,128)(2,1)}, u32[]{:S(2)}, u32[]{:S(2)}) collective-permute-start(bf16[256,4096]{1,0:T(8,128)(2,1)} %grad_rows.27), channel_id=1, source_target_pairs={{0,2},{2,0},{1,3},{3,1},{4,6},{6,4},{5,7},{7,5},{8,10},{10,8},{9,1... | collective-permute-start | bytes 6291464 | tf_op jit(solution)/shard_map/ppermute | solution.py:396
  584.5 171.8 %reduce-scatter.9.cloned.1.call-start = ((), (), s32[]{:S(2)}) async-start(), calls=%async_computation.12 | async-start | bytes 1310720 | tf_op jit(solution)/shard_map/reduce_scatter | solution.py:401
  592.0 57.3 %collective-permute-start.75 = (bf16[1024,1024]{1,0:T(8,128)(2,1)}, bf16[1024,1024]{1,0:T(8,128)(2,1)S(1)}, u32[]{:S(2)}, u32[]{:S(2)}) collective-permute-start(bf16[1024,1024]{1,0:T(8,128)(2,1)} %grad_rows.35), channel_id=1, source_target_pairs={{0,4},{4,0},{1,5},{5,1},{2,6},{6,2},{3,7},{7,3},{8,12},{12,8},{9,1... | collective-permute-start | bytes 6291464 | tf_op jit(solution)/shard_map/ppermute | solution.py:396
  598.6 50.8 %collective-permute-start.76 = (bf16[256,4096]{1,0:T(8,128)(2,1)}, bf16[256,4096]{1,0:T(8,128)(2,1)}, u32[]{:S(2)}, u32[]{:S(2)}) collective-permute-start(bf16[256,4096]{1,0:T(8,128)(2,1)} %grad_rows.39), channel_id=1, source_target_pairs={{0,2},{2,0},{1,3},{3,1},{4,6},{6,4},{5,7},{7,5},{8,10},{10,8},{9,1... | collective-permute-start | bytes 6291464 | tf_op jit(solution)/shard_map/ppermute | solution.py:396
  675.6 80.7 %reduce-scatter.7.cloned.1.call-start = ((), (), s32[]{:S(2)}) async-start(), calls=%async_computation.11 | async-start | bytes 2621440 | tf_op jit(solution)/shard_map/reduce_scatter | solution.py:401
  706.6 78.0 %reduce-scatter.11.cloned.1.call-start = ((), (), s32[]{:S(2)}) async-start(), calls=%async_computation.13 | async-start | bytes 1310720 | tf_op jit(solution)/shard_map/reduce_scatter | solution.py:401
  (164 other events, 2420.9 us)
Sparse Core Ops, SparseCore 0:
  13.0 31.1 all-gather.6
  47.3 25.8 all-gather.8
  78.3 26.8 all-gather.10
  117.7 27.6 all-gather.12
  173.7 27.7 all-gather.14
  232.0 27.1 all-gather.16
  584.6 42.9 reduce-scatter.4
  675.7 26.0 reduce-scatter.8
  706.7 43.4 reduce-scatter.6
  758.7 25.8 reduce-scatter.10
